TPU v7x, 768 devices: a whole 4x8x12 slice. The times are simulated.
768 devices in a mesh: grp: 48 (over y, z_lo), gy: 4 (over z_hi, core), gz: 4 (over x).
Axes of the slice: x: 4, y: 8, z: 12 (z_hi: 2, z_lo: 6; z = z_hi * 6 + z_lo), core: 2. Of those that a mesh axis runs over, the one named last changes fastest.
Arguments:
- fwd_velocity: float32 [3, 192, 32, 512], P(None, 'grp', 'gy', 'gz'), may hold values from -6 to 6
- fwd_stress: float32 [6, 192, 32, 512], P(None, 'grp', 'gy', 'gz'), may hold values from -6 to 6
- density: float32 [192, 32, 512], P('grp', 'gy', 'gz'), may hold values from 1 to 3
- lame: float32 [2, 192, 32, 512], P(None, 'grp', 'gy', 'gz'), may hold values from 0.5 to 2
- adj_velocity: float32 [3, 288, 32, 512], P(None, 'grp', 'gy', 'gz'), may hold values from -6 to 6
- adj_stress: float32 [6, 288, 32, 512], P(None, 'grp', 'gy', 'gz'), may hold values from -6 to 6
- offsets: int32 [48], replicated, may hold values from 0 to 2, as said below
Outputs:
- density_kernel: float32 [288, 32, 512], P('grp', 'gy', 'gz')
- modulus_kernel: float32 [2, 288, 32, 512], P(None, 'grp', 'gy', 'gz')
Inputs may be any that keep to these rules, and one draw needn't show every extreme that they name: offsets[0] is 0; in every draw some block b has offsets[b] = 0 and offsets[b+1] = 2, so some adjoint block has 6 planes.
All inputs are finite; a program needn't handle non-finite values.
Results may differ from a plain program's by a relative error of at most 0.00002.
Values sent between devices are 32-bit elements; how exact they have to be, the bound alone decides.
No kernel may reach another device: no remote copies, remote signals or barrier semaphores. Data moves between devices by JAX's collectives and lax.ppermute only.
A program may use at most 32 MiB of HBM per device.

v0:
```python
import jax
import jax.numpy as jnp
from jax import lax
from jax.sharding import PartitionSpec as P

STEPS = 4


time_step = 0.15
pairs = ((0, 5, 4), (5, 1, 3), (4, 3, 2))


def with_halo(shard, sides, width):
    edges = {}
    for axis, dim in sides:
        count, length = (lax.axis_size(axis), shard.shape[dim])
        up = [(i, (i + 1) % count) for i in range(count - 1)]
        last = lax.slice_in_dim(shard, length - width, length, axis=dim)
        leading = lax.slice_in_dim(shard, 0, width, axis=dim)
        edges[dim] = (
            lax.ppermute(last, axis, up),
            lax.ppermute(leading, axis, [(b, a) for a, b in up]),
        )
    done = []
    for _, dim in sides:
        low, high = edges[dim]
        around = [(width, width) if d in done else (0, 0) for d in range(shard.ndim)]
        shard = jnp.concatenate([jnp.pad(low, around), shard, jnp.pad(high, around)], axis=dim)
        done.append(dim)
    return shard


def with_halo_2(block, sides, width):
    for axis, dim in sides:
        count = lax.axis_size(axis)
        forward = [(i, i + 1) for i in range(count - 1)]
        backward = [(target, source) for source, target in forward]
        low = lax.ppermute(
            lax.slice_in_dim(block, block.shape[dim] - width, None, axis=dim), axis, forward
        )
        high = lax.ppermute(lax.slice_in_dim(block, 0, width, axis=dim), axis, backward)
        block = jnp.concatenate([low, block, high], axis=dim)
    return block


def from_behind(value, axis, steps):
    count = lax.axis_size(axis)
    leading, last = (max(0, -steps), min(count, count - steps))
    return lax.ppermute(value, axis, [(source, source + steps) for source in range(leading, last)])


def back_diffs(stack, extent):
    faces = with_halo(stack, (("gy", 2), ("gz", 3)), 1)
    first_plane = stack[:, 0:1]
    last_plane = lax.dynamic_slice_in_dim(stack, extent - 1, 1, 1)
    edges = with_halo_2(jnp.concatenate([first_plane, last_plane], axis=1), (("grp", 1),), 1)
    widened = jnp.concatenate([edges[:, 0:1], stack, jnp.zeros_like(first_plane)], axis=1)
    widened = lax.dynamic_update_slice_in_dim(widened, edges[:, 3:4], extent + 1, 1)
    along_x = (widened[:, 2:] - widened[:, :-2]) * 0.5
    along_y = (faces[:, :, 2:, 1:-1] - faces[:, :, :-2, 1:-1]) * 0.5
    along_z = (faces[:, :, 1:-1, 2:] - faces[:, :, 1:-1, :-2]) * 0.5
    return (along_x, along_y, along_z)


def velocity_from(velocity, slopes, base, rho_field, delta):
    result = []
    for i in range(3):
        force = (
            slopes[0][base + pairs[i][0]]
            + slopes[1][base + pairs[i][1]]
            + slopes[2][base + pairs[i][2]]
        )
        result.append(velocity[i] + delta / rho_field * force)
    return jnp.stack(result)


def strain_from(slopes, base):
    grads = [[slopes[j][base + i] for j in range(3)] for i in range(3)]
    return jnp.stack(
        [
            grads[0][0],
            grads[1][1],
            grads[2][2],
            0.5 * (grads[1][2] + grads[2][1]),
            0.5 * (grads[0][2] + grads[2][0]),
            0.5 * (grads[0][1] + grads[1][0]),
        ]
    )


def stress_update(stress, strain, moduli, delta):
    trace = strain[0] + strain[1] + strain[2]
    first = moduli[0] * trace
    double = 2.0 * moduli[1]
    normal = stress[:3] + delta * (first[None] + double[None] * strain[:3])
    shear = stress[3:] + delta * (double[None] * strain[3:])
    return jnp.concatenate([normal, shear])


def kernel_terms(back_vel, fore_vel, back_rate, fore_rate):
    rho_term = time_step * (
        back_vel[0] * fore_vel[0] + back_vel[1] * fore_vel[1] + back_vel[2] * fore_vel[2]
    )
    lam_term = time_step * (
        (back_rate[0] + back_rate[1] + back_rate[2]) * (fore_rate[0] + fore_rate[1] + fore_rate[2])
    )
    normal = back_rate[0] * fore_rate[0] + back_rate[1] * fore_rate[1] + back_rate[2] * fore_rate[2]
    shear = back_rate[3] * fore_rate[3] + back_rate[4] * fore_rate[4] + back_rate[5] * fore_rate[5]
    mu_term = time_step * (2.0 * (normal + 2.0 * shear))
    return (rho_term, jnp.stack([lam_term, mu_term]))


def recut(stack, own_offset):
    planes = stack.shape[1]
    lag_rows = planes // 2
    leading = stack[:, :lag_rows]
    arrived = from_behind(leading, "grp", -1)
    joined = jnp.concatenate([stack, arrived, jnp.zeros_like(leading)], axis=1)
    return lax.dynamic_slice_in_dim(joined, own_offset, planes + lag_rows, 1)


def shards(fwd_velocity, fwd_stress, density, lame, adj_velocity, adj_stress, offsets):
    blocks = lax.axis_size("grp")
    place = lax.axis_index("grp")
    planes = fwd_velocity.shape[1]
    held = adj_velocity.shape[1]
    own_offset = lax.dynamic_index_in_dim(offsets, place, 0, keepdims=False)
    next_place = jnp.minimum(place + 1, blocks - 1)
    next_offset = jnp.where(
        place + 1 < blocks, lax.dynamic_index_in_dim(offsets, next_place, 0, keepdims=False), 0
    )
    extent = planes + next_offset - own_offset
    live = (jnp.arange(held, dtype=jnp.int32) < extent)[None, :, None, None]

    def adjoint_diffs(stack):
        return back_diffs(stack, extent)

    back_vel = jnp.where(live, adj_velocity, jnp.float32(0.0))
    back_str = jnp.where(live, adj_stress, jnp.float32(0.0))
    rho_kernel = jnp.zeros((held,) + density.shape[1:], jnp.float32)
    mod_kernel = jnp.zeros((2, held) + density.shape[1:], jnp.float32)
    everything = recut(
        jnp.concatenate([density[None], lame, fwd_velocity, fwd_stress], axis=0), own_offset
    )
    back_rho = jnp.where(live[0], everything[0], jnp.float32(1.0))
    back_lame = jnp.where(live, everything[1:3], jnp.float32(0.0))
    fore_vel = jnp.where(live, everything[3:6], jnp.float32(0.0))
    fore_str = jnp.where(live, everything[6:12], jnp.float32(0.0))
    for step in range(STEPS):
        stress_slopes = adjoint_diffs(jnp.concatenate([back_str, fore_str], axis=0))
        back_vel = velocity_from(back_vel, stress_slopes, 0, back_rho, time_step)
        fore_vel = velocity_from(fore_vel, stress_slopes, 6, back_rho, -time_step)
        back_vel = jnp.where(live, back_vel, jnp.float32(0.0))
        fore_vel = jnp.where(live, fore_vel, jnp.float32(0.0))
        vel_slopes = adjoint_diffs(jnp.concatenate([back_vel, fore_vel], axis=0))
        back_rate = strain_from(vel_slopes, 0)
        fore_rate = strain_from(vel_slopes, 3)
        back_str = jnp.where(
            live, stress_update(back_str, back_rate, back_lame, time_step), jnp.float32(0.0)
        )
        fore_str = jnp.where(
            live, stress_update(fore_str, fore_rate, back_lame, -time_step), jnp.float32(0.0)
        )
        rho_term, mod_term = kernel_terms(back_vel, fore_vel, back_rate, fore_rate)
        rho_kernel = rho_kernel + rho_term
        mod_kernel = mod_kernel + mod_term
    density_kernel = jnp.where(live[0], rho_kernel, jnp.float32(0.0))
    modulus_kernel = jnp.where(live, mod_kernel, jnp.float32(0.0))
    return (density_kernel, modulus_kernel)


def solution(mesh):
    return jax.shard_map(
        shards,
        mesh=mesh,
        in_specs=(
            P(None, "grp", "gy", "gz"),
            P(None, "grp", "gy", "gz"),
            P("grp", "gy", "gz"),
            P(None, "grp", "gy", "gz"),
            P(None, "grp", "gy", "gz"),
            P(None, "grp", "gy", "gz"),
            P(),
        ),
        out_specs=(P("grp", "gy", "gz"), P(None, "grp", "gy", "gz")),
        check_vma=False,
    )
```

profile of v0, /device:TPU:37, one launch (start us, length us, event | category | flops | bytes accessed | tf_op | source)
XLA Modules:
  0.0 285.4 jit_solution(7357560897302171588)
XLA Ops:
  1.5 12.3 %collective-permute-start = (f32[12,2,8,128]{3,2,1,0:T(8,128)S(1)}, f32[12,2,8,128]{3,2,1,0:T(8,128)S(1)}, u32[]{:S(2)}, u32[]{:S(2)}) collective-permute-start(f32[12,2,8,128]{3,2,1,0:T(8,128)S(1)} %pad_maximum_fusion.88), channel_id=1, source_target_pairs={{16,0},{32,16},{48,32},{64,48},{80,64},{96,80},{112,96},{128,112},... | collective-permute-start | bytes 294920 | tf_op jit(solution)/shard_map/ppermute | solution.py:49
  19.9 10.6 %collective-permute-start.4 = (f32[12,6,1,128]{3,2,1,0:T(1,128)S(1)}, f32[12,6,1,128]{3,2,1,0:T(1,128)S(1)}, u32[]{:S(2)}, u32[]{:S(2)}) collective-permute-start(f32[12,6,1,128]{3,2,1,0:T(1,128)S(1)} %get-tuple-element.86), channel_id=1, source_target_pairs={{0,4},{4,8},{8,12},{1,5},{5,9},{9,13},{2,6},{6,10},{10,14},{3,7},{... | collective-permute-start | bytes 110600 | tf_op jit(solution)/shard_map/ppermute | solution.py:21
  40.2 9.8 %collective-permute-start.2 = (f32[12,1,8,128]{3,2,1,0:T(8,128)S(1)}, f32[12,1,8,128]{3,2,1,0:T(8,128)S(1)}, u32[]{:S(2)}, u32[]{:S(2)}) collective-permute-start(f32[12,1,8,128]{3,2,1,0:T(8,128)S(1)} %get-tuple-element.82), channel_id=1, source_target_pairs={{16,0},{32,16},{48,32},{64,48},{80,64},{96,80},{112,96},{128,112},... | collective-permute-start | bytes 147464 | tf_op jit(solution)/shard_map/ppermute | solution.py:41
  51.7 11.6 %collective-permute-start.10 = (f32[6,6,1,128]{3,2,1,0:T(1,128)S(1)}, f32[6,6,1,128]{3,2,1,0:T(1,128)S(1)}, u32[]{:S(2)}, u32[]{:S(2)}) collective-permute-start(f32[6,6,1,128]{3,2,1,0:T(1,128)S(1)} %get-tuple-element.148), channel_id=1, source_target_pairs={{0,4},{4,8},{8,12},{1,5},{5,9},{9,13},{2,6},{6,10},{10,14},{3,7},{... | collective-permute-start | bytes 55304 | tf_op jit(solution)/shard_map/ppermute | solution.py:21
  65.2 2.8 collective-permute-start.12
  72.5 10.3 %collective-permute-start.8 = (f32[6,1,8,128]{3,2,1,0:T(8,128)S(1)}, f32[6,1,8,128]{3,2,1,0:T(8,128)S(1)}, u32[]{:S(2)}, u32[]{:S(2)}) collective-permute-start(f32[6,1,8,128]{3,2,1,0:T(8,128)S(1)} %get-tuple-element.144), channel_id=1, source_target_pairs={{16,0},{32,16},{48,32},{64,48},{80,64},{96,80},{112,96},{128,112},... | collective-permute-start | bytes 73736 | tf_op jit(solution)/shard_map/ppermute | solution.py:41
  84.2 12.0 %collective-permute-start.16 = (f32[12,6,1,128]{3,2,1,0:T(1,128)S(1)}, f32[12,6,1,128]{3,2,1,0:T(1,128)S(1)}, u32[]{:S(2)}, u32[]{:S(2)}) collective-permute-start(f32[12,6,1,128]{3,2,1,0:T(1,128)S(1)} %get-tuple-element.80), channel_id=1, source_target_pairs={{0,4},{4,8},{8,12},{1,5},{5,9},{9,13},{2,6},{6,10},{10,14},{3,7},{... | collective-permute-start | bytes 110600 | tf_op jit(solution)/shard_map/ppermute | solution.py:21
  98.1 2.8 collective-permute-start.18
  105.8 9.9 %collective-permute-start.14 = (f32[12,1,8,128]{3,2,1,0:T(8,128)S(1)}, f32[12,1,8,128]{3,2,1,0:T(8,128)S(1)}, u32[]{:S(2)}, u32[]{:S(2)}) collective-permute-start(f32[12,1,8,128]{3,2,1,0:T(8,128)S(1)} %get-tuple-element.76), channel_id=1, source_target_pairs={{16,0},{32,16},{48,32},{64,48},{80,64},{96,80},{112,96},{128,112},... | collective-permute-start | bytes 147464 | tf_op jit(solution)/shard_map/ppermute | solution.py:41
  117.4 12.6 %collective-permute-start.22 = (f32[6,6,1,128]{3,2,1,0:T(1,128)S(1)}, f32[6,6,1,128]{3,2,1,0:T(1,128)S(1)}, u32[]{:S(2)}, u32[]{:S(2)}) collective-permute-start(f32[6,6,1,128]{3,2,1,0:T(1,128)S(1)} %get-tuple-element.136), channel_id=1, source_target_pairs={{0,4},{4,8},{8,12},{1,5},{5,9},{9,13},{2,6},{6,10},{10,14},{3,7},{... | collective-permute-start | bytes 55304 | tf_op jit(solution)/shard_map/ppermute | solution.py:21
  131.9 2.8 collective-permute-start.24
  139.1 10.3 %collective-permute-start.20 = (f32[6,1,8,128]{3,2,1,0:T(8,128)S(1)}, f32[6,1,8,128]{3,2,1,0:T(8,128)S(1)}, u32[]{:S(2)}, u32[]{:S(2)}) collective-permute-start(f32[6,1,8,128]{3,2,1,0:T(8,128)S(1)} %get-tuple-element.132), channel_id=1, source_target_pairs={{16,0},{32,16},{48,32},{64,48},{80,64},{96,80},{112,96},{128,112},... | collective-permute-start | bytes 73736 | tf_op jit(solution)/shard_map/ppermute | solution.py:41
  150.8 12.0 %collective-permute-start.28 = (f32[12,6,1,128]{3,2,1,0:T(1,128)S(1)}, f32[12,6,1,128]{3,2,1,0:T(1,128)S(1)}, u32[]{:S(2)}, u32[]{:S(2)}) collective-permute-start(f32[12,6,1,128]{3,2,1,0:T(1,128)S(1)} %get-tuple-element.74), channel_id=1, source_target_pairs={{0,4},{4,8},{8,12},{1,5},{5,9},{9,13},{2,6},{6,10},{10,14},{3,7},{... | collective-permute-start | bytes 110600 | tf_op jit(solution)/shard_map/ppermute | solution.py:21
  164.7 2.8 collective-permute-start.30
  172.5 9.9 %collective-permute-start.26 = (f32[12,1,8,128]{3,2,1,0:T(8,128)S(1)}, f32[12,1,8,128]{3,2,1,0:T(8,128)S(1)}, u32[]{:S(2)}, u32[]{:S(2)}) collective-permute-start(f32[12,1,8,128]{3,2,1,0:T(8,128)S(1)} %get-tuple-element.70), channel_id=1, source_target_pairs={{16,0},{32,16},{48,32},{64,48},{80,64},{96,80},{112,96},{128,112},... | collective-permute-start | bytes 147464 | tf_op jit(solution)/shard_map/ppermute | solution.py:41
  184.0 12.6 %collective-permute-start.34 = (f32[6,6,1,128]{3,2,1,0:T(1,128)S(1)}, f32[6,6,1,128]{3,2,1,0:T(1,128)S(1)}, u32[]{:S(2)}, u32[]{:S(2)}) collective-permute-start(f32[6,6,1,128]{3,2,1,0:T(1,128)S(1)} %get-tuple-element.124), channel_id=1, source_target_pairs={{0,4},{4,8},{8,12},{1,5},{5,9},{9,13},{2,6},{6,10},{10,14},{3,7},{... | collective-permute-start | bytes 55304 | tf_op jit(solution)/shard_map/ppermute | solution.py:21
  198.5 2.8 collective-permute-start.36
  205.8 10.3 %collective-permute-start.32 = (f32[6,1,8,128]{3,2,1,0:T(8,128)S(1)}, f32[6,1,8,128]{3,2,1,0:T(8,128)S(1)}, u32[]{:S(2)}, u32[]{:S(2)}) collective-permute-start(f32[6,1,8,128]{3,2,1,0:T(8,128)S(1)} %get-tuple-element.120), channel_id=1, source_target_pairs={{16,0},{32,16},{48,32},{64,48},{80,64},{96,80},{112,96},{128,112},... | collective-permute-start | bytes 73736 | tf_op jit(solution)/shard_map/ppermute | solution.py:41
  217.5 12.0 %collective-permute-start.40 = (f32[12,6,1,128]{3,2,1,0:T(1,128)S(1)}, f32[12,6,1,128]{3,2,1,0:T(1,128)S(1)}, u32[]{:S(2)}, u32[]{:S(2)}) collective-permute-start(f32[12,6,1,128]{3,2,1,0:T(1,128)S(1)} %get-tuple-element.68), channel_id=1, source_target_pairs={{0,4},{4,8},{8,12},{1,5},{5,9},{9,13},{2,6},{6,10},{10,14},{3,7},{... | collective-permute-start | bytes 110600 | tf_op jit(solution)/shard_map/ppermute | solution.py:21
  231.4 2.9 collective-permute-start.42
  239.2 9.9 %collective-permute-start.38 = (f32[12,1,8,128]{3,2,1,0:T(8,128)S(1)}, f32[12,1,8,128]{3,2,1,0:T(8,128)S(1)}, u32[]{:S(2)}, u32[]{:S(2)}) collective-permute-start(f32[12,1,8,128]{3,2,1,0:T(8,128)S(1)} %get-tuple-element.64), channel_id=1, source_target_pairs={{16,0},{32,16},{48,32},{64,48},{80,64},{96,80},{112,96},{128,112},... | collective-permute-start | bytes 147464 | tf_op jit(solution)/shard_map/ppermute | solution.py:41
  251.4 2.9 collective-permute-start.48
  256.2 12.8 %collective-permute-start.46 = (f32[6,6,1,128]{3,2,1,0:T(1,128)S(1)}, f32[6,6,1,128]{3,2,1,0:T(1,128)S(1)}, u32[]{:S(2)}, u32[]{:S(2)}) collective-permute-start(f32[6,6,1,128]{3,2,1,0:T(1,128)S(1)} %get-tuple-element.111), channel_id=1, source_target_pairs={{0,4},{4,8},{8,12},{1,5},{5,9},{9,13},{2,6},{6,10},{10,14},{3,7},{... | collective-permute-start | bytes 55304 | tf_op jit(solution)/shard_map/ppermute | solution.py:21
  273.4 10.3 %collective-permute-start.44 = (f32[6,1,8,128]{3,2,1,0:T(8,128)S(1)}, f32[6,1,8,128]{3,2,1,0:T(8,128)S(1)}, u32[]{:S(2)}, u32[]{:S(2)}) collective-permute-start(f32[6,1,8,128]{3,2,1,0:T(8,128)S(1)} %get-tuple-element.112), channel_id=1, source_target_pairs={{16,0},{32,16},{48,32},{64,48},{80,64},{96,80},{112,96},{128,112},... | collective-permute-start | bytes 73736 | tf_op jit(solution)/shard_map/ppermute | solution.py:41
  (184 shorter events, 71.2 us)
Async XLA Ops:
  1.5 17.1 %collective-permute-start = (f32[12,2,8,128]{3,2,1,0:T(8,128)S(1)}, f32[12,2,8,128]{3,2,1,0:T(8,128)S(1)}, u32[]{:S(2)}, u32[]{:S(2)}) collective-permute-start(f32[12,2,8,128]{3,2,1,0:T(8,128)S(1)} %pad_maximum_fusion.88), channel_id=1, source_target_pairs={{16,0},{32,16},{48,32},{64,48},{80,64},{96,80},{112,96},{128,112},... | collective-permute-start | bytes 294920 | tf_op jit(solution)/shard_map/ppermute | solution.py:49
  19.9 30.1 %collective-permute-start.4 = (f32[12,6,1,128]{3,2,1,0:T(1,128)S(1)}, f32[12,6,1,128]{3,2,1,0:T(1,128)S(1)}, u32[]{:S(2)}, u32[]{:S(2)}) collective-permute-start(f32[12,6,1,128]{3,2,1,0:T(1,128)S(1)} %get-tuple-element.86), channel_id=1, source_target_pairs={{0,4},{4,8},{8,12},{1,5},{5,9},{9,13},{2,6},{6,10},{10,14},{3,7},{... | collective-permute-start | bytes 110600 | tf_op jit(solution)/shard_map/ppermute | solution.py:21
  30.5 19.5 %collective-permute-start.3 = (f32[12,6,1,128]{3,2,1,0:T(1,128)S(1)}, f32[12,6,1,128]{3,2,1,0:T(1,128)S(1)}, u32[]{:S(2)}, u32[]{:S(2)}) collective-permute-start(f32[12,6,1,128]{3,2,1,0:T(1,128)S(1)} %get-tuple-element.87), channel_id=1, source_target_pairs={{4,0},{8,4},{12,8},{5,1},{9,5},{13,9},{6,2},{10,6},{14,10},{7,3},{... | collective-permute-start | bytes 110600 | tf_op jit(solution)/shard_map/ppermute | solution.py:22
  35.3 14.7 %collective-permute-start.5 = (f32[12,6,8,1]{3,2,1,0:T(8,128)S(1)}, f32[12,6,8,1]{3,2,1,0:T(8,128)S(1)}, u32[]{:S(2)}, u32[]{:S(2)}) collective-permute-start(f32[12,6,8,1]{3,2,1,0:T(8,128)S(1)} %get-tuple-element.84), channel_id=1, source_target_pairs={{1,0},{2,1},{3,2},{5,4},{6,5},{7,6},{9,8},{10,9},{11,10},{13,12},{... | collective-permute-start | bytes 6920 | tf_op jit(solution)/shard_map/ppermute | solution.py:22
  51.7 31.1 %collective-permute-start.10 = (f32[6,6,1,128]{3,2,1,0:T(1,128)S(1)}, f32[6,6,1,128]{3,2,1,0:T(1,128)S(1)}, u32[]{:S(2)}, u32[]{:S(2)}) collective-permute-start(f32[6,6,1,128]{3,2,1,0:T(1,128)S(1)} %get-tuple-element.148), channel_id=1, source_target_pairs={{0,4},{4,8},{8,12},{1,5},{5,9},{9,13},{2,6},{6,10},{10,14},{3,7},{... | collective-permute-start | bytes 55304 | tf_op jit(solution)/shard_map/ppermute | solution.py:21
  63.3 19.5 %collective-permute-start.9 = (f32[6,6,1,128]{3,2,1,0:T(1,128)S(1)}, f32[6,6,1,128]{3,2,1,0:T(1,128)S(1)}, u32[]{:S(2)}, u32[]{:S(2)}) collective-permute-start(f32[6,6,1,128]{3,2,1,0:T(1,128)S(1)} %get-tuple-element.149), channel_id=1, source_target_pairs={{4,0},{8,4},{12,8},{5,1},{9,5},{13,9},{6,2},{10,6},{14,10},{7,3},{... | collective-permute-start | bytes 55304 | tf_op jit(solution)/shard_map/ppermute | solution.py:22
  68.1 14.7 %collective-permute-start.11 = (f32[6,6,8,1]{3,2,1,0:T(8,128)S(1)}, f32[6,6,8,1]{3,2,1,0:T(8,128)S(1)}, u32[]{:S(2)}, u32[]{:S(2)}) collective-permute-start(f32[6,6,8,1]{3,2,1,0:T(8,128)S(1)} %get-tuple-element.146), channel_id=1, source_target_pairs={{1,0},{2,1},{3,2},{5,4},{6,5},{7,6},{9,8},{10,9},{11,10},{13,12},{... | collective-permute-start | bytes 3464 | tf_op jit(solution)/shard_map/ppermute | solution.py:22
  84.2 31.6 %collective-permute-start.16 = (f32[12,6,1,128]{3,2,1,0:T(1,128)S(1)}, f32[12,6,1,128]{3,2,1,0:T(1,128)S(1)}, u32[]{:S(2)}, u32[]{:S(2)}) collective-permute-start(f32[12,6,1,128]{3,2,1,0:T(1,128)S(1)} %get-tuple-element.80), channel_id=1, source_target_pairs={{0,4},{4,8},{8,12},{1,5},{5,9},{9,13},{2,6},{6,10},{10,14},{3,7},{... | collective-permute-start | bytes 110600 | tf_op jit(solution)/shard_map/ppermute | solution.py:21
  96.1 19.7 %collective-permute-start.15 = (f32[12,6,1,128]{3,2,1,0:T(1,128)S(1)}, f32[12,6,1,128]{3,2,1,0:T(1,128)S(1)}, u32[]{:S(2)}, u32[]{:S(2)}) collective-permute-start(f32[12,6,1,128]{3,2,1,0:T(1,128)S(1)} %get-tuple-element.81), channel_id=1, source_target_pairs={{4,0},{8,4},{12,8},{5,1},{9,5},{13,9},{6,2},{10,6},{14,10},{7,3},{... | collective-permute-start | bytes 110600 | tf_op jit(solution)/shard_map/ppermute | solution.py:22
  100.9 14.9 %collective-permute-start.17 = (f32[12,6,8,1]{3,2,1,0:T(8,128)S(1)}, f32[12,6,8,1]{3,2,1,0:T(8,128)S(1)}, u32[]{:S(2)}, u32[]{:S(2)}) collective-permute-start(f32[12,6,8,1]{3,2,1,0:T(8,128)S(1)} %get-tuple-element.78), channel_id=1, source_target_pairs={{1,0},{2,1},{3,2},{5,4},{6,5},{7,6},{9,8},{10,9},{11,10},{13,12},{... | collective-permute-start | bytes 6920 | tf_op jit(solution)/shard_map/ppermute | solution.py:22
  117.4 32.1 %collective-permute-start.22 = (f32[6,6,1,128]{3,2,1,0:T(1,128)S(1)}, f32[6,6,1,128]{3,2,1,0:T(1,128)S(1)}, u32[]{:S(2)}, u32[]{:S(2)}) collective-permute-start(f32[6,6,1,128]{3,2,1,0:T(1,128)S(1)} %get-tuple-element.136), channel_id=1, source_target_pairs={{0,4},{4,8},{8,12},{1,5},{5,9},{9,13},{2,6},{6,10},{10,14},{3,7},{... | collective-permute-start | bytes 55304 | tf_op jit(solution)/shard_map/ppermute | solution.py:21
  129.9 19.5 %collective-permute-start.21 = (f32[6,6,1,128]{3,2,1,0:T(1,128)S(1)}, f32[6,6,1,128]{3,2,1,0:T(1,128)S(1)}, u32[]{:S(2)}, u32[]{:S(2)}) collective-permute-start(f32[6,6,1,128]{3,2,1,0:T(1,128)S(1)} %get-tuple-element.137), channel_id=1, source_target_pairs={{4,0},{8,4},{12,8},{5,1},{9,5},{13,9},{6,2},{10,6},{14,10},{7,3},{... | collective-permute-start | bytes 55304 | tf_op jit(solution)/shard_map/ppermute | solution.py:22
  150.8 31.6 %collective-permute-start.28 = (f32[12,6,1,128]{3,2,1,0:T(1,128)S(1)}, f32[12,6,1,128]{3,2,1,0:T(1,128)S(1)}, u32[]{:S(2)}, u32[]{:S(2)}) collective-permute-start(f32[12,6,1,128]{3,2,1,0:T(1,128)S(1)} %get-tuple-element.74), channel_id=1, source_target_pairs={{0,4},{4,8},{8,12},{1,5},{5,9},{9,13},{2,6},{6,10},{10,14},{3,7},{... | collective-permute-start | bytes 110600 | tf_op jit(solution)/shard_map/ppermute | solution.py:21
  162.8 19.7 %collective-permute-start.27 = (f32[12,6,1,128]{3,2,1,0:T(1,128)S(1)}, f32[12,6,1,128]{3,2,1,0:T(1,128)S(1)}, u32[]{:S(2)}, u32[]{:S(2)}) collective-permute-start(f32[12,6,1,128]{3,2,1,0:T(1,128)S(1)} %get-tuple-element.75), channel_id=1, source_target_pairs={{4,0},{8,4},{12,8},{5,1},{9,5},{13,9},{6,2},{10,6},{14,10},{7,3},{... | collective-permute-start | bytes 110600 | tf_op jit(solution)/shard_map/ppermute | solution.py:22
  167.6 14.9 %collective-permute-start.29 = (f32[12,6,8,1]{3,2,1,0:T(8,128)S(1)}, f32[12,6,8,1]{3,2,1,0:T(8,128)S(1)}, u32[]{:S(2)}, u32[]{:S(2)}) collective-permute-start(f32[12,6,8,1]{3,2,1,0:T(8,128)S(1)} %get-tuple-element.72), channel_id=1, source_target_pairs={{1,0},{2,1},{3,2},{5,4},{6,5},{7,6},{9,8},{10,9},{11,10},{13,12},{... | collective-permute-start | bytes 6920 | tf_op jit(solution)/shard_map/ppermute | solution.py:22
  184.0 32.1 %collective-permute-start.34 = (f32[6,6,1,128]{3,2,1,0:T(1,128)S(1)}, f32[6,6,1,128]{3,2,1,0:T(1,128)S(1)}, u32[]{:S(2)}, u32[]{:S(2)}) collective-permute-start(f32[6,6,1,128]{3,2,1,0:T(1,128)S(1)} %get-tuple-element.124), channel_id=1, source_target_pairs={{0,4},{4,8},{8,12},{1,5},{5,9},{9,13},{2,6},{6,10},{10,14},{3,7},{... | collective-permute-start | bytes 55304 | tf_op jit(solution)/shard_map/ppermute | solution.py:21
  196.6 19.5 %collective-permute-start.33 = (f32[6,6,1,128]{3,2,1,0:T(1,128)S(1)}, f32[6,6,1,128]{3,2,1,0:T(1,128)S(1)}, u32[]{:S(2)}, u32[]{:S(2)}) collective-permute-start(f32[6,6,1,128]{3,2,1,0:T(1,128)S(1)} %get-tuple-element.125), channel_id=1, source_target_pairs={{4,0},{8,4},{12,8},{5,1},{9,5},{13,9},{6,2},{10,6},{14,10},{7,3},{... | collective-permute-start | bytes 55304 | tf_op jit(solution)/shard_map/ppermute | solution.py:22
  201.4 14.7 %collective-permute-start.35 = (f32[6,6,8,1]{3,2,1,0:T(8,128)S(1)}, f32[6,6,8,1]{3,2,1,0:T(8,128)S(1)}, u32[]{:S(2)}, u32[]{:S(2)}) collective-permute-start(f32[6,6,8,1]{3,2,1,0:T(8,128)S(1)} %get-tuple-element.122), channel_id=1, source_target_pairs={{1,0},{2,1},{3,2},{5,4},{6,5},{7,6},{9,8},{10,9},{11,10},{13,12},{... | collective-permute-start | bytes 3464 | tf_op jit(solution)/shard_map/ppermute | solution.py:22
  217.5 31.6 %collective-permute-start.40 = (f32[12,6,1,128]{3,2,1,0:T(1,128)S(1)}, f32[12,6,1,128]{3,2,1,0:T(1,128)S(1)}, u32[]{:S(2)}, u32[]{:S(2)}) collective-permute-start(f32[12,6,1,128]{3,2,1,0:T(1,128)S(1)} %get-tuple-element.68), channel_id=1, source_target_pairs={{0,4},{4,8},{8,12},{1,5},{5,9},{9,13},{2,6},{6,10},{10,14},{3,7},{... | collective-permute-start | bytes 110600 | tf_op jit(solution)/shard_map/ppermute | solution.py:21
  229.5 19.7 %collective-permute-start.39 = (f32[12,6,1,128]{3,2,1,0:T(1,128)S(1)}, f32[12,6,1,128]{3,2,1,0:T(1,128)S(1)}, u32[]{:S(2)}, u32[]{:S(2)}) collective-permute-start(f32[12,6,1,128]{3,2,1,0:T(1,128)S(1)} %get-tuple-element.69), channel_id=1, source_target_pairs={{4,0},{8,4},{12,8},{5,1},{9,5},{13,9},{6,2},{10,6},{14,10},{7,3},{... | collective-permute-start | bytes 110600 | tf_op jit(solution)/shard_map/ppermute | solution.py:22
  234.2 14.9 %collective-permute-start.41 = (f32[12,6,8,1]{3,2,1,0:T(8,128)S(1)}, f32[12,6,8,1]{3,2,1,0:T(8,128)S(1)}, u32[]{:S(2)}, u32[]{:S(2)}) collective-permute-start(f32[12,6,8,1]{3,2,1,0:T(8,128)S(1)} %get-tuple-element.66), channel_id=1, source_target_pairs={{1,0},{2,1},{3,2},{5,4},{6,5},{7,6},{9,8},{10,9},{11,10},{13,12},{... | collective-permute-start | bytes 6920 | tf_op jit(solution)/shard_map/ppermute | solution.py:22
  251.4 22.0 %collective-permute-start.48 = (f32[6,6,8,1]{3,2,1,0:T(8,128)S(1)}, f32[6,6,8,1]{3,2,1,0:T(8,128)S(1)}, u32[]{:S(2)}, u32[]{:S(2)}) collective-permute-start(f32[6,6,8,1]{3,2,1,0:T(8,128)S(1)} %get-tuple-element.109), channel_id=1, source_target_pairs={{0,1},{1,2},{2,3},{4,5},{5,6},{6,7},{8,9},{9,10},{10,11},{12,13},{... | collective-permute-start | bytes 3464 | tf_op jit(solution)/shard_map/ppermute | solution.py:21
  254.2 29.5 %collective-permute-start.45 = (f32[6,6,1,128]{3,2,1,0:T(1,128)S(1)}, f32[6,6,1,128]{3,2,1,0:T(1,128)S(1)}, u32[]{:S(2)}, u32[]{:S(2)}) collective-permute-start(f32[6,6,1,128]{3,2,1,0:T(1,128)S(1)} %get-tuple-element.110), channel_id=1, source_target_pairs={{4,0},{8,4},{12,8},{5,1},{9,5},{13,9},{6,2},{10,6},{14,10},{7,3},{... | collective-permute-start | bytes 55304 | tf_op jit(solution)/shard_map/ppermute | solution.py:22
  256.2 27.6 %collective-permute-start.46 = (f32[6,6,1,128]{3,2,1,0:T(1,128)S(1)}, f32[6,6,1,128]{3,2,1,0:T(1,128)S(1)}, u32[]{:S(2)}, u32[]{:S(2)}) collective-permute-start(f32[6,6,1,128]{3,2,1,0:T(1,128)S(1)} %get-tuple-element.111), channel_id=1, source_target_pairs={{0,4},{4,8},{8,12},{1,5},{5,9},{9,13},{2,6},{6,10},{10,14},{3,7},{... | collective-permute-start | bytes 55304 | tf_op jit(solution)/shard_map/ppermute | solution.py:21
  (32 other events, 303.0 us)
where the time goes:
time: 287 us; the launch traced here: 285 us
  starting transfers between devices  262 us (91%)
  other arithmetic  9.73 us (3%)
  waiting for transfers between devices  6.17 us (2%)
  between operations  5.07 us (2%)
    ppermute x16, starting transfers between devices, with_halo(): lax.ppermute(last, axis, up)  119 us
    ppermute x8, starting transfers between devices, with_halo_2(): lax.ppermute(lax.slice_in_dim(block, 0, width, axis=dim), axis, backward)  80.8 us
    ppermute x16, starting transfers between devices, with_halo(): lax.ppermute(leading, axis, [(b, a) for a, b in up])  34.9 us
    ppermute x8, starting transfers between devices, with_halo_2(): lax.ppermute(lax.slice_in_dim(block, block.shape[dim] - width, None, axis...  15.4 us
    ppermute x1, starting transfers between devices, from_behind(): lax.ppermute(value, axis, [(source, source + steps) for source in range(l...  12.3 us
  transfers between devices with their start and end apart: 49, of which 12 were waited for; matrix products, arithmetic and copies ran while one was open for 2% of the time, Pallas kernels for 0%

commit v1 on v0

v1 whole, which is shorter than its diff:
```python
import functools

import jax
import jax.numpy as jnp
from jax import lax
from jax.experimental import pallas as pl
from jax.experimental.pallas import tpu as pltpu
from jax.sharding import PartitionSpec as P

STEPS = 4
H = 0.15
PAIRS = ((0, 5, 4), (5, 1, 3), (4, 3, 2))

VB, CB, LB, MB = 120, 168, 176, 182
N = 192
PA, PV, PS, PR, PL, NP1 = 0, 36, 45, 69, 72, 76
NF = 81


def swaps(count, first):
    out = []
    for i in range(first, count - 1, 2):
        out += [(i, i + 1), (i + 1, i)]
    return out


def both_swaps(value_a, value_b, axis):
    count = lax.axis_size(axis)
    second = lax.ppermute(value_b, axis, swaps(count, 1))
    first = lax.ppermute(value_a, axis, swaps(count, 0))
    return first, second


def pack_kernel(sc, fv, fs, rho, lam, av, as_, out_a, out_b):
    odd, off = sc[0], sc[1]
    for out, up in ((out_a, 1 - odd), (out_b, odd)):
        for i in range(4):
            row = jnp.maximum(2 * up + i - off, 0)
            for c in range(3):
                out[PA + i * 9 + c] = av[c, row]
            for c in range(6):
                out[PA + i * 9 + 3 + c] = as_[c, row]
                out[PS + i * 6 + c] = fs[c, i]
        for i in range(3):
            for c in range(3):
                out[PV + i * 3 + c] = fv[c, i + up]
            out[PR + i] = rho[i + up]
        for i in range(2):
            for c in range(2):
                out[PL + i * 2 + c] = lam[c, i]


def window_kernel(sc, fv, fs, rho, lam, av, as_, ra, rb, w):
    odd, off, noff = sc[0], sc[1], sc[2]
    low_is_a = odd == 1

    def low(n):
        return jnp.where(low_is_a, ra[n], rb[n])

    def high(n):
        return jnp.where(low_is_a, rb[n], ra[n])

    def adjoint(p, ref, c, slot):
        if p < 2:
            return low(PA + p * 9 + slot)
        if p > 7:
            return high(PA + (p - 6) * 9 + slot)
        j = p - 2
        own = ref[c, jnp.clip(j - off, 0, 5)]
        if j < 2:
            return jnp.where(j < off, low(PA + p * 9 + slot), own)
        if j > 3:
            return jnp.where(j - 4 < noff, own, high(PA + (p - 6) * 9 + slot))
        return own

    for p in range(10):
        for c in range(6):
            if p < 2:
                f = low(PS + (p + 2) * 6 + c)
            elif p < 6:
                f = fs[c, p - 2]
            else:
                f = high(PS + (p - 6) * 6 + c)
            w[p * 12 + c] = f
            w[p * 12 + 6 + c] = adjoint(p, as_, c, 3 + c)
    for p in range(1, 9):
        for c in range(3):
            if p < 2:
                f = low(PV + 2 * 3 + c)
            elif p < 6:
                f = fv[c, p - 2]
            else:
                f = high(PV + (p - 6) * 3 + c)
            w[VB + (p - 1) * 6 + c] = f
            w[VB + (p - 1) * 6 + 3 + c] = adjoint(p, av, c, c)
        if p < 2:
            r = low(PR + 2)
        elif p < 6:
            r = rho[p - 2]
        else:
            r = high(PR + p - 6)
        live = r > 0.0
        w[CB + p - 1] = jnp.where(live, (0.5 * H) / jnp.where(live, r, 1.0), 0.0)
    for p in range(2, 8):
        for c, base in ((0, LB), (1, MB)):
            m = lam[c, p - 2] if p < 6 else high(PL + (p - 6) * 2 + c)
            w[base + p - 2] = (0.5 * H) * m
    for n in range(188, N):
        w[n] = jnp.zeros((8, 128), jnp.float32)


def lanes():
    return lax.broadcasted_iota(jnp.int32, (8, 128), 1)


def edge_kernel(sc, w, ga, gb, out_a, out_b):
    gy_odd, gz_odd = sc[3], sc[4]
    lane = lanes()

    def group(g, carry):
        for out, up in ((out_a, 1 - gz_odd), (out_b, gz_odd)):
            for t in range(3):
                acc = jnp.zeros((8, 128), jnp.float32)
                for k in range(16):
                    n = g * 16 + k
                    if t == 1:
                        x = w[n]
                    else:
                        x = jnp.where((gy_odd == 1) == (t == 0), ga[n], gb[n])
                    x = pltpu.roll(x, lax.rem(8 * k + 8 * up, 128), 1)
                    acc = jnp.where((lane >= 8 * k) & (lane < 8 * k + 8), x, acc)
                out[t * 12 + g] = acc
        return carry

    lax.fori_loop(0, 12, group, 0)


def rows_diff(x):
    return pltpu.roll(x, 23, 0) - pltpu.roll(x, 1, 0)


def lanes_diff(x):
    return pltpu.roll(x, 255, 1) - pltpu.roll(x, 1, 1)


def one_step(st, kern):
    def velocity(p, carry):
        coef = st[CB + p - 1]
        for q in range(2):
            base = p * 12 + q * 6
            for i in range(3):
                x, y, z = PAIRS[i]
                force = st[base + 12 + x] - st[base - 12 + x]
                force = force + rows_diff(st[base + y]) + lanes_diff(st[base + z])
                n = VB + (p - 1) * 6 + q * 3 + i
                if q == 0:
                    st[n] = st[n] - coef * force
                else:
                    st[n] = st[n] + coef * force
        return carry

    lax.fori_loop(1, 9, velocity, 0)

    def stress(p, carry):
        lam, mu = st[LB + p - 2], st[MB + p - 2]
        traces, diags, shears, vels = [], [], [], []
        for q in range(2):
            v = VB + (p - 1) * 6 + q * 3
            own = [st[v + i] for i in range(3)]
            dx = [st[v + 6 + i] - st[v - 6 + i] for i in range(3)]
            dy = [rows_diff(f) for f in own]
            dz = [lanes_diff(f) for f in own]
            diag = [dx[0], dy[1], dz[2]]
            shear = [dy[2] + dz[1], dx[2] + dz[0], dx[1] + dy[0]]
            trace = diag[0] + diag[1] + diag[2]
            iso = lam * trace
            s = p * 12 + q * 6
            for c in range(3):
                a = iso + (2.0 * mu) * diag[c]
                b = mu * shear[c]
                if q == 0:
                    st[s + c] = st[s + c] - a
                    st[s + 3 + c] = st[s + 3 + c] - b
                else:
                    st[s + c] = st[s + c] + a
                    st[s + 3 + c] = st[s + 3 + c] + b
            cut = lambda f: f[8:16, 0:128]
            traces.append(cut(trace))
            diags.append([cut(f) for f in diag])
            shears.append([cut(f) for f in shear])
            vels.append([cut(f) for f in own])
        dot = lambda pair: (
            pair[0][0] * pair[1][0] + pair[0][1] * pair[1][1] + pair[0][2] * pair[1][2]
        )
        kern[p - 2] += H * dot(vels)
        kern[6 + p - 2] += (0.25 * H) * (traces[0] * traces[1])
        kern[12 + p - 2] += (0.5 * H) * dot(diags) + (0.25 * H) * dot(shears)
        return carry

    lax.fori_loop(2, 8, stress, 0)


def write_faces(st, face):
    lane = lanes()
    for t in range(3):
        for g in range(3):
            acc = jnp.zeros((8, 128), jnp.float32)
            for k in range(8):
                n = g * 8 + k
                face[t * 24 + n] = st[48 + n, 8 * t : 8 * t + 8, 0:128]
                x = st[48 + n, 8 * t : 8 * t + 8, 128:256]
                x = pltpu.roll(x, (8 + 16 * k) % 128, 1)
                acc = jnp.where((lane >= 16 * k) & (lane < 16 * k + 16), x, acc)
            face[72 + t * 3 + g] = acc


def read_faces(sc, ra, rb, st):
    lane = lanes()
    halo = (lane < 8) | (lane >= 120)
    low_is_a = sc[0] == 1
    for low in (True, False):
        first = 0 if low else 96
        pick = low_is_a if low else jnp.logical_not(low_is_a)
        get = lambda n: jnp.where(pick, ra[n], rb[n])
        for t in range(3):
            for g in range(3):
                packed = get(72 + t * 3 + g)
                for k in range(8):
                    n = g * 8 + k
                    st[first + n, 8 * t : 8 * t + 8, 0:128] = get(t * 24 + n)
                    x = pltpu.roll(packed, (120 - 16 * k) % 128, 1)
                    st[first + n, 8 * t : 8 * t + 8, 128:256] = jnp.where(halo, x, 0.0)


def first_kernel(sc, w, ga, gb, za, zb, st, kern, face):
    gy_odd, gz_odd = sc[3], sc[4]
    lane = lanes()

    def group(g, carry):
        for t in range(3):
            a, b = za[t * 12 + g], zb[t * 12 + g]
            low = jnp.where(gz_odd == 1, a, b)
            high = jnp.where(gz_odd == 1, b, a)
            for k in range(16):
                n = g * 16 + k
                if t == 1:
                    x = w[n]
                else:
                    x = jnp.where((gy_odd == 1) == (t == 0), ga[n], gb[n])
                st[n, 8 * t : 8 * t + 8, 0:128] = x
                h = pltpu.roll(high, (128 - 8 * k) % 128, 1)
                l = pltpu.roll(low, (120 - 8 * k) % 128, 1)
                st[n, 8 * t : 8 * t + 8, 128:256] = jnp.where(
                    lane < 8, h, jnp.where(lane >= 120, l, 0.0)
                )
        return carry

    lax.fori_loop(0, 12, group, 0)
    for n in range(18):
        kern[n] = jnp.zeros((8, 128), jnp.float32)
    one_step(st, kern)
    write_faces(st, face)


def carry_over(st_in, kern_in, st, kern):
    def move(n, carry):
        st[n] = st_in[n]
        return carry

    lax.fori_loop(24, 96, move, 0, unroll=4)
    lax.fori_loop(VB, 188, move, 0, unroll=4)
    for n in range(18):
        kern[n] = kern_in[n]


def step_kernel(sc, st_in, kern_in, ra, rb, st, kern, face):
    carry_over(st_in, kern_in, st, kern)
    read_faces(sc, ra, rb, st)
    one_step(st, kern)
    write_faces(st, face)


def last_kernel(sc, st_in, kern_in, ra, rb, dens, modu, st, kern):
    carry_over(st_in, kern_in, st, kern)
    read_faces(sc, ra, rb, st)
    one_step(st, kern)
    off, noff = sc[1], sc[2]
    extent = 4 + noff - off
    for r in range(6):
        row = jnp.minimum(off + r, 5)
        live = r < extent
        dens[r] = jnp.where(live, kern[row], 0.0)
        modu[0, r] = jnp.where(live, kern[6 + row], 0.0)
        modu[1, r] = jnp.where(live, kern[12 + row], 0.0)


def call(kernel, outs, args, scratch=()):
    vmem = pl.BlockSpec(memory_space=pltpu.VMEM)
    return pl.pallas_call(
        kernel,
        out_shape=[jax.ShapeDtypeStruct(s, jnp.float32) for s in outs],
        in_specs=[pl.BlockSpec(memory_space=pltpu.SMEM)] + [vmem] * (len(args) - 1),
        out_specs=[vmem] * len(outs),
        scratch_shapes=[pltpu.VMEM(s, jnp.float32) for s in scratch],
        name=kernel.__name__,
    )(*args)


def shards(fwd_velocity, fwd_stress, density, lame, adj_velocity, adj_stress, offsets):
    blocks = lax.axis_size("grp")
    place = lax.axis_index("grp")
    padded = jnp.concatenate([offsets.astype(jnp.int32), jnp.zeros((1,), jnp.int32)])
    pair = lax.dynamic_slice_in_dim(padded, place, 2, 0)
    spot = jnp.arange(8, dtype=jnp.int32)
    sc = jnp.where(
        spot == 0,
        place % 2,
        jnp.where(spot == 3, lax.axis_index("gy") % 2, lax.axis_index("gz") % 2),
    ).astype(jnp.int32)
    sc = jnp.where(spot == 1, pair[0], jnp.where(spot == 2, pair[1], sc))

    raw = (fwd_velocity, fwd_stress, density, lame, adj_velocity, adj_stress)
    send_a, send_b = call(pack_kernel, [(NP1, 8, 128)] * 2, (sc, *raw))
    recv = both_swaps(send_a, send_b, "grp")
    (win,) = call(window_kernel, [(N, 8, 128)], (sc, *raw, *recv))
    ga, gb = both_swaps(win, win, "gy")
    edges = call(edge_kernel, [(36, 8, 128)] * 2, (sc, win, ga, gb))
    za, zb = both_swaps(*edges, "gz")
    state, kern, face = call(
        first_kernel,
        [(N, 24, 256), (18, 8, 128), (NF, 8, 128)],
        (sc, win, ga, gb, za, zb),
    )
    for _ in range(STEPS - 2):
        recv = both_swaps(face, face, "grp")
        state, kern, face = call(
            step_kernel,
            [(N, 24, 256), (18, 8, 128), (NF, 8, 128)],
            (sc, state, kern, *recv),
        )
    recv = both_swaps(face, face, "grp")
    dens, modu = call(
        last_kernel,
        [(6, 8, 128), (2, 6, 8, 128)],
        (sc, state, kern, *recv),
        [(N, 24, 256), (18, 8, 128)],
    )
    return dens, modu


def solution(mesh):
    return jax.shard_map(
        shards,
        mesh=mesh,
        in_specs=(
            P(None, "grp", "gy", "gz"),
            P(None, "grp", "gy", "gz"),
            P("grp", "gy", "gz"),
            P(None, "grp", "gy", "gz"),
            P(None, "grp", "gy", "gz"),
            P(None, "grp", "gy", "gz"),
            P(),
        ),
        out_specs=(P("grp", "gy", "gz"), P(None, "grp", "gy", "gz")),
        check_vma=False,
    )
```

time: 287 us -> 187 us (0.65)
  the two profiles are of different devices: /device:TPU:37 before, /device:TPU:420 now
where the time goes in v1:
time: 187 us
  waiting for transfers between devices  74.6 us (40%)
  starting transfers between devices  51.9 us (28%)
  Pallas kernels  50.9 us (27%)
  local copies, waits for them, and re-layouts  6.02 us (3%)
  other arithmetic  2.56 us (1%)
    ppermute x6, waiting for transfers between devices, both_swaps(): second = lax.ppermute(value_b, axis, swaps(count, 1))  56.2 us
    pallas_call x7, Pallas kernels, call(): pl.pallas_call(kernel, out_shape=[jax.ShapeDtypeStruct(s, jnp.float32) fo...  50.9 us
    ppermute x6, starting transfers between devices, both_swaps(): second = lax.ppermute(value_b, axis, swaps(count, 1))  33.8 us
    ppermute x6, waiting for transfers between devices, both_swaps(): first = lax.ppermute(value_a, axis, swaps(count, 0))  18.4 us
    ppermute x6, starting transfers between devices, both_swaps(): first = lax.ppermute(value_a, axis, swaps(count, 0))  18.1 us
    unnamed x24, local copies, waits for them, and re-layouts  5.36 us
  transfers between devices with their start and end apart: 12, of which 11 were waited for; matrix products, arithmetic and copies ran while one was open for 0% of the time, Pallas kernels for 0%

profile of v1, /device:TPU:420, one launch (start us, length us, event | category | flops | bytes accessed | tf_op | source)
XLA Modules:
  0.0 186.8 jit_solution(5914830966640366968)
XLA Ops:
  3.9 1.9 %pack_kernel.1 = (f32[76,8,128]{2,1,0:T(8,128)}, f32[76,8,128]{2,1,0:T(8,128)}) custom-call(s32[8]{0:T(128)} %compare_select_fusion.3.sc, f32[3,4,8,128]{3,2,1,0:T(8,128)} %fv.3, f32[6,4,8,128]{3,2,1,0:T(8,128)} %fs.3, f32[4,8,128]{2,1,0:T(8,128)} %rho.3, f32[2,4,8,128]{3,2,1,0:T(8,128)} %lam.3, f32[3,6,8,128]{3,2,1,0:T(8,128)} %av.3, f32[6,6,8,128]{3,2,1,0:T(8,128)} %as_.3), custom_call_target="tpu_custom_call" | custom-call | tf_op jit(solution)/shard_map/pack_kernel/pallas_call | solution.py:299
  5.8 4.0 %collective-permute-start = (f32[76,8,128]{2,1,0:T(8,128)}, f32[76,8,128]{2,1,0:T(8,128)S(1)}, u32[]{:S(2)}, u32[]{:S(2)}) collective-permute-start(f32[76,8,128]{2,1,0:T(8,128)} %get-tuple-element.15), channel_id=1, source_target_pairs={{0,16},{16,0},{32,48},{48,32},{64,80},{80,64},{96,112},{112,96},{1... | collective-permute-start | bytes 933896 | tf_op jit(solution)/shard_map/ppermute | solution.py:30
  9.8 6.0 %collective-permute-start.1 = (f32[76,8,128]{2,1,0:T(8,128)}, f32[76,8,128]{2,1,0:T(8,128)S(1)}, u32[]{:S(2)}, u32[]{:S(2)}) collective-permute-start(f32[76,8,128]{2,1,0:T(8,128)} %get-tuple-element.16), channel_id=1, source_target_pairs={{16,32},{32,16},{48,64},{64,48},{80,96},{96,80},{112,128},{128,112... | collective-permute-start | bytes 933896 | tf_op jit(solution)/shard_map/ppermute | solution.py:29
  17.7 10.2 %collective-permute-done.1.rb = f32[76,8,128]{2,1,0:T(8,128)S(1)} collective-permute-done((f32[76,8,128]{2,1,0:T(8,128)}, f32[76,8,128]{2,1,0:T(8,128)S(1)}, u32[]{:S(2)}, u32[]{:S(2)}) %collective-permute-start.1) | collective-permute-done | bytes 311328 | tf_op jit(solution)/shard_map/ppermute | solution.py:29
  28.6 2.3 %window_kernel.1.w = f32[192,8,128]{2,1,0:T(8,128)} custom-call(s32[8]{0:T(128)} %compare_select_fusion.3.sc, f32[3,4,8,128]{3,2,1,0:T(8,128)} %fv.3, f32[6,4,8,128]{3,2,1,0:T(8,128)} %fs.3, f32[4,8,128]{2,1,0:T(8,128)} %rho.3, f32[2,4,8,128]{3,2,1,0:T(8,128)} %lam.3, f32[3,6,8,128]{3,2,1,0:T(8,128)} %av.3, f32[6,6,8,128]{3,2,1,0:T(8,128)} %as_.3, ...), custom_call_target="tpu_custom_call" | custom-call | tf_op jit(solution)/shard_map/window_kernel/pallas_call | solution.py:299
  32.8 1.9 %collective-permute-start.2 = (f32[192,8,128]{2,1,0:T(8,128)}, f32[192,8,128]{2,1,0:T(8,128)S(1)}, u32[]{:S(2)}, u32[]{:S(2)}) collective-permute-start(f32[192,8,128]{2,1,0:T(8,128)} %window_kernel.1.w), channel_id=1, source_target_pairs={{0,4},{4,0},{8,12},{12,8},{1,5},{5,1},{9,13},{13,9},{2,6},{6,2},{1... | collective-permute-start | bytes 2359304 | tf_op jit(solution)/shard_map/ppermute | solution.py:30
  34.7 18.4 %collective-permute-done.3.gb = f32[192,8,128]{2,1,0:T(8,128)S(1)} collective-permute-done((f32[192,8,128]{2,1,0:T(8,128)}, f32[192,8,128]{2,1,0:T(8,128)S(1)}, u32[]{:S(2)}, u32[]{:S(2)}) %collective-permute-start.3) | collective-permute-done | bytes 786464 | tf_op jit(solution)/shard_map/ppermute | solution.py:29
  54.9 4.6 %edge_kernel.1 = (f32[36,8,128]{2,1,0:T(8,128)}, f32[36,8,128]{2,1,0:T(8,128)}) custom-call(s32[8]{0:T(128)} %compare_select_fusion.3.sc, f32[192,8,128]{2,1,0:T(8,128)} %window_kernel.1.w, f32[192,8,128]{2,1,0:T(8,128)} %copy-done.1, f32[192,8,128]{2,1,0:T(8,128)} %copy-done), custom_call_target="tpu_custom_call" | custom-call | tf_op jit(solution)/shard_map/edge_kernel/pallas_call | solution.py:299
  59.5 3.1 %collective-permute-start.4 = (f32[36,8,128]{2,1,0:T(8,128)}, f32[36,8,128]{2,1,0:T(8,128)S(1)}, u32[]{:S(2)}, u32[]{:S(2)}) collective-permute-start(f32[36,8,128]{2,1,0:T(8,128)} %get-tuple-element.17), channel_id=1, source_target_pairs={{0,1},{1,0},{2,3},{3,2},{4,5},{5,4},{6,7},{7,6},{8,9},{9,8},{10,11... | collective-permute-start | bytes 442376 | tf_op jit(solution)/shard_map/ppermute | solution.py:30
  64.5 2.2 %collective-permute-done.4.za = f32[36,8,128]{2,1,0:T(8,128)S(1)} collective-permute-done((f32[36,8,128]{2,1,0:T(8,128)}, f32[36,8,128]{2,1,0:T(8,128)S(1)}, u32[]{:S(2)}, u32[]{:S(2)}) %collective-permute-start.4) | collective-permute-done | bytes 147488 | tf_op jit(solution)/shard_map/ppermute | solution.py:30
  66.7 3.1 %collective-permute-done.5.zb = f32[36,8,128]{2,1,0:T(8,128)S(1)} collective-permute-done((f32[36,8,128]{2,1,0:T(8,128)}, f32[36,8,128]{2,1,0:T(8,128)S(1)}, u32[]{:S(2)}, u32[]{:S(2)}) %collective-permute-start.5) | collective-permute-done | bytes 147488 | tf_op jit(solution)/shard_map/ppermute | solution.py:29
  70.5 11.3 %first_kernel.1 = (f32[192,24,256]{2,1,0:T(8,128)}, f32[18,8,128]{2,1,0:T(8,128)}, f32[81,8,128]{2,1,0:T(8,128)}) custom-call(s32[8]{0:T(128)} %compare_select_fusion.3.sc, f32[192,8,128]{2,1,0:T(8,128)} %window_kernel.1.w, f32[192,8,128]{2,1,0:T(8,128)} %copy-done.1, f32[192,8,128]{2,1,0:T(8,128)} %copy-done, f32[36,8,128]{2,1,0:T(8,128)} %copy-done.10, ...), custom_call_target="tpu_custom_call" | custom-call | tf_op jit(solution)/shard_map/first_kernel/pallas_call | solution.py:299
  81.8 14.0 %collective-permute-start.7 = (f32[81,8,128]{2,1,0:T(8,128)}, f32[81,8,128]{2,1,0:T(8,128)S(1)}, u32[]{:S(2)}, u32[]{:S(2)}) collective-permute-start(f32[81,8,128]{2,1,0:T(8,128)} %get-tuple-element.21), channel_id=1, source_target_pairs={{16,32},{32,16},{48,64},{64,48},{80,96},{96,80},{112,128},{128,112... | collective-permute-start | bytes 995336 | tf_op jit(solution)/shard_map/ppermute | solution.py:29
  95.9 5.2 %collective-permute-start.6 = (f32[81,8,128]{2,1,0:T(8,128)}, f32[81,8,128]{2,1,0:T(8,128)S(1)}, u32[]{:S(2)}, u32[]{:S(2)}) collective-permute-start(f32[81,8,128]{2,1,0:T(8,128)} %get-tuple-element.21), channel_id=1, source_target_pairs={{0,16},{16,0},{32,48},{48,32},{64,80},{80,64},{96,112},{112,96},{1... | collective-permute-start | bytes 995336 | tf_op jit(solution)/shard_map/ppermute | solution.py:30
  101.1 2.5 %collective-permute-done.7.rb = f32[81,8,128]{2,1,0:T(8,128)S(1)} collective-permute-done((f32[81,8,128]{2,1,0:T(8,128)}, f32[81,8,128]{2,1,0:T(8,128)S(1)}, u32[]{:S(2)}, u32[]{:S(2)}) %collective-permute-start.7) | collective-permute-done | bytes 331808 | tf_op jit(solution)/shard_map/ppermute | solution.py:29
  103.6 9.1 %collective-permute-done.6.ra = f32[81,8,128]{2,1,0:T(8,128)S(1)} collective-permute-done((f32[81,8,128]{2,1,0:T(8,128)}, f32[81,8,128]{2,1,0:T(8,128)S(1)}, u32[]{:S(2)}, u32[]{:S(2)}) %collective-permute-start.6) | collective-permute-done | bytes 331808 | tf_op jit(solution)/shard_map/ppermute | solution.py:30
  113.4 10.8 %step_kernel.2 = (f32[192,24,256]{2,1,0:T(8,128)}, f32[18,8,128]{2,1,0:T(8,128)}, f32[81,8,128]{2,1,0:T(8,128)}) custom-call(s32[8]{0:T(128)} %compare_select_fusion.3.sc, f32[192,24,256]{2,1,0:T(8,128)} %get-tuple-element.19.st_in, f32[18,8,128]{2,1,0:T(8,128)} %get-tuple-element.20.kern_in, f32[81,8,128]{2,1,0:T(8,128)} %copy-done.5, f32[81,8,128]{2,1,0:T(8,128)} %copy-done.2), custom_call_target="tpu_custom_call" | custom-call | tf_op jit(solution)/shard_map/step_kernel/pallas_call | solution.py:299
  124.2 4.9 %collective-permute-start.9 = (f32[81,8,128]{2,1,0:T(8,128)}, f32[81,8,128]{2,1,0:T(8,128)S(1)}, u32[]{:S(2)}, u32[]{:S(2)}) collective-permute-start(f32[81,8,128]{2,1,0:T(8,128)} %get-tuple-element.24), channel_id=1, source_target_pairs={{16,32},{32,16},{48,64},{64,48},{80,96},{96,80},{112,128},{128,112... | collective-permute-start | bytes 995336 | tf_op jit(solution)/shard_map/ppermute | solution.py:29
  131.1 12.8 %collective-permute-done.9.rb = f32[81,8,128]{2,1,0:T(8,128)S(1)} collective-permute-done((f32[81,8,128]{2,1,0:T(8,128)}, f32[81,8,128]{2,1,0:T(8,128)S(1)}, u32[]{:S(2)}, u32[]{:S(2)}) %collective-permute-start.9) | collective-permute-done | bytes 331808 | tf_op jit(solution)/shard_map/ppermute | solution.py:29
  143.9 4.0 %collective-permute-done.8.ra = f32[81,8,128]{2,1,0:T(8,128)S(1)} collective-permute-done((f32[81,8,128]{2,1,0:T(8,128)}, f32[81,8,128]{2,1,0:T(8,128)S(1)}, u32[]{:S(2)}, u32[]{:S(2)}) %collective-permute-start.8) | collective-permute-done | bytes 331808 | tf_op jit(solution)/shard_map/ppermute | solution.py:30
  148.7 10.8 %step_kernel.3 = (f32[192,24,256]{2,1,0:T(8,128)}, f32[18,8,128]{2,1,0:T(8,128)}, f32[81,8,128]{2,1,0:T(8,128)}) custom-call(s32[8]{0:T(128)} %compare_select_fusion.3.sc, f32[192,24,256]{2,1,0:T(8,128)} %get-tuple-element.22.st_in, f32[18,8,128]{2,1,0:T(8,128)} %get-tuple-element.23.kern_in, f32[81,8,128]{2,1,0:T(8,128)} %copy-done.6, f32[81,8,128]{2,1,0:T(8,128)} %copy-done.3), custom_call_target="tpu_custom_call" | custom-call | tf_op jit(solution)/shard_map/step_kernel/pallas_call | solution.py:299
  159.5 5.1 %collective-permute-start.11 = (f32[81,8,128]{2,1,0:T(8,128)}, f32[81,8,128]{2,1,0:T(8,128)S(1)}, u32[]{:S(2)}, u32[]{:S(2)}) collective-permute-start(f32[81,8,128]{2,1,0:T(8,128)} %get-tuple-element.27), channel_id=1, source_target_pairs={{16,32},{32,16},{48,64},{64,48},{80,96},{96,80},{112,128},{128,112... | collective-permute-start | bytes 995336 | tf_op jit(solution)/shard_map/ppermute | solution.py:29
  166.5 9.2 %collective-permute-done.11.rb = f32[81,8,128]{2,1,0:T(8,128)S(1)} collective-permute-done((f32[81,8,128]{2,1,0:T(8,128)}, f32[81,8,128]{2,1,0:T(8,128)S(1)}, u32[]{:S(2)}, u32[]{:S(2)}) %collective-permute-start.11) | collective-permute-done | bytes 331808 | tf_op jit(solution)/shard_map/ppermute | solution.py:29
  177.7 9.1 %last_kernel.1 = (f32[6,8,128]{2,1,0:T(8,128)}, f32[2,6,8,128]{3,2,1,0:T(8,128)}) custom-call(s32[8]{0:T(128)} %compare_select_fusion.3.sc, f32[192,24,256]{2,1,0:T(8,128)} %get-tuple-element.25.st_in, f32[18,8,128]{2,1,0:T(8,128)} %get-tuple-element.26.kern_in, f32[81,8,128]{2,1,0:T(8,128)} %copy-done.7, f32[81,8,128]{2,1,0:T(8,128)} %copy-done.4), custom_call_target="tpu_custom_call" | custom-call | tf_op jit(solution)/shard_map/last_kernel/pallas_call | solution.py:299
  (35 shorter events, 19.4 us)
Async XLA Ops:
  5.8 11.9 %collective-permute-start = (f32[76,8,128]{2,1,0:T(8,128)}, f32[76,8,128]{2,1,0:T(8,128)S(1)}, u32[]{:S(2)}, u32[]{:S(2)}) collective-permute-start(f32[76,8,128]{2,1,0:T(8,128)} %get-tuple-element.15), channel_id=1, source_target_pairs={{0,16},{16,0},{32,48},{48,32},{64,80},{80,64},{96,112},{112,96},{1... | collective-permute-start | bytes 933896 | tf_op jit(solution)/shard_map/ppermute | solution.py:30
  9.8 18.1 %collective-permute-start.1 = (f32[76,8,128]{2,1,0:T(8,128)}, f32[76,8,128]{2,1,0:T(8,128)S(1)}, u32[]{:S(2)}, u32[]{:S(2)}) collective-permute-start(f32[76,8,128]{2,1,0:T(8,128)} %get-tuple-element.16), channel_id=1, source_target_pairs={{16,32},{32,16},{48,64},{64,48},{80,96},{96,80},{112,128},{128,112... | collective-permute-start | bytes 933896 | tf_op jit(solution)/shard_map/ppermute | solution.py:29
  17.7 10.2 %copy-start.8 = (f32[76,8,128]{2,1,0:T(8,128)}, f32[76,8,128]{2,1,0:T(8,128)S(1)}, u32[]{:S(2)}) copy-start(f32[76,8,128]{2,1,0:T(8,128)S(1)} %collective-permute-done.ra) | copy-start | bytes 933892
  27.9 0.7 copy-start.9
  30.9 22.2 %collective-permute-start.3 = (f32[192,8,128]{2,1,0:T(8,128)}, f32[192,8,128]{2,1,0:T(8,128)S(1)}, u32[]{:S(2)}, u32[]{:S(2)}) collective-permute-start(f32[192,8,128]{2,1,0:T(8,128)} %window_kernel.1.w), channel_id=1, source_target_pairs={{4,8},{8,4},{5,9},{9,5},{6,10},{10,6},{7,11},{11,7},{20,24},{24,20... | collective-permute-start | bytes 2359304 | tf_op jit(solution)/shard_map/ppermute | solution.py:29
  32.8 20.3 %collective-permute-start.2 = (f32[192,8,128]{2,1,0:T(8,128)}, f32[192,8,128]{2,1,0:T(8,128)S(1)}, u32[]{:S(2)}, u32[]{:S(2)}) collective-permute-start(f32[192,8,128]{2,1,0:T(8,128)} %window_kernel.1.w), channel_id=1, source_target_pairs={{0,4},{4,0},{8,12},{12,8},{1,5},{5,1},{9,13},{13,9},{2,6},{6,2},{1... | collective-permute-start | bytes 2359304 | tf_op jit(solution)/shard_map/ppermute | solution.py:30
  53.1 0.9 copy-start
  54.0 0.9 copy-start.1
  59.5 7.2 %collective-permute-start.4 = (f32[36,8,128]{2,1,0:T(8,128)}, f32[36,8,128]{2,1,0:T(8,128)S(1)}, u32[]{:S(2)}, u32[]{:S(2)}) collective-permute-start(f32[36,8,128]{2,1,0:T(8,128)} %get-tuple-element.17), channel_id=1, source_target_pairs={{0,1},{1,0},{2,3},{3,2},{4,5},{5,4},{6,7},{7,6},{8,9},{9,8},{10,11... | collective-permute-start | bytes 442376 | tf_op jit(solution)/shard_map/ppermute | solution.py:30
  62.6 7.2 %collective-permute-start.5 = (f32[36,8,128]{2,1,0:T(8,128)}, f32[36,8,128]{2,1,0:T(8,128)S(1)}, u32[]{:S(2)}, u32[]{:S(2)}) collective-permute-start(f32[36,8,128]{2,1,0:T(8,128)} %get-tuple-element.18), channel_id=1, source_target_pairs={{1,2},{2,1},{5,6},{6,5},{9,10},{10,9},{13,14},{14,13},{17,18},{18,... | collective-permute-start | bytes 442376 | tf_op jit(solution)/shard_map/ppermute | solution.py:29
  66.7 3.1 %copy-start.10 = (f32[36,8,128]{2,1,0:T(8,128)}, f32[36,8,128]{2,1,0:T(8,128)S(1)}, u32[]{:S(2)}) copy-start(f32[36,8,128]{2,1,0:T(8,128)S(1)} %collective-permute-done.4.za) | copy-start | bytes 442372
  69.8 0.7 copy-start.11
  81.8 21.8 %collective-permute-start.7 = (f32[81,8,128]{2,1,0:T(8,128)}, f32[81,8,128]{2,1,0:T(8,128)S(1)}, u32[]{:S(2)}, u32[]{:S(2)}) collective-permute-start(f32[81,8,128]{2,1,0:T(8,128)} %get-tuple-element.21), channel_id=1, source_target_pairs={{16,32},{32,16},{48,64},{64,48},{80,96},{96,80},{112,128},{128,112... | collective-permute-start | bytes 995336 | tf_op jit(solution)/shard_map/ppermute | solution.py:29
  95.9 16.8 %collective-permute-start.6 = (f32[81,8,128]{2,1,0:T(8,128)}, f32[81,8,128]{2,1,0:T(8,128)S(1)}, u32[]{:S(2)}, u32[]{:S(2)}) collective-permute-start(f32[81,8,128]{2,1,0:T(8,128)} %get-tuple-element.21), channel_id=1, source_target_pairs={{0,16},{16,0},{32,48},{48,32},{64,80},{80,64},{96,112},{112,96},{1... | collective-permute-start | bytes 995336 | tf_op jit(solution)/shard_map/ppermute | solution.py:30
  103.6 9.1 %copy-start.2 = (f32[81,8,128]{2,1,0:T(8,128)}, f32[81,8,128]{2,1,0:T(8,128)S(1)}, u32[]{:S(2)}) copy-start(f32[81,8,128]{2,1,0:T(8,128)S(1)} %collective-permute-done.7.rb) | copy-start | bytes 995332
  112.7 0.7 copy-start.5
  124.2 19.7 %collective-permute-start.9 = (f32[81,8,128]{2,1,0:T(8,128)}, f32[81,8,128]{2,1,0:T(8,128)S(1)}, u32[]{:S(2)}, u32[]{:S(2)}) collective-permute-start(f32[81,8,128]{2,1,0:T(8,128)} %get-tuple-element.24), channel_id=1, source_target_pairs={{16,32},{32,16},{48,64},{64,48},{80,96},{96,80},{112,128},{128,112... | collective-permute-start | bytes 995336 | tf_op jit(solution)/shard_map/ppermute | solution.py:29
  129.2 18.7 %collective-permute-start.8 = (f32[81,8,128]{2,1,0:T(8,128)}, f32[81,8,128]{2,1,0:T(8,128)S(1)}, u32[]{:S(2)}, u32[]{:S(2)}) collective-permute-start(f32[81,8,128]{2,1,0:T(8,128)} %get-tuple-element.24), channel_id=1, source_target_pairs={{0,16},{16,0},{32,48},{48,32},{64,80},{80,64},{96,112},{112,96},{1... | collective-permute-start | bytes 995336 | tf_op jit(solution)/shard_map/ppermute | solution.py:30
  143.9 4.0 %copy-start.3 = (f32[81,8,128]{2,1,0:T(8,128)}, f32[81,8,128]{2,1,0:T(8,128)S(1)}, u32[]{:S(2)}) copy-start(f32[81,8,128]{2,1,0:T(8,128)S(1)} %collective-permute-done.9.rb) | copy-start | bytes 995332
  147.9 0.7 copy-start.6
  159.5 16.2 %collective-permute-start.11 = (f32[81,8,128]{2,1,0:T(8,128)}, f32[81,8,128]{2,1,0:T(8,128)S(1)}, u32[]{:S(2)}, u32[]{:S(2)}) collective-permute-start(f32[81,8,128]{2,1,0:T(8,128)} %get-tuple-element.27), channel_id=1, source_target_pairs={{16,32},{32,16},{48,64},{64,48},{80,96},{96,80},{112,128},{128,112... | collective-permute-start | bytes 995336 | tf_op jit(solution)/shard_map/ppermute | solution.py:29
  164.5 12.4 %collective-permute-start.10 = (f32[81,8,128]{2,1,0:T(8,128)}, f32[81,8,128]{2,1,0:T(8,128)S(1)}, u32[]{:S(2)}, u32[]{:S(2)}) collective-permute-start(f32[81,8,128]{2,1,0:T(8,128)} %get-tuple-element.27), channel_id=1, source_target_pairs={{0,16},{16,0},{32,48},{48,32},{64,80},{80,64},{96,112},{112,96},{1... | collective-permute-start | bytes 995336 | tf_op jit(solution)/shard_map/ppermute | solution.py:30
  175.7 1.2 copy-start.4
  176.9 0.7 copy-start.7

commit v2 on v1

--- a/solution.py
+++ b/solution.py
@@ -15,6 +15,7 @@
 N = 192
 PA, PV, PS, PR, PL, NP1 = 0, 36, 45, 69, 72, 76
 NF = 81
+VMEM_LIMIT = 16 << 20
 
 
 def swaps(count, first):
@@ -143,83 +144,87 @@
     return pltpu.roll(x, 255, 1) - pltpu.roll(x, 1, 1)
 
 
-def one_step(st, kern):
-    def velocity(p, carry):
-        coef = st[CB + p - 1]
+def cut(f):
+    return f[8:16, 0:128]
+
+
+def one_step(coefs, stress_at, v_old, kern_old, v_new, kern, s_new=None):
+    for p in range(1, 9):
+        coef = coefs[CB + p - 1]
         for q in range(2):
-            base = p * 12 + q * 6
             for i in range(3):
                 x, y, z = PAIRS[i]
-                force = st[base + 12 + x] - st[base - 12 + x]
-                force = force + rows_diff(st[base + y]) + lanes_diff(st[base + z])
-                n = VB + (p - 1) * 6 + q * 3 + i
-                if q == 0:
-                    st[n] = st[n] - coef * force
-                else:
-                    st[n] = st[n] + coef * force
-        return carry
-
-    lax.fori_loop(1, 9, velocity, 0)
-
-    def stress(p, carry):
-        lam, mu = st[LB + p - 2], st[MB + p - 2]
+                force = stress_at(p + 1, q * 6 + x) - stress_at(p - 1, q * 6 + x)
+                force = force + rows_diff(stress_at(p, q * 6 + y))
+                force = force + lanes_diff(stress_at(p, q * 6 + z))
+                n = (p - 1) * 6 + q * 3 + i
+                v_new[n] = v_old(n) - coef * force if q == 0 else v_old(n) + coef * force
+    last = s_new is None
+    keep = cut if last else (lambda f: f)
+    own_cut = (lambda f: f) if last else cut
+    for p in range(2, 8):
+        if not last:
+            lam, mu = coefs[LB + p - 2], coefs[MB + p - 2]
         traces, diags, shears, vels = [], [], [], []
         for q in range(2):
-            v = VB + (p - 1) * 6 + q * 3
-            own = [st[v + i] for i in range(3)]
-            dx = [st[v + 6 + i] - st[v - 6 + i] for i in range(3)]
-            dy = [rows_diff(f) for f in own]
-            dz = [lanes_diff(f) for f in own]
+            v = (p - 1) * 6 + q * 3
+            own = [v_new[v + i] for i in range(3)]
+            dx = [keep(v_new[v + 6 + i]) - keep(v_new[v - 6 + i]) for i in range(3)]
+            dy = [keep(rows_diff(f)) for f in own]
+            dz = [keep(lanes_diff(f)) for f in own]
             diag = [dx[0], dy[1], dz[2]]
             shear = [dy[2] + dz[1], dx[2] + dz[0], dx[1] + dy[0]]
             trace = diag[0] + diag[1] + diag[2]
-            iso = lam * trace
-            s = p * 12 + q * 6
-            for c in range(3):
-                a = iso + (2.0 * mu) * diag[c]
-                b = mu * shear[c]
-                if q == 0:
-                    st[s + c] = st[s + c] - a
-                    st[s + 3 + c] = st[s + 3 + c] - b
-                else:
-                    st[s + c] = st[s + c] + a
-                    st[s + 3 + c] = st[s + 3 + c] + b
-            cut = lambda f: f[8:16, 0:128]
-            traces.append(cut(trace))
-            diags.append([cut(f) for f in diag])
-            shears.append([cut(f) for f in shear])
+            if not last:
+                iso = lam * trace
+                for c in range(3):
+                    a = iso + (2.0 * mu) * diag[c]
+                    b = mu * shear[c]
+                    e = q * 6 + c
+                    n = (p - 2) * 12 + e
+                    if q == 0:
+                        s_new[n] = stress_at(p, e) - a
+                        s_new[n + 3] = stress_at(p, e + 3) - b
+                    else:
+                        s_new[n] = stress_at(p, e) + a
+                        s_new[n + 3] = stress_at(p, e + 3) + b
+            traces.append(own_cut(trace))
+            diags.append([own_cut(f) for f in diag])
+            shears.append([own_cut(f) for f in shear])
             vels.append([cut(f) for f in own])
         dot = lambda pair: (
             pair[0][0] * pair[1][0] + pair[0][1] * pair[1][1] + pair[0][2] * pair[1][2]
         )
-        kern[p - 2] += H * dot(vels)
-        kern[6 + p - 2] += (0.25 * H) * (traces[0] * traces[1])
-        kern[12 + p - 2] += (0.5 * H) * dot(diags) + (0.25 * H) * dot(shears)
-        return carry
-
-    lax.fori_loop(2, 8, stress, 0)
-
-
-def write_faces(st, face):
+        new = (
+            H * dot(vels),
+            (0.25 * H) * (traces[0] * traces[1]),
+            (0.5 * H) * dot(diags) + (0.25 * H) * dot(shears),
+        )
+        for k in range(3):
+            n = 6 * k + p - 2
+            kern[n] = new[k] if kern_old is None else kern_old[n] + new[k]
+
+
+def write_faces(s_new, face):
     lane = lanes()
     for t in range(3):
         for g in range(3):
             acc = jnp.zeros((8, 128), jnp.float32)
             for k in range(8):
                 n = g * 8 + k
-                face[t * 24 + n] = st[48 + n, 8 * t : 8 * t + 8, 0:128]
-                x = st[48 + n, 8 * t : 8 * t + 8, 128:256]
+                face[t * 24 + n] = s_new[24 + n, 8 * t : 8 * t + 8, 0:128]
+                x = s_new[24 + n, 8 * t : 8 * t + 8, 128:256]
                 x = pltpu.roll(x, (8 + 16 * k) % 128, 1)
                 acc = jnp.where((lane >= 16 * k) & (lane < 16 * k + 16), x, acc)
             face[72 + t * 3 + g] = acc
 
 
-def read_faces(sc, ra, rb, st):
+def read_faces(sc, ra, rb, halo):
     lane = lanes()
-    halo = (lane < 8) | (lane >= 120)
+    edge = (lane < 8) | (lane >= 120)
     low_is_a = sc[0] == 1
     for low in (True, False):
-        first = 0 if low else 96
+        first = 0 if low else 24
         pick = low_is_a if low else jnp.logical_not(low_is_a)
         get = lambda n: jnp.where(pick, ra[n], rb[n])
         for t in range(3):
@@ -227,12 +232,12 @@
                 packed = get(72 + t * 3 + g)
                 for k in range(8):
                     n = g * 8 + k
-                    st[first + n, 8 * t : 8 * t + 8, 0:128] = get(t * 24 + n)
+                    halo[first + n, 8 * t : 8 * t + 8, 0:128] = get(t * 24 + n)
                     x = pltpu.roll(packed, (120 - 16 * k) % 128, 1)
-                    st[first + n, 8 * t : 8 * t + 8, 128:256] = jnp.where(halo, x, 0.0)
-
-
-def first_kernel(sc, w, ga, gb, za, zb, st, kern, face):
+                    halo[first + n, 8 * t : 8 * t + 8, 128:256] = jnp.where(edge, x, 0.0)
+
+
+def first_kernel(sc, w, ga, gb, za, zb, st, s_new, v_new, kern, face):
     gy_odd, gz_odd = sc[3], sc[4]
     lane = lanes()
 
@@ -256,34 +261,30 @@
         return carry
 
     lax.fori_loop(0, 12, group, 0)
-    for n in range(18):
-        kern[n] = jnp.zeros((8, 128), jnp.float32)
-    one_step(st, kern)
-    write_faces(st, face)
-
-
-def carry_over(st_in, kern_in, st, kern):
-    def move(n, carry):
-        st[n] = st_in[n]
-        return carry
-
-    lax.fori_loop(24, 96, move, 0, unroll=4)
-    lax.fori_loop(VB, 188, move, 0, unroll=4)
-    for n in range(18):
-        kern[n] = kern_in[n]
-
-
-def step_kernel(sc, st_in, kern_in, ra, rb, st, kern, face):
-    carry_over(st_in, kern_in, st, kern)
-    read_faces(sc, ra, rb, st)
-    one_step(st, kern)
-    write_faces(st, face)
-
-
-def last_kernel(sc, st_in, kern_in, ra, rb, dens, modu, st, kern):
-    carry_over(st_in, kern_in, st, kern)
-    read_faces(sc, ra, rb, st)
-    one_step(st, kern)
+    one_step(st, lambda p, e: st[p * 12 + e], lambda n: st[VB + n], None, v_new, kern, s_new)
+    write_faces(s_new, face)
+
+
+def with_halo(s_old, halo):
+    def stress_at(p, e):
+        if p < 2:
+            return halo[p * 12 + e]
+        if p > 7:
+            return halo[24 + (p - 8) * 12 + e]
+        return s_old[(p - 2) * 12 + e]
+
+    return stress_at
+
+
+def step_kernel(sc, st, s_old, v_old, kern_old, ra, rb, s_new, v_new, kern, face, halo):
+    read_faces(sc, ra, rb, halo)
+    one_step(st, with_halo(s_old, halo), lambda n: v_old[n], kern_old, v_new, kern, s_new)
+    write_faces(s_new, face)
+
+
+def last_kernel(sc, st, s_old, v_old, kern_old, ra, rb, dens, modu, halo, v_new, kern):
+    read_faces(sc, ra, rb, halo)
+    one_step(st, with_halo(s_old, halo), lambda n: v_old[n], kern_old, v_new, kern)
     off, noff = sc[1], sc[2]
     extent = 4 + noff - off
     for r in range(6):
@@ -302,6 +303,7 @@
         in_specs=[pl.BlockSpec(memory_space=pltpu.SMEM)] + [vmem] * (len(args) - 1),
         out_specs=[vmem] * len(outs),
         scratch_shapes=[pltpu.VMEM(s, jnp.float32) for s in scratch],
+        compiler_params=pltpu.CompilerParams(vmem_limit_bytes=VMEM_LIMIT),
         name=kernel.__name__,
     )(*args)
 
@@ -326,24 +328,21 @@
     ga, gb = both_swaps(win, win, "gy")
     edges = call(edge_kernel, [(36, 8, 128)] * 2, (sc, win, ga, gb))
     za, zb = both_swaps(*edges, "gz")
-    state, kern, face = call(
-        first_kernel,
-        [(N, 24, 256), (18, 8, 128), (NF, 8, 128)],
-        (sc, win, ga, gb, za, zb),
+    carried = [(72, 24, 256), (48, 24, 256), (18, 8, 128), (NF, 8, 128)]
+    state, *moving, face = call(
+        first_kernel, [(N, 24, 256)] + carried, (sc, win, ga, gb, za, zb)
     )
     for _ in range(STEPS - 2):
         recv = both_swaps(face, face, "grp")
-        state, kern, face = call(
-            step_kernel,
-            [(N, 24, 256), (18, 8, 128), (NF, 8, 128)],
-            (sc, state, kern, *recv),
+        *moving, face = call(
+            step_kernel, carried, (sc, state, *moving, *recv), [(48, 24, 256)]
         )
     recv = both_swaps(face, face, "grp")
     dens, modu = call(
         last_kernel,
         [(6, 8, 128), (2, 6, 8, 128)],
-        (sc, state, kern, *recv),
-        [(N, 24, 256), (18, 8, 128)],
+        (sc, state, *moving, *recv),
+        [(48, 24, 256), (48, 24, 256), (18, 8, 128)],
     )
     return dens, modu
 

time: 187 us -> 149 us (0.80)
  the two profiles are of different devices: /device:TPU:420 before, /device:TPU:29 now
where the time goes in v2:
time: 149 us; the launch traced here: 148 us
  starting transfers between devices  79.6 us (53%)
  waiting for transfers between devices  45.8 us (31%)
  Pallas kernels  14.1 us (9%)
  local copies, waits for them, and re-layouts  5.61 us (4%)
  other arithmetic  2.03 us (1%)
    ppermute x6, starting transfers between devices, both_swaps(): second = lax.ppermute(value_b, axis, swaps(count, 1))  52.6 us
    ppermute x6, waiting for transfers between devices, both_swaps(): second = lax.ppermute(value_b, axis, swaps(count, 1))  28.8 us
    ppermute x6, starting transfers between devices, both_swaps(): first = lax.ppermute(value_a, axis, swaps(count, 0))  27.1 us
    ppermute x6, waiting for transfers between devices, both_swaps(): first = lax.ppermute(value_a, axis, swaps(count, 0))  17 us
    pallas_call x7, Pallas kernels, call(): pl.pallas_call(kernel, out_shape=[jax.ShapeDtypeStruct(s, jnp.float32) fo...  14.1 us
    unnamed x12, local copies, waits for them, and re-layouts  4.95 us
  transfers between devices with their start and end apart: 12, of which 9 were waited for; matrix products, arithmetic and copies ran while one was open for 0% of the time, Pallas kernels for 0%

profile of v2, /device:TPU:29, one launch (start us, length us, event | category | flops | bytes accessed | tf_op | source)
XLA Modules:
  0.0 148.0 jit_solution(16446752789212045723)
XLA Ops:
  8.9 4.0 %collective-permute-start = (f32[76,8,128]{2,1,0:T(8,128)S(1)}, f32[76,8,128]{2,1,0:T(8,128)S(1)}, u32[]{:S(2)}, u32[]{:S(2)}) collective-permute-start(f32[76,8,128]{2,1,0:T(8,128)S(1)} %get-tuple-element.19), channel_id=1, source_target_pairs={{0,16},{16,0},{32,48},{48,32},{64,80},{80,64},{96,112},{112,96},{1... | collective-permute-start | bytes 933896 | tf_op jit(solution)/shard_map/ppermute | solution.py:31
  12.9 10.2 %collective-permute-start.1 = (f32[76,8,128]{2,1,0:T(8,128)S(1)}, f32[76,8,128]{2,1,0:T(8,128)S(1)}, u32[]{:S(2)}, u32[]{:S(2)}) collective-permute-start(f32[76,8,128]{2,1,0:T(8,128)S(1)} %get-tuple-element.20), channel_id=1, source_target_pairs={{16,32},{32,16},{48,64},{64,48},{80,96},{96,80},{112,128},{128,112... | collective-permute-start | bytes 933896 | tf_op jit(solution)/shard_map/ppermute | solution.py:30
  23.2 11.8 %collective-permute-done.1.rb = f32[76,8,128]{2,1,0:T(8,128)S(1)} collective-permute-done((f32[76,8,128]{2,1,0:T(8,128)S(1)}, f32[76,8,128]{2,1,0:T(8,128)S(1)}, u32[]{:S(2)}, u32[]{:S(2)}) %collective-permute-start.1) | collective-permute-done | bytes 311328 | tf_op jit(solution)/shard_map/ppermute | solution.py:30
  35.6 11.2 %collective-permute-start.3 = (f32[192,8,128]{2,1,0:T(8,128)S(1)}, f32[192,8,128]{2,1,0:T(8,128)S(1)}, u32[]{:S(2)}, u32[]{:S(2)}) collective-permute-start(f32[192,8,128]{2,1,0:T(8,128)S(1)} %window_kernel.1.w), channel_id=1, source_target_pairs={{4,8},{8,4},{5,9},{9,5},{6,10},{10,6},{7,11},{11,7},{20,24},{24,20... | collective-permute-start | bytes 2359304 | tf_op jit(solution)/shard_map/ppermute | solution.py:30
  46.8 1.9 %collective-permute-start.2 = (f32[192,8,128]{2,1,0:T(8,128)S(1)}, f32[192,8,128]{2,1,0:T(8,128)S(1)}, u32[]{:S(2)}, u32[]{:S(2)}) collective-permute-start(f32[192,8,128]{2,1,0:T(8,128)S(1)} %window_kernel.1.w), channel_id=1, source_target_pairs={{0,4},{4,0},{8,12},{12,8},{1,5},{5,1},{9,13},{13,9},{2,6},{6,2},{1... | collective-permute-start | bytes 2359304 | tf_op jit(solution)/shard_map/ppermute | solution.py:31
  48.8 9.9 %collective-permute-done.3.gb = f32[192,8,128]{2,1,0:T(8,128)S(1)} collective-permute-done((f32[192,8,128]{2,1,0:T(8,128)S(1)}, f32[192,8,128]{2,1,0:T(8,128)S(1)}, u32[]{:S(2)}, u32[]{:S(2)}) %collective-permute-start.3) | collective-permute-done | bytes 786464 | tf_op jit(solution)/shard_map/ppermute | solution.py:30
  58.7 2.8 %edge_kernel.1 = (f32[36,8,128]{2,1,0:T(8,128)S(1)}, f32[36,8,128]{2,1,0:T(8,128)S(1)}) custom-call(s32[8]{0:T(128)S(1)} %compare_select_fusion.3.sc, f32[192,8,128]{2,1,0:T(8,128)S(1)} %window_kernel.1.w, f32[192,8,128]{2,1,0:T(8,128)S(1)} %collective-permute-done.2.ga, f32[192,8,128]{2,1,0:T(8,128)S(1)} %collective-permute-done.3.gb), custom_call_target="tpu_custom_call" | custom-call | tf_op jit(solution)/shard_map/edge_kernel/pallas_call | solution.py:300
  61.6 2.8 %collective-permute-start.4 = (f32[36,8,128]{2,1,0:T(8,128)S(1)}, f32[36,8,128]{2,1,0:T(8,128)S(1)}, u32[]{:S(2)}, u32[]{:S(2)}) collective-permute-start(f32[36,8,128]{2,1,0:T(8,128)S(1)} %get-tuple-element.21), channel_id=1, source_target_pairs={{0,1},{1,0},{2,3},{3,2},{4,5},{5,4},{6,7},{7,6},{8,9},{9,8},{10,11... | collective-permute-start | bytes 442376 | tf_op jit(solution)/shard_map/ppermute | solution.py:31
  64.4 1.9 %collective-permute-start.5 = (f32[36,8,128]{2,1,0:T(8,128)S(1)}, f32[36,8,128]{2,1,0:T(8,128)S(1)}, u32[]{:S(2)}, u32[]{:S(2)}) collective-permute-start(f32[36,8,128]{2,1,0:T(8,128)S(1)} %get-tuple-element.22), channel_id=1, source_target_pairs={{1,2},{2,1},{5,6},{6,5},{9,10},{10,9},{13,14},{14,13},{17,18},{18,... | collective-permute-start | bytes 442376 | tf_op jit(solution)/shard_map/ppermute | solution.py:30
  67.5 2.8 %collective-permute-done.5.zb = f32[36,8,128]{2,1,0:T(8,128)S(1)} collective-permute-done((f32[36,8,128]{2,1,0:T(8,128)S(1)}, f32[36,8,128]{2,1,0:T(8,128)S(1)}, u32[]{:S(2)}, u32[]{:S(2)}) %collective-permute-start.5) | collective-permute-done | bytes 147488 | tf_op jit(solution)/shard_map/ppermute | solution.py:30
  70.3 3.9 %first_kernel.1 = (f32[192,24,256]{2,1,0:T(8,128)S(1)}, f32[72,24,256]{2,1,0:T(8,128)S(1)}, f32[48,24,256]{2,1,0:T(8,128)S(1)}, f32[18,8,128]{2,1,0:T(8,128)S(1)}, f32[81,8,128]{2,1,0:T(8,128)S(1)}) custom-call(s32[8]{0:T(128)S(1)} %compare_select_fusion.3.sc, f32[192,8,128]{2,1,0:T(8,128)S(1)} %window_kernel.1.w, ...), custom_call_target="tpu_custom_call" | custom-call | tf_op jit(solution)/shard_map/first_kernel/pallas_call | solution.py:300
  74.2 5.9 %collective-permute-start.7 = (f32[81,8,128]{2,1,0:T(8,128)S(1)}, f32[81,8,128]{2,1,0:T(8,128)S(1)}, u32[]{:S(2)}, u32[]{:S(2)}) collective-permute-start(f32[81,8,128]{2,1,0:T(8,128)S(1)} %get-tuple-element.27), channel_id=1, source_target_pairs={{16,32},{32,16},{48,64},{64,48},{80,96},{96,80},{112,128},{128,112... | collective-permute-start | bytes 995336 | tf_op jit(solution)/shard_map/ppermute | solution.py:30
  80.2 13.4 %collective-permute-start.6 = (f32[81,8,128]{2,1,0:T(8,128)S(1)}, f32[81,8,128]{2,1,0:T(8,128)S(1)}, u32[]{:S(2)}, u32[]{:S(2)}) collective-permute-start(f32[81,8,128]{2,1,0:T(8,128)S(1)} %get-tuple-element.27), channel_id=1, source_target_pairs={{0,16},{16,0},{32,48},{48,32},{64,80},{80,64},{96,112},{112,96},{1... | collective-permute-start | bytes 995336 | tf_op jit(solution)/shard_map/ppermute | solution.py:31
  93.6 4.9 %collective-permute-done.6.ra = f32[81,8,128]{2,1,0:T(8,128)S(1)} collective-permute-done((f32[81,8,128]{2,1,0:T(8,128)S(1)}, f32[81,8,128]{2,1,0:T(8,128)S(1)}, u32[]{:S(2)}, u32[]{:S(2)}) %collective-permute-start.6) | collective-permute-done | bytes 331808 | tf_op jit(solution)/shard_map/ppermute | solution.py:31
  98.5 2.0 %step_kernel.2 = (f32[72,24,256]{2,1,0:T(8,128)S(1)}, f32[48,24,256]{2,1,0:T(8,128)S(1)}, f32[18,8,128]{2,1,0:T(8,128)S(1)}, f32[81,8,128]{2,1,0:T(8,128)S(1)}) custom-call(s32[8]{0:T(128)S(1)} %compare_select_fusion.3.sc, f32[192,24,256]{2,1,0:T(8,128)S(1)} %get-tuple-element.23.st, f32[72,24,256]{2,1,0:T(8,128)S(1)} %get-tuple-element.24.s_old, ...), custom_call_target="tpu_custom_call" | custom-call | tf_op jit(solution)/shard_map/step_kernel/pallas_call | solution.py:300
  100.5 9.1 %collective-permute-start.9 = (f32[81,8,128]{2,1,0:T(8,128)S(1)}, f32[81,8,128]{2,1,0:T(8,128)S(1)}, u32[]{:S(2)}, u32[]{:S(2)}) collective-permute-start(f32[81,8,128]{2,1,0:T(8,128)S(1)} %get-tuple-element.31), channel_id=1, source_target_pairs={{16,32},{32,16},{48,64},{64,48},{80,96},{96,80},{112,128},{128,112... | collective-permute-start | bytes 995336 | tf_op jit(solution)/shard_map/ppermute | solution.py:30
  109.6 3.0 %collective-permute-start.8 = (f32[81,8,128]{2,1,0:T(8,128)S(1)}, f32[81,8,128]{2,1,0:T(8,128)S(1)}, u32[]{:S(2)}, u32[]{:S(2)}) collective-permute-start(f32[81,8,128]{2,1,0:T(8,128)S(1)} %get-tuple-element.31), channel_id=1, source_target_pairs={{0,16},{16,0},{32,48},{48,32},{64,80},{80,64},{96,112},{112,96},{1... | collective-permute-start | bytes 995336 | tf_op jit(solution)/shard_map/ppermute | solution.py:31
  114.2 5.0 %collective-permute-done.8.ra = f32[81,8,128]{2,1,0:T(8,128)S(1)} collective-permute-done((f32[81,8,128]{2,1,0:T(8,128)S(1)}, f32[81,8,128]{2,1,0:T(8,128)S(1)}, u32[]{:S(2)}, u32[]{:S(2)}) %collective-permute-start.8) | collective-permute-done | bytes 331808 | tf_op jit(solution)/shard_map/ppermute | solution.py:31
  119.3 2.0 %step_kernel.3 = (f32[72,24,256]{2,1,0:T(8,128)S(1)}, f32[48,24,256]{2,1,0:T(8,128)S(1)}, f32[18,8,128]{2,1,0:T(8,128)S(1)}, f32[81,8,128]{2,1,0:T(8,128)S(1)}) custom-call(s32[8]{0:T(128)S(1)} %compare_select_fusion.3.sc, f32[192,24,256]{2,1,0:T(8,128)S(1)} %get-tuple-element.23.st, f32[72,24,256]{2,1,0:T(8,128)S(1)} %get-tuple-element.28.s_old, ...), custom_call_target="tpu_custom_call" | custom-call | tf_op jit(solution)/shard_map/step_kernel/pallas_call | solution.py:300
  121.3 14.1 %collective-permute-start.11 = (f32[81,8,128]{2,1,0:T(8,128)S(1)}, f32[81,8,128]{2,1,0:T(8,128)S(1)}, u32[]{:S(2)}, u32[]{:S(2)}) collective-permute-start(f32[81,8,128]{2,1,0:T(8,128)S(1)} %get-tuple-element.35), channel_id=1, source_target_pairs={{16,32},{32,16},{48,64},{64,48},{80,96},{96,80},{112,128},{128,112... | collective-permute-start | bytes 995336 | tf_op jit(solution)/shard_map/ppermute | solution.py:30
  135.5 1.9 %collective-permute-start.10 = (f32[81,8,128]{2,1,0:T(8,128)S(1)}, f32[81,8,128]{2,1,0:T(8,128)S(1)}, u32[]{:S(2)}, u32[]{:S(2)}) collective-permute-start(f32[81,8,128]{2,1,0:T(8,128)S(1)} %get-tuple-element.35), channel_id=1, source_target_pairs={{0,16},{16,0},{32,48},{48,32},{64,80},{80,64},{96,112},{112,96},{1... | collective-permute-start | bytes 995336 | tf_op jit(solution)/shard_map/ppermute | solution.py:31
  137.4 2.7 %collective-permute-done.11.rb = f32[81,8,128]{2,1,0:T(8,128)S(1)} collective-permute-done((f32[81,8,128]{2,1,0:T(8,128)S(1)}, f32[81,8,128]{2,1,0:T(8,128)S(1)}, u32[]{:S(2)}, u32[]{:S(2)}) %collective-permute-start.11) | collective-permute-done | bytes 331808 | tf_op jit(solution)/shard_map/ppermute | solution.py:30
  140.1 5.9 %collective-permute-done.10.ra = f32[81,8,128]{2,1,0:T(8,128)S(1)} collective-permute-done((f32[81,8,128]{2,1,0:T(8,128)S(1)}, f32[81,8,128]{2,1,0:T(8,128)S(1)}, u32[]{:S(2)}, u32[]{:S(2)}) %collective-permute-start.10) | collective-permute-done | bytes 331808 | tf_op jit(solution)/shard_map/ppermute | solution.py:31
  146.0 2.0 %last_kernel.1 = (f32[6,8,128]{2,1,0:T(8,128)}, f32[2,6,8,128]{3,2,1,0:T(8,128)}) custom-call(s32[8]{0:T(128)S(1)} %compare_select_fusion.3.sc, f32[192,24,256]{2,1,0:T(8,128)S(1)} %get-tuple-element.23.st, f32[72,24,256]{2,1,0:T(8,128)S(1)} %get-tuple-element.32.s_old, f32[48,24,256]{2,1,0:T(8,128)S(1)} %get-tuple-element.33.v_old, ...), custom_call_target="tpu_custom_call" | custom-call | tf_op jit(solution)/shard_map/last_kernel/pallas_call | solution.py:300
  (23 shorter events, 11.5 us)
Async XLA Ops:
  3.3 0.9 copy-start
  4.3 0.9 copy-start.1
  5.2 0.9 copy-start.2
  6.0 0.8 copy-start.3
  6.8 0.8 copy-start.4
  7.6 0.7 copy-start.5
  8.9 14.3 %collective-permute-start = (f32[76,8,128]{2,1,0:T(8,128)S(1)}, f32[76,8,128]{2,1,0:T(8,128)S(1)}, u32[]{:S(2)}, u32[]{:S(2)}) collective-permute-start(f32[76,8,128]{2,1,0:T(8,128)S(1)} %get-tuple-element.19), channel_id=1, source_target_pairs={{0,16},{16,0},{32,48},{48,32},{64,80},{80,64},{96,112},{112,96},{1... | collective-permute-start | bytes 933896 | tf_op jit(solution)/shard_map/ppermute | solution.py:31
  12.9 22.1 %collective-permute-start.1 = (f32[76,8,128]{2,1,0:T(8,128)S(1)}, f32[76,8,128]{2,1,0:T(8,128)S(1)}, u32[]{:S(2)}, u32[]{:S(2)}) collective-permute-start(f32[76,8,128]{2,1,0:T(8,128)S(1)} %get-tuple-element.20), channel_id=1, source_target_pairs={{16,32},{32,16},{48,64},{64,48},{80,96},{96,80},{112,128},{128,112... | collective-permute-start | bytes 933896 | tf_op jit(solution)/shard_map/ppermute | solution.py:30
  35.6 23.1 %collective-permute-start.3 = (f32[192,8,128]{2,1,0:T(8,128)S(1)}, f32[192,8,128]{2,1,0:T(8,128)S(1)}, u32[]{:S(2)}, u32[]{:S(2)}) collective-permute-start(f32[192,8,128]{2,1,0:T(8,128)S(1)} %window_kernel.1.w), channel_id=1, source_target_pairs={{4,8},{8,4},{5,9},{9,5},{6,10},{10,6},{7,11},{11,7},{20,24},{24,20... | collective-permute-start | bytes 2359304 | tf_op jit(solution)/shard_map/ppermute | solution.py:30
  46.8 11.9 %collective-permute-start.2 = (f32[192,8,128]{2,1,0:T(8,128)S(1)}, f32[192,8,128]{2,1,0:T(8,128)S(1)}, u32[]{:S(2)}, u32[]{:S(2)}) collective-permute-start(f32[192,8,128]{2,1,0:T(8,128)S(1)} %window_kernel.1.w), channel_id=1, source_target_pairs={{0,4},{4,0},{8,12},{12,8},{1,5},{5,1},{9,13},{13,9},{2,6},{6,2},{1... | collective-permute-start | bytes 2359304 | tf_op jit(solution)/shard_map/ppermute | solution.py:31
  61.6 5.9 %collective-permute-start.4 = (f32[36,8,128]{2,1,0:T(8,128)S(1)}, f32[36,8,128]{2,1,0:T(8,128)S(1)}, u32[]{:S(2)}, u32[]{:S(2)}) collective-permute-start(f32[36,8,128]{2,1,0:T(8,128)S(1)} %get-tuple-element.21), channel_id=1, source_target_pairs={{0,1},{1,0},{2,3},{3,2},{4,5},{5,4},{6,7},{7,6},{8,9},{9,8},{10,11... | collective-permute-start | bytes 442376 | tf_op jit(solution)/shard_map/ppermute | solution.py:31
  64.4 5.9 %collective-permute-start.5 = (f32[36,8,128]{2,1,0:T(8,128)S(1)}, f32[36,8,128]{2,1,0:T(8,128)S(1)}, u32[]{:S(2)}, u32[]{:S(2)}) collective-permute-start(f32[36,8,128]{2,1,0:T(8,128)S(1)} %get-tuple-element.22), channel_id=1, source_target_pairs={{1,2},{2,1},{5,6},{6,5},{9,10},{10,9},{13,14},{14,13},{17,18},{18,... | collective-permute-start | bytes 442376 | tf_op jit(solution)/shard_map/ppermute | solution.py:30
  74.2 19.4 %collective-permute-start.7 = (f32[81,8,128]{2,1,0:T(8,128)S(1)}, f32[81,8,128]{2,1,0:T(8,128)S(1)}, u32[]{:S(2)}, u32[]{:S(2)}) collective-permute-start(f32[81,8,128]{2,1,0:T(8,128)S(1)} %get-tuple-element.27), channel_id=1, source_target_pairs={{16,32},{32,16},{48,64},{64,48},{80,96},{96,80},{112,128},{128,112... | collective-permute-start | bytes 995336 | tf_op jit(solution)/shard_map/ppermute | solution.py:30
  80.2 18.3 %collective-permute-start.6 = (f32[81,8,128]{2,1,0:T(8,128)S(1)}, f32[81,8,128]{2,1,0:T(8,128)S(1)}, u32[]{:S(2)}, u32[]{:S(2)}) collective-permute-start(f32[81,8,128]{2,1,0:T(8,128)S(1)} %get-tuple-element.27), channel_id=1, source_target_pairs={{0,16},{16,0},{32,48},{48,32},{64,80},{80,64},{96,112},{112,96},{1... | collective-permute-start | bytes 995336 | tf_op jit(solution)/shard_map/ppermute | solution.py:31
  100.5 13.7 %collective-permute-start.9 = (f32[81,8,128]{2,1,0:T(8,128)S(1)}, f32[81,8,128]{2,1,0:T(8,128)S(1)}, u32[]{:S(2)}, u32[]{:S(2)}) collective-permute-start(f32[81,8,128]{2,1,0:T(8,128)S(1)} %get-tuple-element.31), channel_id=1, source_target_pairs={{16,32},{32,16},{48,64},{64,48},{80,96},{96,80},{112,128},{128,112... | collective-permute-start | bytes 995336 | tf_op jit(solution)/shard_map/ppermute | solution.py:30
  109.6 9.6 %collective-permute-start.8 = (f32[81,8,128]{2,1,0:T(8,128)S(1)}, f32[81,8,128]{2,1,0:T(8,128)S(1)}, u32[]{:S(2)}, u32[]{:S(2)}) collective-permute-start(f32[81,8,128]{2,1,0:T(8,128)S(1)} %get-tuple-element.31), channel_id=1, source_target_pairs={{0,16},{16,0},{32,48},{48,32},{64,80},{80,64},{96,112},{112,96},{1... | collective-permute-start | bytes 995336 | tf_op jit(solution)/shard_map/ppermute | solution.py:31
  121.3 18.7 %collective-permute-start.11 = (f32[81,8,128]{2,1,0:T(8,128)S(1)}, f32[81,8,128]{2,1,0:T(8,128)S(1)}, u32[]{:S(2)}, u32[]{:S(2)}) collective-permute-start(f32[81,8,128]{2,1,0:T(8,128)S(1)} %get-tuple-element.35), channel_id=1, source_target_pairs={{16,32},{32,16},{48,64},{64,48},{80,96},{96,80},{112,128},{128,112... | collective-permute-start | bytes 995336 | tf_op jit(solution)/shard_map/ppermute | solution.py:30
  135.5 10.5 %collective-permute-start.10 = (f32[81,8,128]{2,1,0:T(8,128)S(1)}, f32[81,8,128]{2,1,0:T(8,128)S(1)}, u32[]{:S(2)}, u32[]{:S(2)}) collective-permute-start(f32[81,8,128]{2,1,0:T(8,128)S(1)} %get-tuple-element.35), channel_id=1, source_target_pairs={{0,16},{16,0},{32,48},{48,32},{64,80},{80,64},{96,112},{112,96},{1... | collective-permute-start | bytes 995336 | tf_op jit(solution)/shard_map/ppermute | solution.py:31

commit v3 on v2

--- a/solution.py
+++ b/solution.py
@@ -14,7 +14,9 @@
 VB, CB, LB, MB = 120, 168, 176, 182
 N = 192
 PA, PV, PS, PR, PL, NP1 = 0, 36, 45, 69, 72, 76
-NF = 81
+ALL12 = list(range(12))
+X6 = [0, 5, 4, 6, 11, 10]
+DEPTHS = ((8, 4), (4, 2), (1, 0))
 VMEM_LIMIT = 16 << 20
 
 
@@ -32,8 +34,29 @@
     return first, second
 
 
-def pack_kernel(sc, fv, fs, rho, lam, av, as_, out_a, out_b):
-    odd, off = sc[0], sc[1]
+def where_am_i(offsets):
+    place = lax.axis_index("grp")
+    last = lax.axis_size("grp") - 1
+    off = offsets[place]
+    noff = jnp.where(place < last, offsets[jnp.minimum(place + 1, last)], 0)
+    return (
+        lax.rem(place, 2),
+        off,
+        noff,
+        lax.rem(lax.axis_index("gy"), 2),
+        lax.rem(lax.axis_index("gz"), 2),
+    )
+
+
+def pack_kernel(offsets, *refs):
+    raw, (out_a, out_b), held, sems = refs[:6], refs[6:8], refs[8:14], refs[14]
+    copies = [pltpu.make_async_copy(raw[k], held[k], sems.at[k]) for k in range(6)]
+    for copy in copies:
+        copy.start()
+    for copy in copies:
+        copy.wait()
+    fv, fs, rho, lam, av, as_ = held
+    odd, off, _, _, _ = where_am_i(offsets)
     for out, up in ((out_a, 1 - odd), (out_b, odd)):
         for i in range(4):
             row = jnp.maximum(2 * up + i - off, 0)
@@ -51,8 +74,8 @@
                 out[PL + i * 2 + c] = lam[c, i]
 
 
-def window_kernel(sc, fv, fs, rho, lam, av, as_, ra, rb, w):
-    odd, off, noff = sc[0], sc[1], sc[2]
+def window_kernel(offsets, fv, fs, rho, lam, av, as_, ra, rb, w):
+    odd, off, noff, _, _ = where_am_i(offsets)
     low_is_a = odd == 1
 
     def low(n):
@@ -114,8 +137,8 @@
     return lax.broadcasted_iota(jnp.int32, (8, 128), 1)
 
 
-def edge_kernel(sc, w, ga, gb, out_a, out_b):
-    gy_odd, gz_odd = sc[3], sc[4]
+def edge_kernel(offsets, w, ga, gb, out_a, out_b):
+    _, _, _, gy_odd, gz_odd = where_am_i(offsets)
     lane = lanes()
 
     def group(g, carry):
@@ -205,40 +228,91 @@
             kern[n] = new[k] if kern_old is None else kern_old[n] + new[k]
 
 
-def write_faces(s_new, face):
+def row_groups(entries, m):
+    size = 4 // m
+    return [entries[k : k + size] for k in range(0, len(entries), size)]
+
+
+def face_blocks(depths):
+    blocks = [(1, "own", [e]) for e in ALL12] + [(2, "own", [e]) for e in X6]
+    for dx, entries, m in ((1, ALL12, depths[0]), (2, X6, depths[1])):
+        if m == 8:
+            blocks += [(dx, side, [e]) for e in entries for side in ("low", "high")]
+        elif m:
+            blocks += [(dx, m, group) for group in row_groups(entries, m)]
+    return blocks
+
+
+def face_tiles(depths):
+    count = len(face_blocks(depths))
+    return count + -(-count // 8)
+
+
+def write_faces(odd, depths, s_new, face_a, face_b):
     lane = lanes()
-    for t in range(3):
-        for g in range(3):
-            acc = jnp.zeros((8, 128), jnp.float32)
-            for k in range(8):
-                n = g * 8 + k
-                face[t * 24 + n] = s_new[24 + n, 8 * t : 8 * t + 8, 0:128]
-                x = s_new[24 + n, 8 * t : 8 * t + 8, 128:256]
-                x = pltpu.roll(x, (8 + 16 * k) % 128, 1)
-                acc = jnp.where((lane >= 16 * k) & (lane < 16 * k + 16), x, acc)
-            face[72 + t * 3 + g] = acc
-
-
-def read_faces(sc, ra, rb, halo):
+    row = lax.broadcasted_iota(jnp.int32, (8, 256), 0)
+    blocks = face_blocks(depths)
+    count = len(blocks)
+    for face, up in ((face_a, 1 - odd), (face_b, odd)):
+        first = {1: (2 + up) * 12, 2: (3 - up) * 12}
+        acc = None
+        for j, (dx, halo, entries) in enumerate(blocks):
+            at = lambda e: first[dx] + e
+            if halo == "own":
+                x = s_new[at(entries[0]), 8:16, :]
+            elif halo == "low":
+                x = s_new[at(entries[0]), 0:8, :]
+            elif halo == "high":
+                x = s_new[at(entries[0]), 16:24, :]
+            else:
+                m, x = halo, None
+                for k, e in enumerate(entries):
+                    c = jnp.where(row < 4, s_new[at(e), 16:24, :], s_new[at(e), 0:8, :])
+                    if m < 4:
+                        c = pltpu.roll(c, (m + 2 * m * k) % 8, 0)
+                    x = c if x is None else jnp.where(row < 2 * m * k, x, c)
+            face[j] = x[:, 0:128]
+            k = j % 8
+            h = pltpu.roll(x[:, 128:256], (8 + 16 * k) % 128, 1)
+            acc = h if k == 0 else jnp.where(lane < 16 * k, acc, h)
+            if k == 7 or j == count - 1:
+                face[count + j // 8] = acc
+
+
+def read_faces(odd, depths, ra, rb, halo):
     lane = lanes()
     edge = (lane < 8) | (lane >= 120)
-    low_is_a = sc[0] == 1
+    low_is_a = odd == 1
+    blocks = face_blocks(depths)
+    count = len(blocks)
     for low in (True, False):
-        first = 0 if low else 24
+        first = {1: 12 if low else 24, 2: 0 if low else 36}
         pick = low_is_a if low else jnp.logical_not(low_is_a)
         get = lambda n: jnp.where(pick, ra[n], rb[n])
-        for t in range(3):
-            for g in range(3):
-                packed = get(72 + t * 3 + g)
-                for k in range(8):
-                    n = g * 8 + k
-                    halo[first + n, 8 * t : 8 * t + 8, 0:128] = get(t * 24 + n)
-                    x = pltpu.roll(packed, (120 - 16 * k) % 128, 1)
-                    halo[first + n, 8 * t : 8 * t + 8, 128:256] = jnp.where(edge, x, 0.0)
-
-
-def first_kernel(sc, w, ga, gb, za, zb, st, s_new, v_new, kern, face):
-    gy_odd, gz_odd = sc[3], sc[4]
+        packed = None
+        for j, (dx, kind, entries) in enumerate(blocks):
+            k = j % 8
+            if k == 0:
+                packed = get(count + j // 8)
+            h = pltpu.roll(packed, (120 - 16 * k) % 128, 1)
+            x = jnp.concatenate([get(j), jnp.where(edge, h, 0.0)], axis=1)
+            if kind in ("own", "low", "high"):
+                r = {"low": 0, "own": 8, "high": 16}[kind]
+                halo[first[dx] + entries[0], r : r + 8, :] = x
+            else:
+                m = kind
+                for i, e in enumerate(entries):
+                    c = x if m == 4 else pltpu.roll(x, (16 - m - 2 * m * i) % 8, 0)
+                    halo[first[dx] + e, 0:8, :] = c
+                    halo[first[dx] + e, 16:24, :] = c
+        if depths[1] == 0:
+            for e in X6:
+                halo[first[2] + e, 0:8, :] = jnp.zeros((8, 256), jnp.float32)
+                halo[first[2] + e, 16:24, :] = jnp.zeros((8, 256), jnp.float32)
+
+
+def first_kernel(depths, offsets, w, ga, gb, za, zb, st, s_new, v_new, kern, face_a, face_b):
+    odd, _, _, gy_odd, gz_odd = where_am_i(offsets)
     lane = lanes()
 
     def group(g, carry):
@@ -262,7 +336,7 @@
 
     lax.fori_loop(0, 12, group, 0)
     one_step(st, lambda p, e: st[p * 12 + e], lambda n: st[VB + n], None, v_new, kern, s_new)
-    write_faces(s_new, face)
+    write_faces(odd, depths, s_new, face_a, face_b)
 
 
 def with_halo(s_old, halo):
@@ -276,16 +350,21 @@
     return stress_at
 
 
-def step_kernel(sc, st, s_old, v_old, kern_old, ra, rb, s_new, v_new, kern, face, halo):
-    read_faces(sc, ra, rb, halo)
+def step_kernel(
+    before, after, offsets, st, s_old, v_old, kern_old, ra, rb, s_new, v_new, kern, face_a, face_b, halo
+):
+    odd = where_am_i(offsets)[0]
+    read_faces(odd, before, ra, rb, halo)
     one_step(st, with_halo(s_old, halo), lambda n: v_old[n], kern_old, v_new, kern, s_new)
-    write_faces(s_new, face)
-
-
-def last_kernel(sc, st, s_old, v_old, kern_old, ra, rb, dens, modu, halo, v_new, kern):
-    read_faces(sc, ra, rb, halo)
+    write_faces(odd, after, s_new, face_a, face_b)
+
+
+def last_kernel(
+    before, offsets, st, s_old, v_old, kern_old, ra, rb, dens, modu, halo, v_new, kern
+):
+    odd, off, noff, _, _ = where_am_i(offsets)
+    read_faces(odd, before, ra, rb, halo)
     one_step(st, with_halo(s_old, halo), lambda n: v_old[n], kern_old, v_new, kern)
-    off, noff = sc[1], sc[2]
     extent = 4 + noff - off
     for r in range(6):
         row = jnp.minimum(off + r, 5)
@@ -295,53 +374,59 @@
         modu[1, r] = jnp.where(live, kern[12 + row], 0.0)
 
 
-def call(kernel, outs, args, scratch=()):
+def call(kernel, name, outs, args, scratch=(), space=pltpu.VMEM):
     vmem = pl.BlockSpec(memory_space=pltpu.VMEM)
     return pl.pallas_call(
         kernel,
         out_shape=[jax.ShapeDtypeStruct(s, jnp.float32) for s in outs],
-        in_specs=[pl.BlockSpec(memory_space=pltpu.SMEM)] + [vmem] * (len(args) - 1),
+        in_specs=[pl.BlockSpec(memory_space=pltpu.SMEM)]
+        + [pl.BlockSpec(memory_space=space)] * (len(args) - 1),
         out_specs=[vmem] * len(outs),
-        scratch_shapes=[pltpu.VMEM(s, jnp.float32) for s in scratch],
+        scratch_shapes=[pltpu.VMEM(s, jnp.float32) if isinstance(s, tuple) else s for s in scratch],
         compiler_params=pltpu.CompilerParams(vmem_limit_bytes=VMEM_LIMIT),
-        name=kernel.__name__,
+        name=name,
     )(*args)
 
 
 def shards(fwd_velocity, fwd_stress, density, lame, adj_velocity, adj_stress, offsets):
-    blocks = lax.axis_size("grp")
-    place = lax.axis_index("grp")
-    padded = jnp.concatenate([offsets.astype(jnp.int32), jnp.zeros((1,), jnp.int32)])
-    pair = lax.dynamic_slice_in_dim(padded, place, 2, 0)
-    spot = jnp.arange(8, dtype=jnp.int32)
-    sc = jnp.where(
-        spot == 0,
-        place % 2,
-        jnp.where(spot == 3, lax.axis_index("gy") % 2, lax.axis_index("gz") % 2),
-    ).astype(jnp.int32)
-    sc = jnp.where(spot == 1, pair[0], jnp.where(spot == 2, pair[1], sc))
-
     raw = (fwd_velocity, fwd_stress, density, lame, adj_velocity, adj_stress)
-    send_a, send_b = call(pack_kernel, [(NP1, 8, 128)] * 2, (sc, *raw))
+    raw = [pltpu.with_memory_space_constraint(a, pltpu.HBM) for a in raw]
+    send_a, send_b, *held = call(
+        pack_kernel,
+        "pack",
+        [(NP1, 8, 128)] * 2 + [a.shape for a in raw],
+        (offsets, *raw),
+        [pltpu.SemaphoreType.DMA((6,))],
+        pltpu.HBM,
+    )
     recv = both_swaps(send_a, send_b, "grp")
-    (win,) = call(window_kernel, [(N, 8, 128)], (sc, *raw, *recv))
+    (win,) = call(window_kernel, "window", [(N, 8, 128)], (offsets, *held, *recv))
     ga, gb = both_swaps(win, win, "gy")
-    edges = call(edge_kernel, [(36, 8, 128)] * 2, (sc, win, ga, gb))
+    edges = call(edge_kernel, "edge", [(36, 8, 128)] * 2, (offsets, win, ga, gb))
     za, zb = both_swaps(*edges, "gz")
-    carried = [(72, 24, 256), (48, 24, 256), (18, 8, 128), (NF, 8, 128)]
-    state, *moving, face = call(
-        first_kernel, [(N, 24, 256)] + carried, (sc, win, ga, gb, za, zb)
+    carried = [(72, 24, 256), (48, 24, 256), (18, 8, 128)]
+    faces = lambda k: [(face_tiles(DEPTHS[k]), 8, 128)] * 2
+    state, *moving, face_a, face_b = call(
+        functools.partial(first_kernel, DEPTHS[0]),
+        "first",
+        [(N, 24, 256)] + carried + faces(0),
+        (offsets, win, ga, gb, za, zb),
     )
-    for _ in range(STEPS - 2):
-        recv = both_swaps(face, face, "grp")
-        *moving, face = call(
-            step_kernel, carried, (sc, state, *moving, *recv), [(48, 24, 256)]
+    for k in range(STEPS - 2):
+        recv = both_swaps(face_a, face_b, "grp")
+        *moving, face_a, face_b = call(
+            functools.partial(step_kernel, DEPTHS[k], DEPTHS[k + 1]),
+            "step",
+            carried + faces(k + 1),
+            (offsets, state, *moving, *recv),
+            [(48, 24, 256)],
         )
-    recv = both_swaps(face, face, "grp")
+    recv = both_swaps(face_a, face_b, "grp")
     dens, modu = call(
-        last_kernel,
+        functools.partial(last_kernel, DEPTHS[STEPS - 2]),
+        "last",
         [(6, 8, 128), (2, 6, 8, 128)],
-        (sc, state, *moving, *recv),
+        (offsets, state, *moving, *recv),
         [(48, 24, 256), (48, 24, 256), (18, 8, 128)],
     )
     return dens, modu

time: 149 us -> 138 us (0.926)
  the two profiles are of different devices: /device:TPU:29 before, /device:TPU:420 now
where the time goes in v3:
time: 138 us
  waiting for transfers between devices  62.8 us (46%)
  starting transfers between devices  58.1 us (42%)
  Pallas kernels  15.2 us (11%)
    ppermute x6, waiting for transfers between devices, both_swaps(): second = lax.ppermute(value_b, axis, swaps(count, 1))  58.9 us
    ppermute x6, starting transfers between devices, both_swaps(): first = lax.ppermute(value_a, axis, swaps(count, 0))  32.6 us
    ppermute x6, starting transfers between devices, both_swaps(): second = lax.ppermute(value_b, axis, swaps(count, 1))  25.5 us
    pallas_call x7, Pallas kernels, call(): pl.pallas_call(kernel, out_shape=[jax.ShapeDtypeStruct(s, jnp.float32) fo...  15.2 us
    ppermute x6, waiting for transfers between devices, both_swaps(): first = lax.ppermute(value_a, axis, swaps(count, 0))  3.92 us
  transfers between devices with their start and end apart: 12, of which 9 were waited for; matrix products, arithmetic and copies ran while one was open for 0% of the time, Pallas kernels for 0%

profile of v3, /device:TPU:420, one launch (start us, length us, event | category | flops | bytes accessed | tf_op | source)
XLA Modules:
  0.0 137.6 jit_solution(3228502003485640370)
XLA Ops:
  3.0 4.0 %collective-permute-start = (f32[76,8,128]{2,1,0:T(8,128)S(1)}, f32[76,8,128]{2,1,0:T(8,128)S(1)}, u32[]{:S(2)}, u32[]{:S(2)}) collective-permute-start(f32[76,8,128]{2,1,0:T(8,128)S(1)} %get-tuple-element.34), channel_id=1, source_target_pairs={{0,16},{16,0},{32,48},{48,32},{64,80},{80,64},{96,112},{112,96},{1... | collective-permute-start | bytes 933896 | tf_op jit(solution)/shard_map/ppermute | solution.py:33
  7.0 6.0 %collective-permute-start.1 = (f32[76,8,128]{2,1,0:T(8,128)S(1)}, f32[76,8,128]{2,1,0:T(8,128)S(1)}, u32[]{:S(2)}, u32[]{:S(2)}) collective-permute-start(f32[76,8,128]{2,1,0:T(8,128)S(1)} %get-tuple-element.35), channel_id=1, source_target_pairs={{16,32},{32,16},{48,64},{64,48},{80,96},{96,80},{112,128},{128,112... | collective-permute-start | bytes 933896 | tf_op jit(solution)/shard_map/ppermute | solution.py:32
  14.5 10.4 %collective-permute-done.1.rb = f32[76,8,128]{2,1,0:T(8,128)S(1)} collective-permute-done((f32[76,8,128]{2,1,0:T(8,128)S(1)}, f32[76,8,128]{2,1,0:T(8,128)S(1)}, u32[]{:S(2)}, u32[]{:S(2)}) %collective-permute-start.1) | collective-permute-done | bytes 311328 | tf_op jit(solution)/shard_map/ppermute | solution.py:32
  25.5 1.9 %collective-permute-start.3 = (f32[192,8,128]{2,1,0:T(8,128)S(1)}, f32[192,8,128]{2,1,0:T(8,128)S(1)}, u32[]{:S(2)}, u32[]{:S(2)}) collective-permute-start(f32[192,8,128]{2,1,0:T(8,128)S(1)} %window.1.w), channel_id=1, source_target_pairs={{4,8},{8,4},{5,9},{9,5},{6,10},{10,6},{7,11},{11,7},{20,24},{24,20... | collective-permute-start | bytes 2359304 | tf_op jit(solution)/shard_map/ppermute | solution.py:32
  27.5 1.9 %collective-permute-start.2 = (f32[192,8,128]{2,1,0:T(8,128)S(1)}, f32[192,8,128]{2,1,0:T(8,128)S(1)}, u32[]{:S(2)}, u32[]{:S(2)}) collective-permute-start(f32[192,8,128]{2,1,0:T(8,128)S(1)} %window.1.w), channel_id=1, source_target_pairs={{0,4},{4,0},{8,12},{12,8},{1,5},{5,1},{9,13},{13,9},{2,6},{6,2},{1... | collective-permute-start | bytes 2359304 | tf_op jit(solution)/shard_map/ppermute | solution.py:33
  29.4 18.1 %collective-permute-done.3.gb = f32[192,8,128]{2,1,0:T(8,128)S(1)} collective-permute-done((f32[192,8,128]{2,1,0:T(8,128)S(1)}, f32[192,8,128]{2,1,0:T(8,128)S(1)}, u32[]{:S(2)}, u32[]{:S(2)}) %collective-permute-start.3) | collective-permute-done | bytes 786464 | tf_op jit(solution)/shard_map/ppermute | solution.py:32
  47.5 2.6 %edge.1 = (f32[36,8,128]{2,1,0:T(8,128)S(1)}, f32[36,8,128]{2,1,0:T(8,128)S(1)}) custom-call(s32[48]{0:T(128)S(1)} %copy-done, f32[192,8,128]{2,1,0:T(8,128)S(1)} %window.1.w, f32[192,8,128]{2,1,0:T(8,128)S(1)} %collective-permute-done.2.ga, f32[192,8,128]{2,1,0:T(8,128)S(1)} %collective-permute-done.3.gb), custom_call_target="tpu_custom_call" | custom-call | tf_op jit(solution)/shard_map/edge/pallas_call | solution.py:379
  50.2 3.1 %collective-permute-start.4 = (f32[36,8,128]{2,1,0:T(8,128)S(1)}, f32[36,8,128]{2,1,0:T(8,128)S(1)}, u32[]{:S(2)}, u32[]{:S(2)}) collective-permute-start(f32[36,8,128]{2,1,0:T(8,128)S(1)} %get-tuple-element.36), channel_id=1, source_target_pairs={{0,1},{1,0},{2,3},{3,2},{4,5},{5,4},{6,7},{7,6},{8,9},{9,8},{10,11... | collective-permute-start | bytes 442376 | tf_op jit(solution)/shard_map/ppermute | solution.py:33
  53.3 1.9 %collective-permute-start.5 = (f32[36,8,128]{2,1,0:T(8,128)S(1)}, f32[36,8,128]{2,1,0:T(8,128)S(1)}, u32[]{:S(2)}, u32[]{:S(2)}) collective-permute-start(f32[36,8,128]{2,1,0:T(8,128)S(1)} %get-tuple-element.37), channel_id=1, source_target_pairs={{1,2},{2,1},{5,6},{6,5},{9,10},{10,9},{13,14},{14,13},{17,18},{18,... | collective-permute-start | bytes 442376 | tf_op jit(solution)/shard_map/ppermute | solution.py:32
  55.2 2.0 %collective-permute-done.4.za = f32[36,8,128]{2,1,0:T(8,128)S(1)} collective-permute-done((f32[36,8,128]{2,1,0:T(8,128)S(1)}, f32[36,8,128]{2,1,0:T(8,128)S(1)}, u32[]{:S(2)}, u32[]{:S(2)}) %collective-permute-start.4) | collective-permute-done | bytes 147488 | tf_op jit(solution)/shard_map/ppermute | solution.py:33
  57.2 3.1 %collective-permute-done.5.zb = f32[36,8,128]{2,1,0:T(8,128)S(1)} collective-permute-done((f32[36,8,128]{2,1,0:T(8,128)S(1)}, f32[36,8,128]{2,1,0:T(8,128)S(1)}, u32[]{:S(2)}, u32[]{:S(2)}) %collective-permute-start.5) | collective-permute-done | bytes 147488 | tf_op jit(solution)/shard_map/ppermute | solution.py:32
  60.3 4.1 %first.1 = (f32[192,24,256]{2,1,0:T(8,128)S(1)}, f32[72,24,256]{2,1,0:T(8,128)S(1)}, f32[48,24,256]{2,1,0:T(8,128)S(1)}, f32[18,8,128]{2,1,0:T(8,128)S(1)}, f32[...) custom-call(s32[48]{0:T(128)S(1)} %copy-done, f32[192,8,128]{2,1,0:T(8,128)S(1)} %window.1.w, ...), custom_call_target="tpu_custom_call" | custom-call | tf_op jit(solution)/shard_map/first/pallas_call | solution.py:379
  64.4 19.7 %collective-permute-start.6 = (f32[54,8,128]{2,1,0:T(8,128)S(1)}, f32[54,8,128]{2,1,0:T(8,128)S(1)}, u32[]{:S(2)}, u32[]{:S(2)}) collective-permute-start(f32[54,8,128]{2,1,0:T(8,128)S(1)} %get-tuple-element.42), channel_id=1, source_target_pairs={{0,16},{16,0},{32,48},{48,32},{64,80},{80,64},{96,112},{112,96},{1... | collective-permute-start | bytes 663560 | tf_op jit(solution)/shard_map/ppermute | solution.py:33
  84.2 6.0 %collective-permute-start.7 = (f32[54,8,128]{2,1,0:T(8,128)S(1)}, f32[54,8,128]{2,1,0:T(8,128)S(1)}, u32[]{:S(2)}, u32[]{:S(2)}) collective-permute-start(f32[54,8,128]{2,1,0:T(8,128)S(1)} %get-tuple-element.43), channel_id=1, source_target_pairs={{16,32},{32,16},{48,64},{64,48},{80,96},{96,80},{112,128},{128,112... | collective-permute-start | bytes 663560 | tf_op jit(solution)/shard_map/ppermute | solution.py:32
  90.2 9.9 %collective-permute-done.7.rb = f32[54,8,128]{2,1,0:T(8,128)S(1)} collective-permute-done((f32[54,8,128]{2,1,0:T(8,128)S(1)}, f32[54,8,128]{2,1,0:T(8,128)S(1)}, u32[]{:S(2)}, u32[]{:S(2)}) %collective-permute-start.7) | collective-permute-done | bytes 221216 | tf_op jit(solution)/shard_map/ppermute | solution.py:32
  100.1 2.1 %step.2 = (f32[72,24,256]{2,1,0:T(8,128)S(1)}, f32[48,24,256]{2,1,0:T(8,128)S(1)}, f32[18,8,128]{2,1,0:T(8,128)S(1)}, f32[38,8,128]{2,1,0:T(8,128)S(1)}, f32[38,8,128]{2,1,0:T(8,128)S(1)}) custom-call(s32[48]{0:T(128)S(1)} %copy-done, f32[192,24,256]{2,1,0:T(8,128)S(1)} %get-tuple-element.38.st, f32[72,24,256]{2,1,0:T(8,128)S(1)} %get-tuple-element.39.s_old, ...), custom_call_target="tpu_custom_call" | custom-call | tf_op jit(solution)/shard_map/step/pallas_call | solution.py:379
  102.2 1.9 %collective-permute-start.8 = (f32[38,8,128]{2,1,0:T(8,128)S(1)}, f32[38,8,128]{2,1,0:T(8,128)S(1)}, u32[]{:S(2)}, u32[]{:S(2)}) collective-permute-start(f32[38,8,128]{2,1,0:T(8,128)S(1)} %get-tuple-element.47), channel_id=1, source_target_pairs={{0,16},{16,0},{32,48},{48,32},{64,80},{80,64},{96,112},{112,96},{1... | collective-permute-start | bytes 466952 | tf_op jit(solution)/shard_map/ppermute | solution.py:33
  104.1 4.8 %collective-permute-start.9 = (f32[38,8,128]{2,1,0:T(8,128)S(1)}, f32[38,8,128]{2,1,0:T(8,128)S(1)}, u32[]{:S(2)}, u32[]{:S(2)}) collective-permute-start(f32[38,8,128]{2,1,0:T(8,128)S(1)} %get-tuple-element.48), channel_id=1, source_target_pairs={{16,32},{32,16},{48,64},{64,48},{80,96},{96,80},{112,128},{128,112... | collective-permute-start | bytes 466952 | tf_op jit(solution)/shard_map/ppermute | solution.py:32
  109.3 8.8 %collective-permute-done.9.rb = f32[38,8,128]{2,1,0:T(8,128)S(1)} collective-permute-done((f32[38,8,128]{2,1,0:T(8,128)S(1)}, f32[38,8,128]{2,1,0:T(8,128)S(1)}, u32[]{:S(2)}, u32[]{:S(2)}) %collective-permute-start.9) | collective-permute-done | bytes 155680 | tf_op jit(solution)/shard_map/ppermute | solution.py:32
  118.1 2.1 %step.3 = (f32[72,24,256]{2,1,0:T(8,128)S(1)}, f32[48,24,256]{2,1,0:T(8,128)S(1)}, f32[18,8,128]{2,1,0:T(8,128)S(1)}, f32[24,8,128]{2,1,0:T(8,128)S(1)}, f32[24,8,128]{2,1,0:T(8,128)S(1)}) custom-call(s32[48]{0:T(128)S(1)} %copy-done, f32[192,24,256]{2,1,0:T(8,128)S(1)} %get-tuple-element.38.st, f32[72,24,256]{2,1,0:T(8,128)S(1)} %get-tuple-element.44.s_old, ...), custom_call_target="tpu_custom_call" | custom-call | tf_op jit(solution)/shard_map/step/pallas_call | solution.py:379
  120.2 1.9 %collective-permute-start.10 = (f32[24,8,128]{2,1,0:T(8,128)S(1)}, f32[24,8,128]{2,1,0:T(8,128)S(1)}, u32[]{:S(2)}, u32[]{:S(2)}) collective-permute-start(f32[24,8,128]{2,1,0:T(8,128)S(1)} %get-tuple-element.52), channel_id=1, source_target_pairs={{0,16},{16,0},{32,48},{48,32},{64,80},{80,64},{96,112},{112,96},{1... | collective-permute-start | bytes 294920 | tf_op jit(solution)/shard_map/ppermute | solution.py:33
  122.1 4.8 %collective-permute-start.11 = (f32[24,8,128]{2,1,0:T(8,128)S(1)}, f32[24,8,128]{2,1,0:T(8,128)S(1)}, u32[]{:S(2)}, u32[]{:S(2)}) collective-permute-start(f32[24,8,128]{2,1,0:T(8,128)S(1)} %get-tuple-element.53), channel_id=1, source_target_pairs={{16,32},{32,16},{48,64},{64,48},{80,96},{96,80},{112,128},{128,112... | collective-permute-start | bytes 294920 | tf_op jit(solution)/shard_map/ppermute | solution.py:32
  127.0 8.6 %collective-permute-done.11.rb = f32[24,8,128]{2,1,0:T(8,128)S(1)} collective-permute-done((f32[24,8,128]{2,1,0:T(8,128)S(1)}, f32[24,8,128]{2,1,0:T(8,128)S(1)}, u32[]{:S(2)}, u32[]{:S(2)}) %collective-permute-start.11) | collective-permute-done | bytes 98336 | tf_op jit(solution)/shard_map/ppermute | solution.py:32
  135.6 2.0 %last.1 = (f32[6,8,128]{2,1,0:T(8,128)}, f32[2,6,8,128]{3,2,1,0:T(8,128)}) custom-call(s32[48]{0:T(128)S(1)} %copy-done, f32[192,24,256]{2,1,0:T(8,128)S(1)} %get-tuple-element.38.st, f32[72,24,256]{2,1,0:T(8,128)S(1)} %get-tuple-element.49.s_old, f32[48,24,256]{2,1,0:T(8,128)S(1)} %get-tuple-element.50.v_old, f32[18,8,128]{2,1,0:T(8,128)S(1)} %get-tuple-element.51.kern_old, ...), custom_call_target="tpu_custom_call" | custom-call | tf_op jit(solution)/shard_map/last/pallas_call | solution.py:379
  (9 shorter events, 4.9 us)
Async XLA Ops:
  0.6 0.7 copy-start
  3.0 11.5 %collective-permute-start = (f32[76,8,128]{2,1,0:T(8,128)S(1)}, f32[76,8,128]{2,1,0:T(8,128)S(1)}, u32[]{:S(2)}, u32[]{:S(2)}) collective-permute-start(f32[76,8,128]{2,1,0:T(8,128)S(1)} %get-tuple-element.34), channel_id=1, source_target_pairs={{0,16},{16,0},{32,48},{48,32},{64,80},{80,64},{96,112},{112,96},{1... | collective-permute-start | bytes 933896 | tf_op jit(solution)/shard_map/ppermute | solution.py:33
  7.0 17.9 %collective-permute-start.1 = (f32[76,8,128]{2,1,0:T(8,128)S(1)}, f32[76,8,128]{2,1,0:T(8,128)S(1)}, u32[]{:S(2)}, u32[]{:S(2)}) collective-permute-start(f32[76,8,128]{2,1,0:T(8,128)S(1)} %get-tuple-element.35), channel_id=1, source_target_pairs={{16,32},{32,16},{48,64},{64,48},{80,96},{96,80},{112,128},{128,112... | collective-permute-start | bytes 933896 | tf_op jit(solution)/shard_map/ppermute | solution.py:32
  25.5 22.0 %collective-permute-start.3 = (f32[192,8,128]{2,1,0:T(8,128)S(1)}, f32[192,8,128]{2,1,0:T(8,128)S(1)}, u32[]{:S(2)}, u32[]{:S(2)}) collective-permute-start(f32[192,8,128]{2,1,0:T(8,128)S(1)} %window.1.w), channel_id=1, source_target_pairs={{4,8},{8,4},{5,9},{9,5},{6,10},{10,6},{7,11},{11,7},{20,24},{24,20... | collective-permute-start | bytes 2359304 | tf_op jit(solution)/shard_map/ppermute | solution.py:32
  27.5 20.1 %collective-permute-start.2 = (f32[192,8,128]{2,1,0:T(8,128)S(1)}, f32[192,8,128]{2,1,0:T(8,128)S(1)}, u32[]{:S(2)}, u32[]{:S(2)}) collective-permute-start(f32[192,8,128]{2,1,0:T(8,128)S(1)} %window.1.w), channel_id=1, source_target_pairs={{0,4},{4,0},{8,12},{12,8},{1,5},{5,1},{9,13},{13,9},{2,6},{6,2},{1... | collective-permute-start | bytes 2359304 | tf_op jit(solution)/shard_map/ppermute | solution.py:33
  50.2 7.0 %collective-permute-start.4 = (f32[36,8,128]{2,1,0:T(8,128)S(1)}, f32[36,8,128]{2,1,0:T(8,128)S(1)}, u32[]{:S(2)}, u32[]{:S(2)}) collective-permute-start(f32[36,8,128]{2,1,0:T(8,128)S(1)} %get-tuple-element.36), channel_id=1, source_target_pairs={{0,1},{1,0},{2,3},{3,2},{4,5},{5,4},{6,7},{7,6},{8,9},{9,8},{10,11... | collective-permute-start | bytes 442376 | tf_op jit(solution)/shard_map/ppermute | solution.py:33
  53.3 7.0 %collective-permute-start.5 = (f32[36,8,128]{2,1,0:T(8,128)S(1)}, f32[36,8,128]{2,1,0:T(8,128)S(1)}, u32[]{:S(2)}, u32[]{:S(2)}) collective-permute-start(f32[36,8,128]{2,1,0:T(8,128)S(1)} %get-tuple-element.37), channel_id=1, source_target_pairs={{1,2},{2,1},{5,6},{6,5},{9,10},{10,9},{13,14},{14,13},{17,18},{18,... | collective-permute-start | bytes 442376 | tf_op jit(solution)/shard_map/ppermute | solution.py:32
  64.4 25.8 %collective-permute-start.6 = (f32[54,8,128]{2,1,0:T(8,128)S(1)}, f32[54,8,128]{2,1,0:T(8,128)S(1)}, u32[]{:S(2)}, u32[]{:S(2)}) collective-permute-start(f32[54,8,128]{2,1,0:T(8,128)S(1)} %get-tuple-element.42), channel_id=1, source_target_pairs={{0,16},{16,0},{32,48},{48,32},{64,80},{80,64},{96,112},{112,96},{1... | collective-permute-start | bytes 663560 | tf_op jit(solution)/shard_map/ppermute | solution.py:33
  84.2 15.9 %collective-permute-start.7 = (f32[54,8,128]{2,1,0:T(8,128)S(1)}, f32[54,8,128]{2,1,0:T(8,128)S(1)}, u32[]{:S(2)}, u32[]{:S(2)}) collective-permute-start(f32[54,8,128]{2,1,0:T(8,128)S(1)} %get-tuple-element.43), channel_id=1, source_target_pairs={{16,32},{32,16},{48,64},{64,48},{80,96},{96,80},{112,128},{128,112... | collective-permute-start | bytes 663560 | tf_op jit(solution)/shard_map/ppermute | solution.py:32
  102.2 7.1 %collective-permute-start.8 = (f32[38,8,128]{2,1,0:T(8,128)S(1)}, f32[38,8,128]{2,1,0:T(8,128)S(1)}, u32[]{:S(2)}, u32[]{:S(2)}) collective-permute-start(f32[38,8,128]{2,1,0:T(8,128)S(1)} %get-tuple-element.47), channel_id=1, source_target_pairs={{0,16},{16,0},{32,48},{48,32},{64,80},{80,64},{96,112},{112,96},{1... | collective-permute-start | bytes 466952 | tf_op jit(solution)/shard_map/ppermute | solution.py:33
  104.1 14.0 %collective-permute-start.9 = (f32[38,8,128]{2,1,0:T(8,128)S(1)}, f32[38,8,128]{2,1,0:T(8,128)S(1)}, u32[]{:S(2)}, u32[]{:S(2)}) collective-permute-start(f32[38,8,128]{2,1,0:T(8,128)S(1)} %get-tuple-element.48), channel_id=1, source_target_pairs={{16,32},{32,16},{48,64},{64,48},{80,96},{96,80},{112,128},{128,112... | collective-permute-start | bytes 466952 | tf_op jit(solution)/shard_map/ppermute | solution.py:32
  120.2 6.8 %collective-permute-start.10 = (f32[24,8,128]{2,1,0:T(8,128)S(1)}, f32[24,8,128]{2,1,0:T(8,128)S(1)}, u32[]{:S(2)}, u32[]{:S(2)}) collective-permute-start(f32[24,8,128]{2,1,0:T(8,128)S(1)} %get-tuple-element.52), channel_id=1, source_target_pairs={{0,16},{16,0},{32,48},{48,32},{64,80},{80,64},{96,112},{112,96},{1... | collective-permute-start | bytes 294920 | tf_op jit(solution)/shard_map/ppermute | solution.py:33
  122.1 13.4 %collective-permute-start.11 = (f32[24,8,128]{2,1,0:T(8,128)S(1)}, f32[24,8,128]{2,1,0:T(8,128)S(1)}, u32[]{:S(2)}, u32[]{:S(2)}) collective-permute-start(f32[24,8,128]{2,1,0:T(8,128)S(1)} %get-tuple-element.53), channel_id=1, source_target_pairs={{16,32},{32,16},{48,64},{64,48},{80,96},{96,80},{112,128},{128,112... | collective-permute-start | bytes 294920 | tf_op jit(solution)/shard_map/ppermute | solution.py:32

commit v4 on v3

--- a/solution.py
+++ b/solution.py
@@ -1,5 +1,3 @@
-import functools
-
 import jax
 import jax.numpy as jnp
 from jax import lax
@@ -7,7 +5,6 @@
 from jax.experimental.pallas import tpu as pltpu
 from jax.sharding import PartitionSpec as P
 
-STEPS = 4
 H = 0.15
 PAIRS = ((0, 5, 4), (5, 1, 3), (4, 3, 2))
 
@@ -16,7 +13,22 @@
 PA, PV, PS, PR, PL, NP1 = 0, 36, 45, 69, 72, 76
 ALL12 = list(range(12))
 X6 = [0, 5, 4, 6, 11, 10]
-DEPTHS = ((8, 4), (4, 2), (1, 0))
+MID = [
+    ([("s", 1, e) for e in ALL12], 5),
+    (
+        [("s", dx, e) for dx in (2, 3) for e in ALL12]
+        + [("v", 2, e) for e in range(6)]
+        + [("c", 2, 0), ("l", 1, 0), ("m", 1, 0)],
+        4,
+    ),
+    (
+        [("s", 4, e) for e in X6]
+        + [("v", 3, e) for e in range(6)]
+        + [("c", 3, 0), ("l", 2, 0), ("m", 2, 0)],
+        2,
+    ),
+]
+LAST = [([("s", 1, e) for e in ALL12], 1), ([("s", 2, e) for e in X6], 0)]
 VMEM_LIMIT = 16 << 20
 
 
@@ -171,28 +183,37 @@
     return f[8:16, 0:128]
 
 
-def one_step(coefs, stress_at, v_old, kern_old, v_new, kern, s_new=None):
-    for p in range(1, 9):
-        coef = coefs[CB + p - 1]
+def cut(f):
+    return f[8:16, 0:128]
+
+
+def velocity_step(planes, coef_at, stress_at, v_old, v_new, base):
+    for p in planes:
+        coef = coef_at(p)
         for q in range(2):
             for i in range(3):
                 x, y, z = PAIRS[i]
                 force = stress_at(p + 1, q * 6 + x) - stress_at(p - 1, q * 6 + x)
                 force = force + rows_diff(stress_at(p, q * 6 + y))
                 force = force + lanes_diff(stress_at(p, q * 6 + z))
-                n = (p - 1) * 6 + q * 3 + i
-                v_new[n] = v_old(n) - coef * force if q == 0 else v_old(n) + coef * force
+                e = q * 3 + i
+                step = coef * force
+                old = v_old(p, e)
+                v_new[(p - base) * 6 + e] = old - step if q == 0 else old + step
+
+
+def stress_step(planes, lame_at, stress_at, v, v_base, kern_old, kern, s_new=None, s_base=2):
     last = s_new is None
     keep = cut if last else (lambda f: f)
     own_cut = (lambda f: f) if last else cut
-    for p in range(2, 8):
+    for p in planes:
         if not last:
-            lam, mu = coefs[LB + p - 2], coefs[MB + p - 2]
+            lam, mu = lame_at(p)
         traces, diags, shears, vels = [], [], [], []
         for q in range(2):
-            v = (p - 1) * 6 + q * 3
-            own = [v_new[v + i] for i in range(3)]
-            dx = [keep(v_new[v + 6 + i]) - keep(v_new[v - 6 + i]) for i in range(3)]
+            n = (p - v_base) * 6 + q * 3
+            own = [v[n + i] for i in range(3)]
+            dx = [keep(v[n + 6 + i]) - keep(v[n - 6 + i]) for i in range(3)]
             dy = [keep(rows_diff(f)) for f in own]
             dz = [keep(lanes_diff(f)) for f in own]
             diag = [dx[0], dy[1], dz[2]]
@@ -204,17 +225,20 @@
                     a = iso + (2.0 * mu) * diag[c]
                     b = mu * shear[c]
                     e = q * 6 + c
-                    n = (p - 2) * 12 + e
+                    n = (p - s_base) * 12 + e
                     if q == 0:
                         s_new[n] = stress_at(p, e) - a
                         s_new[n + 3] = stress_at(p, e + 3) - b
                     else:
                         s_new[n] = stress_at(p, e) + a
                         s_new[n + 3] = stress_at(p, e + 3) + b
-            traces.append(own_cut(trace))
-            diags.append([own_cut(f) for f in diag])
-            shears.append([own_cut(f) for f in shear])
-            vels.append([cut(f) for f in own])
+            if 2 <= p < 8:
+                traces.append(own_cut(trace))
+                diags.append([own_cut(f) for f in diag])
+                shears.append([own_cut(f) for f in shear])
+                vels.append([cut(f) for f in own])
+        if not 2 <= p < 8:
+            continue
         dot = lambda pair: (
             pair[0][0] * pair[1][0] + pair[0][1] * pair[1][1] + pair[0][2] * pair[1][2]
         )
@@ -228,46 +252,59 @@
             kern[n] = new[k] if kern_old is None else kern_old[n] + new[k]
 
 
-def row_groups(entries, m):
-    size = 4 // m
-    return [entries[k : k + size] for k in range(0, len(entries), size)]
-
-
-def face_blocks(depths):
-    blocks = [(1, "own", [e]) for e in ALL12] + [(2, "own", [e]) for e in X6]
-    for dx, entries, m in ((1, ALL12, depths[0]), (2, X6, depths[1])):
-        if m == 8:
-            blocks += [(dx, side, [e]) for e in entries for side in ("low", "high")]
+def face_blocks(spec):
+    blocks = [("own", [item]) for items, _ in spec for item in items]
+    for items, m in spec:
+        if m == 5:
+            blocks += [(4, [item]) for item in items]
+            blocks += [(5, items[k : k + 4]) for k in range(0, len(items), 4)]
         elif m:
-            blocks += [(dx, m, group) for group in row_groups(entries, m)]
+            size = 4 // m
+            blocks += [(m, items[k : k + size]) for k in range(0, len(items), size)]
     return blocks
 
 
-def face_tiles(depths):
-    count = len(face_blocks(depths))
+def face_tiles(spec):
+    count = len(face_blocks(spec))
     return count + -(-count // 8)
 
 
-def write_faces(odd, depths, s_new, face_a, face_b):
+def face_places(spec):
+    items = [item for group, _ in spec for item in group]
+    return {item: k for k, item in enumerate(items)}, len(items)
+
+
+def write_faces(odd, spec, st, s_new, v_new, face_a, face_b):
     lane = lanes()
     row = lax.broadcasted_iota(jnp.int32, (8, 256), 0)
-    blocks = face_blocks(depths)
+    blocks = face_blocks(spec)
     count = len(blocks)
     for face, up in ((face_a, 1 - odd), (face_b, odd)):
-        first = {1: (2 + up) * 12, 2: (3 - up) * 12}
+
+        def source(item):
+            kind, dx, e = item
+            p = (3 + dx) + up * (3 - 2 * dx)
+            if kind == "s":
+                return s_new, (p - 2) * 12 + e
+            if kind == "v":
+                return v_new, (p - 1) * 6 + e
+            return st, {"c": CB - 1, "l": LB - 2, "m": MB - 2}[kind] + p
+
         acc = None
-        for j, (dx, halo, entries) in enumerate(blocks):
-            at = lambda e: first[dx] + e
-            if halo == "own":
-                x = s_new[at(entries[0]), 8:16, :]
-            elif halo == "low":
-                x = s_new[at(entries[0]), 0:8, :]
-            elif halo == "high":
-                x = s_new[at(entries[0]), 16:24, :]
+        for j, (kind, items) in enumerate(blocks):
+            if kind == "own":
+                ref, n = source(items[0])
+                x = ref[n, 8:16, :]
             else:
-                m, x = halo, None
-                for k, e in enumerate(entries):
-                    c = jnp.where(row < 4, s_new[at(e), 16:24, :], s_new[at(e), 0:8, :])
+                m, x = kind, None
+                for k, item in enumerate(items):
+                    ref, n = source(item)
+                    low, high = ref[n, 0:8, :], ref[n, 16:24, :]
+                    if m == 5:
+                        c = pltpu.roll(jnp.where(row == 3, low, high), (2 * k + 5) % 8, 0)
+                        x = c if x is None else jnp.where(row < 2 * k, x, c)
+                        continue
+                    c = jnp.where(row < 4, high, low)
                     if m < 4:
                         c = pltpu.roll(c, (m + 2 * m * k) % 8, 0)
                     x = c if x is None else jnp.where(row < 2 * m * k, x, c)
@@ -279,39 +316,43 @@
                 face[count + j // 8] = acc
 
 
-def read_faces(odd, depths, ra, rb, halo):
+def read_faces(odd, spec, ra, rb, halo):
     lane = lanes()
     edge = (lane < 8) | (lane >= 120)
     low_is_a = odd == 1
-    blocks = face_blocks(depths)
+    blocks = face_blocks(spec)
     count = len(blocks)
+    place, total = face_places(spec)
     for low in (True, False):
-        first = {1: 12 if low else 24, 2: 0 if low else 36}
+        first = 0 if low else total
         pick = low_is_a if low else jnp.logical_not(low_is_a)
         get = lambda n: jnp.where(pick, ra[n], rb[n])
         packed = None
-        for j, (dx, kind, entries) in enumerate(blocks):
+        for j, (kind, items) in enumerate(blocks):
             k = j % 8
             if k == 0:
                 packed = get(count + j // 8)
             h = pltpu.roll(packed, (120 - 16 * k) % 128, 1)
             x = jnp.concatenate([get(j), jnp.where(edge, h, 0.0)], axis=1)
-            if kind in ("own", "low", "high"):
-                r = {"low": 0, "own": 8, "high": 16}[kind]
-                halo[first[dx] + entries[0], r : r + 8, :] = x
-            else:
-                m = kind
-                for i, e in enumerate(entries):
-                    c = x if m == 4 else pltpu.roll(x, (16 - m - 2 * m * i) % 8, 0)
-                    halo[first[dx] + e, 0:8, :] = c
-                    halo[first[dx] + e, 16:24, :] = c
-        if depths[1] == 0:
-            for e in X6:
-                halo[first[2] + e, 0:8, :] = jnp.zeros((8, 256), jnp.float32)
-                halo[first[2] + e, 16:24, :] = jnp.zeros((8, 256), jnp.float32)
-
-
-def first_kernel(depths, offsets, w, ga, gb, za, zb, st, s_new, v_new, kern, face_a, face_b):
+            for i, item in enumerate(items):
+                n = first + place[item]
+                if kind == "own":
+                    halo[n, 8:16, :] = x
+                elif kind == 5:
+                    c = pltpu.roll(x, (11 - 2 * i) % 8, 0)
+                    halo[n, 3:4, :] = c[3:4, :]
+                    halo[n, 20:21, :] = c[4:5, :]
+                else:
+                    c = x if kind == 4 else pltpu.roll(x, (16 - kind - 2 * kind * i) % 8, 0)
+                    halo[n, 0:8, :] = c
+                    halo[n, 16:24, :] = c
+        for items, m in spec:
+            for item in items if m == 0 else ():
+                halo[first + place[item], 0:8, :] = jnp.zeros((8, 256), jnp.float32)
+                halo[first + place[item], 16:24, :] = jnp.zeros((8, 256), jnp.float32)
+
+
+def first_kernel(offsets, w, ga, gb, za, zb, st, s_new, v_new, kern, face_a, face_b):
     odd, _, _, gy_odd, gz_odd = where_am_i(offsets)
     lane = lanes()
 
@@ -335,36 +376,71 @@
         return carry
 
     lax.fori_loop(0, 12, group, 0)
-    one_step(st, lambda p, e: st[p * 12 + e], lambda n: st[VB + n], None, v_new, kern, s_new)
-    write_faces(odd, depths, s_new, face_a, face_b)
-
-
-def with_halo(s_old, halo):
-    def stress_at(p, e):
-        if p < 2:
-            return halo[p * 12 + e]
-        if p > 7:
-            return halo[24 + (p - 8) * 12 + e]
-        return s_old[(p - 2) * 12 + e]
-
-    return stress_at
-
-
-def step_kernel(
-    before, after, offsets, st, s_old, v_old, kern_old, ra, rb, s_new, v_new, kern, face_a, face_b, halo
+    stress_at = lambda p, e: st[p * 12 + e]
+    velocity_step(
+        range(1, 9),
+        lambda p: st[CB + p - 1],
+        stress_at,
+        lambda p, e: st[VB + (p - 1) * 6 + e],
+        v_new,
+        1,
+    )
+    lame_at = lambda p: (st[LB + p - 2], st[MB + p - 2])
+    stress_step(range(2, 8), lame_at, stress_at, v_new, 1, None, kern, s_new)
+    write_faces(odd, MID, st, s_new, v_new, face_a, face_b)
+
+
+def reader(spec, halo):
+    place, total = face_places(spec)
+
+    def at(kind, p, first, e, inside):
+        if first <= p <= 9 - first:
+            return inside()
+        low = p < first
+        dx = 2 - p if low else p - 7
+        return halo[place[(kind, dx, e)] + (0 if low else total)]
+
+    return at
+
+
+def middle_kernel(
+    offsets, st, s_old, v_old, kern_old, ra, rb, s_new, v_new, kern, face_a, face_b, halo, s_mid, v_mid
 ):
     odd = where_am_i(offsets)[0]
-    read_faces(odd, before, ra, rb, halo)
-    one_step(st, with_halo(s_old, halo), lambda n: v_old[n], kern_old, v_new, kern, s_new)
-    write_faces(odd, after, s_new, face_a, face_b)
+    read_faces(odd, MID, ra, rb, halo)
+    at = reader(MID, halo)
+    coef_at = lambda p: at("c", p, 1, 0, lambda: st[CB + p - 1])
+    lame_at = lambda p: (
+        at("l", p, 2, 0, lambda: st[LB + p - 2]),
+        at("m", p, 2, 0, lambda: st[MB + p - 2]),
+    )
+    stress_at = lambda p, e: at("s", p, 2, e, lambda: s_old[(p - 2) * 12 + e])
+    v_at = lambda p, e: at("v", p, 1, e, lambda: v_old[(p - 1) * 6 + e])
+    velocity_step(range(-1, 11), coef_at, stress_at, v_at, v_mid, -1)
+    stress_step(range(0, 10), lame_at, stress_at, v_mid, -1, kern_old, kern, s_mid, 0)
+    stress_mid = lambda p, e: s_mid[p * 12 + e]
+    v_at_mid = lambda p, e: v_mid[(p + 1) * 6 + e]
+    velocity_step(range(1, 9), coef_at, stress_mid, v_at_mid, v_new, 1)
+    stress_step(range(2, 8), lame_at, stress_mid, v_new, 1, kern, kern, s_new)
+    write_faces(odd, LAST, st, s_new, v_new, face_a, face_b)
 
 
 def last_kernel(
-    before, offsets, st, s_old, v_old, kern_old, ra, rb, dens, modu, halo, v_new, kern
+    offsets, st, s_old, v_old, kern_old, ra, rb, dens, modu, halo, v_new, kern
 ):
     odd, off, noff, _, _ = where_am_i(offsets)
-    read_faces(odd, before, ra, rb, halo)
-    one_step(st, with_halo(s_old, halo), lambda n: v_old[n], kern_old, v_new, kern)
+    read_faces(odd, LAST, ra, rb, halo)
+    at = reader(LAST, halo)
+    stress_at = lambda p, e: at("s", p, 2, e, lambda: s_old[(p - 2) * 12 + e])
+    velocity_step(
+        range(1, 9),
+        lambda p: st[CB + p - 1],
+        stress_at,
+        lambda p, e: v_old[(p - 1) * 6 + e],
+        v_new,
+        1,
+    )
+    stress_step(range(2, 8), None, stress_at, v_new, 1, kern_old, kern)
     extent = 4 + noff - off
     for r in range(6):
         row = jnp.minimum(off + r, 5)
@@ -405,29 +481,29 @@
     edges = call(edge_kernel, "edge", [(36, 8, 128)] * 2, (offsets, win, ga, gb))
     za, zb = both_swaps(*edges, "gz")
     carried = [(72, 24, 256), (48, 24, 256), (18, 8, 128)]
-    faces = lambda k: [(face_tiles(DEPTHS[k]), 8, 128)] * 2
+    faces = lambda spec: [(face_tiles(spec), 8, 128)] * 2
+    halos = lambda spec: (2 * face_places(spec)[1], 24, 256)
     state, *moving, face_a, face_b = call(
-        functools.partial(first_kernel, DEPTHS[0]),
+        first_kernel,
         "first",
-        [(N, 24, 256)] + carried + faces(0),
+        [(N, 24, 256)] + carried + faces(MID),
         (offsets, win, ga, gb, za, zb),
     )
-    for k in range(STEPS - 2):
-        recv = both_swaps(face_a, face_b, "grp")
-        *moving, face_a, face_b = call(
-            functools.partial(step_kernel, DEPTHS[k], DEPTHS[k + 1]),
-            "step",
-            carried + faces(k + 1),
-            (offsets, state, *moving, *recv),
-            [(48, 24, 256)],
-        )
+    recv = both_swaps(face_a, face_b, "grp")
+    *moving, face_a, face_b = call(
+        middle_kernel,
+        "middle",
+        carried + faces(LAST),
+        (offsets, state, *moving, *recv),
+        [halos(MID), (120, 24, 256), (72, 24, 256)],
+    )
     recv = both_swaps(face_a, face_b, "grp")
     dens, modu = call(
-        functools.partial(last_kernel, DEPTHS[STEPS - 2]),
+        last_kernel,
         "last",
         [(6, 8, 128), (2, 6, 8, 128)],
         (offsets, state, *moving, *recv),
-        [(48, 24, 256), (48, 24, 256), (18, 8, 128)],
+        [halos(LAST), (48, 24, 256), (18, 8, 128)],
     )
     return dens, modu
 

time: 138 us -> 130 us (0.942)
  the two profiles are of different devices: /device:TPU:420 before, /device:TPU:37 now
where the time goes in v4:
time: 130 us
  starting transfers between devices  67.9 us (52%)
  waiting for transfers between devices  44.3 us (34%)
  Pallas kernels  16 us (12%)
    ppermute x5, waiting for transfers between devices, both_swaps(): second = lax.ppermute(value_b, axis, swaps(count, 1))  42.5 us
    ppermute x5, starting transfers between devices, both_swaps(): second = lax.ppermute(value_b, axis, swaps(count, 1))  36.9 us
    ppermute x5, starting transfers between devices, both_swaps(): first = lax.ppermute(value_a, axis, swaps(count, 0))  31 us
    pallas_call x6, Pallas kernels, call(): pl.pallas_call(kernel, out_shape=[jax.ShapeDtypeStruct(s, jnp.float32) fo...  16 us
  transfers between devices with their start and end apart: 10, of which 7 were waited for; matrix products, arithmetic and copies ran while one was open for 0% of the time, Pallas kernels for 0%

profile of v4, /device:TPU:37, one launch (start us, length us, event | category | flops | bytes accessed | tf_op | source)
XLA Modules:
  0.0 129.6 jit_solution(4748934429544254726)
XLA Ops:
  0.6 0.6 copy-done
  1.3 1.7 %pack.1 = (f32[76,8,128]{2,1,0:T(8,128)S(1)}, f32[76,8,128]{2,1,0:T(8,128)S(1)}, f32[3,4,8,128]{3,2,1,0:T(8,128)S(1)}, f32[6,4,8,128]{3,2,1,0:T(8,128)S(1)}, f32...) custom-call(s32[48]{0:T(128)S(1)} %copy-done, ...), custom_call_target="tpu_custom_call" | custom-call | tf_op jit(solution)/shard_map/pack/pallas_call | solution.py:455
  3.0 4.0 %collective-permute-start = (f32[76,8,128]{2,1,0:T(8,128)S(1)}, f32[76,8,128]{2,1,0:T(8,128)S(1)}, u32[]{:S(2)}, u32[]{:S(2)}) collective-permute-start(f32[76,8,128]{2,1,0:T(8,128)S(1)} %get-tuple-element.29), channel_id=1, source_target_pairs={{0,16},{16,0},{32,48},{48,32},{64,80},{80,64},{96,112},{112,96},{1... | collective-permute-start | bytes 933896 | tf_op jit(solution)/shard_map/ppermute | solution.py:45
  7.0 10.2 %collective-permute-start.1 = (f32[76,8,128]{2,1,0:T(8,128)S(1)}, f32[76,8,128]{2,1,0:T(8,128)S(1)}, u32[]{:S(2)}, u32[]{:S(2)}) collective-permute-start(f32[76,8,128]{2,1,0:T(8,128)S(1)} %get-tuple-element.30), channel_id=1, source_target_pairs={{16,32},{32,16},{48,64},{64,48},{80,96},{96,80},{112,128},{128,112... | collective-permute-start | bytes 933896 | tf_op jit(solution)/shard_map/ppermute | solution.py:44
  17.3 11.8 %collective-permute-done.1.rb = f32[76,8,128]{2,1,0:T(8,128)S(1)} collective-permute-done((f32[76,8,128]{2,1,0:T(8,128)S(1)}, f32[76,8,128]{2,1,0:T(8,128)S(1)}, u32[]{:S(2)}, u32[]{:S(2)}) %collective-permute-start.1) | collective-permute-done | bytes 311328 | tf_op jit(solution)/shard_map/ppermute | solution.py:44
  29.1 0.6 window.1.w
  29.7 11.2 %collective-permute-start.3 = (f32[192,8,128]{2,1,0:T(8,128)S(1)}, f32[192,8,128]{2,1,0:T(8,128)S(1)}, u32[]{:S(2)}, u32[]{:S(2)}) collective-permute-start(f32[192,8,128]{2,1,0:T(8,128)S(1)} %window.1.w), channel_id=1, source_target_pairs={{4,8},{8,4},{5,9},{9,5},{6,10},{10,6},{7,11},{11,7},{20,24},{24,20... | collective-permute-start | bytes 2359304 | tf_op jit(solution)/shard_map/ppermute | solution.py:44
  41.0 1.9 %collective-permute-start.2 = (f32[192,8,128]{2,1,0:T(8,128)S(1)}, f32[192,8,128]{2,1,0:T(8,128)S(1)}, u32[]{:S(2)}, u32[]{:S(2)}) collective-permute-start(f32[192,8,128]{2,1,0:T(8,128)S(1)} %window.1.w), channel_id=1, source_target_pairs={{0,4},{4,0},{8,12},{12,8},{1,5},{5,1},{9,13},{13,9},{2,6},{6,2},{1... | collective-permute-start | bytes 2359304 | tf_op jit(solution)/shard_map/ppermute | solution.py:45
  42.9 9.9 %collective-permute-done.3.gb = f32[192,8,128]{2,1,0:T(8,128)S(1)} collective-permute-done((f32[192,8,128]{2,1,0:T(8,128)S(1)}, f32[192,8,128]{2,1,0:T(8,128)S(1)}, u32[]{:S(2)}, u32[]{:S(2)}) %collective-permute-start.3) | collective-permute-done | bytes 786464 | tf_op jit(solution)/shard_map/ppermute | solution.py:44
  52.8 2.6 %edge.1 = (f32[36,8,128]{2,1,0:T(8,128)S(1)}, f32[36,8,128]{2,1,0:T(8,128)S(1)}) custom-call(s32[48]{0:T(128)S(1)} %copy-done, f32[192,8,128]{2,1,0:T(8,128)S(1)} %window.1.w, f32[192,8,128]{2,1,0:T(8,128)S(1)} %collective-permute-done.2.ga, f32[192,8,128]{2,1,0:T(8,128)S(1)} %collective-permute-done.3.gb), custom_call_target="tpu_custom_call" | custom-call | tf_op jit(solution)/shard_map/edge/pallas_call | solution.py:455
  55.5 2.8 %collective-permute-start.4 = (f32[36,8,128]{2,1,0:T(8,128)S(1)}, f32[36,8,128]{2,1,0:T(8,128)S(1)}, u32[]{:S(2)}, u32[]{:S(2)}) collective-permute-start(f32[36,8,128]{2,1,0:T(8,128)S(1)} %get-tuple-element.31), channel_id=1, source_target_pairs={{0,1},{1,0},{2,3},{3,2},{4,5},{5,4},{6,7},{7,6},{8,9},{9,8},{10,11... | collective-permute-start | bytes 442376 | tf_op jit(solution)/shard_map/ppermute | solution.py:45
  58.3 1.9 %collective-permute-start.5 = (f32[36,8,128]{2,1,0:T(8,128)S(1)}, f32[36,8,128]{2,1,0:T(8,128)S(1)}, u32[]{:S(2)}, u32[]{:S(2)}) collective-permute-start(f32[36,8,128]{2,1,0:T(8,128)S(1)} %get-tuple-element.32), channel_id=1, source_target_pairs={{1,2},{2,1},{5,6},{6,5},{9,10},{10,9},{13,14},{14,13},{17,18},{18,... | collective-permute-start | bytes 442376 | tf_op jit(solution)/shard_map/ppermute | solution.py:44
  60.2 1.1 collective-permute-done.4.za
  61.4 2.8 %collective-permute-done.5.zb = f32[36,8,128]{2,1,0:T(8,128)S(1)} collective-permute-done((f32[36,8,128]{2,1,0:T(8,128)S(1)}, f32[36,8,128]{2,1,0:T(8,128)S(1)}, u32[]{:S(2)}, u32[]{:S(2)}) %collective-permute-start.5) | collective-permute-done | bytes 147488 | tf_op jit(solution)/shard_map/ppermute | solution.py:44
  64.2 4.3 %first.1 = (f32[192,24,256]{2,1,0:T(8,128)S(1)}, f32[72,24,256]{2,1,0:T(8,128)S(1)}, f32[48,24,256]{2,1,0:T(8,128)S(1)}, f32[18,8,128]{2,1,0:T(8,128)S(1)}, f32[...) custom-call(s32[48]{0:T(128)S(1)} %copy-done, f32[192,8,128]{2,1,0:T(8,128)S(1)} %window.1.w, ...), custom_call_target="tpu_custom_call" | custom-call | tf_op jit(solution)/shard_map/first/pallas_call | solution.py:455
  68.5 20.3 %collective-permute-start.6 = (f32[131,8,128]{2,1,0:T(8,128)S(1)}, f32[131,8,128]{2,1,0:T(8,128)S(1)}, u32[]{:S(2)}, u32[]{:S(2)}) collective-permute-start(f32[131,8,128]{2,1,0:T(8,128)S(1)} %get-tuple-element.37), channel_id=1, source_target_pairs={{0,16},{16,0},{32,48},{48,32},{64,80},{80,64},{96,112},{112,96},{1... | collective-permute-start | bytes 1609736 | tf_op jit(solution)/shard_map/ppermute | solution.py:45
  88.9 7.1 %collective-permute-start.7 = (f32[131,8,128]{2,1,0:T(8,128)S(1)}, f32[131,8,128]{2,1,0:T(8,128)S(1)}, u32[]{:S(2)}, u32[]{:S(2)}) collective-permute-start(f32[131,8,128]{2,1,0:T(8,128)S(1)} %get-tuple-element.38), channel_id=1, source_target_pairs={{16,32},{32,16},{48,64},{64,48},{80,96},{96,80},{112,128},{128,112... | collective-permute-start | bytes 1609736 | tf_op jit(solution)/shard_map/ppermute | solution.py:44
  96.0 0.6 collective-permute-done.6.ra
  96.6 12.1 %collective-permute-done.7.rb = f32[131,8,128]{2,1,0:T(8,128)S(1)} collective-permute-done((f32[131,8,128]{2,1,0:T(8,128)S(1)}, f32[131,8,128]{2,1,0:T(8,128)S(1)}, u32[]{:S(2)}, u32[]{:S(2)}) %collective-permute-start.7) | collective-permute-done | bytes 536608 | tf_op jit(solution)/shard_map/ppermute | solution.py:44
  108.7 4.7 %middle.1 = (f32[72,24,256]{2,1,0:T(8,128)S(1)}, f32[48,24,256]{2,1,0:T(8,128)S(1)}, f32[18,8,128]{2,1,0:T(8,128)S(1)}, f32[24,8,128]{2,1,0:T(8,128)S(1)}, f32[24,8,128]{2,1,0:T(8,128)S(1)}) custom-call(s32[48]{0:T(128)S(1)} %copy-done, f32[192,24,256]{2,1,0:T(8,128)S(1)} %get-tuple-element.33.st, f32[72,24,256]{2,1,0:T(8,128)S(1)} %get-tuple-element.34.s_old, ...), custom_call_target="tpu_custom_call" | custom-call | tf_op jit(solution)/shard_map/middle/pallas_call | solution.py:455
  113.4 1.9 %collective-permute-start.8 = (f32[24,8,128]{2,1,0:T(8,128)S(1)}, f32[24,8,128]{2,1,0:T(8,128)S(1)}, u32[]{:S(2)}, u32[]{:S(2)}) collective-permute-start(f32[24,8,128]{2,1,0:T(8,128)S(1)} %get-tuple-element.42), channel_id=1, source_target_pairs={{0,16},{16,0},{32,48},{48,32},{64,80},{80,64},{96,112},{112,96},{1... | collective-permute-start | bytes 294920 | tf_op jit(solution)/shard_map/ppermute | solution.py:45
  115.3 6.4 %collective-permute-start.9 = (f32[24,8,128]{2,1,0:T(8,128)S(1)}, f32[24,8,128]{2,1,0:T(8,128)S(1)}, u32[]{:S(2)}, u32[]{:S(2)}) collective-permute-start(f32[24,8,128]{2,1,0:T(8,128)S(1)} %get-tuple-element.43), channel_id=1, source_target_pairs={{16,32},{32,16},{48,64},{64,48},{80,96},{96,80},{112,128},{128,112... | collective-permute-start | bytes 294920 | tf_op jit(solution)/shard_map/ppermute | solution.py:44
  121.7 5.9 %collective-permute-done.9.rb = f32[24,8,128]{2,1,0:T(8,128)S(1)} collective-permute-done((f32[24,8,128]{2,1,0:T(8,128)S(1)}, f32[24,8,128]{2,1,0:T(8,128)S(1)}, u32[]{:S(2)}, u32[]{:S(2)}) %collective-permute-start.9) | collective-permute-done | bytes 98336 | tf_op jit(solution)/shard_map/ppermute | solution.py:44
  127.6 2.0 %last.1 = (f32[6,8,128]{2,1,0:T(8,128)}, f32[2,6,8,128]{3,2,1,0:T(8,128)}) custom-call(s32[48]{0:T(128)S(1)} %copy-done, f32[192,24,256]{2,1,0:T(8,128)S(1)} %get-tuple-element.33.st, f32[72,24,256]{2,1,0:T(8,128)S(1)} %get-tuple-element.39.s_old, f32[48,24,256]{2,1,0:T(8,128)S(1)} %get-tuple-element.40.v_old, f32[18,8,128]{2,1,0:T(8,128)S(1)} %get-tuple-element.41.kern_old, ...), custom_call_target="tpu_custom_call" | custom-call | tf_op jit(solution)/shard_map/last/pallas_call | solution.py:455
  (4 shorter events, 0.0 us)
Async XLA Ops:
  0.6 0.7 copy-start
  3.0 14.3 %collective-permute-start = (f32[76,8,128]{2,1,0:T(8,128)S(1)}, f32[76,8,128]{2,1,0:T(8,128)S(1)}, u32[]{:S(2)}, u32[]{:S(2)}) collective-permute-start(f32[76,8,128]{2,1,0:T(8,128)S(1)} %get-tuple-element.29), channel_id=1, source_target_pairs={{0,16},{16,0},{32,48},{48,32},{64,80},{80,64},{96,112},{112,96},{1... | collective-permute-start | bytes 933896 | tf_op jit(solution)/shard_map/ppermute | solution.py:45
  7.0 22.1 %collective-permute-start.1 = (f32[76,8,128]{2,1,0:T(8,128)S(1)}, f32[76,8,128]{2,1,0:T(8,128)S(1)}, u32[]{:S(2)}, u32[]{:S(2)}) collective-permute-start(f32[76,8,128]{2,1,0:T(8,128)S(1)} %get-tuple-element.30), channel_id=1, source_target_pairs={{16,32},{32,16},{48,64},{64,48},{80,96},{96,80},{112,128},{128,112... | collective-permute-start | bytes 933896 | tf_op jit(solution)/shard_map/ppermute | solution.py:44
  29.7 23.1 %collective-permute-start.3 = (f32[192,8,128]{2,1,0:T(8,128)S(1)}, f32[192,8,128]{2,1,0:T(8,128)S(1)}, u32[]{:S(2)}, u32[]{:S(2)}) collective-permute-start(f32[192,8,128]{2,1,0:T(8,128)S(1)} %window.1.w), channel_id=1, source_target_pairs={{4,8},{8,4},{5,9},{9,5},{6,10},{10,6},{7,11},{11,7},{20,24},{24,20... | collective-permute-start | bytes 2359304 | tf_op jit(solution)/shard_map/ppermute | solution.py:44
  41.0 11.9 %collective-permute-start.2 = (f32[192,8,128]{2,1,0:T(8,128)S(1)}, f32[192,8,128]{2,1,0:T(8,128)S(1)}, u32[]{:S(2)}, u32[]{:S(2)}) collective-permute-start(f32[192,8,128]{2,1,0:T(8,128)S(1)} %window.1.w), channel_id=1, source_target_pairs={{0,4},{4,0},{8,12},{12,8},{1,5},{5,1},{9,13},{13,9},{2,6},{6,2},{1... | collective-permute-start | bytes 2359304 | tf_op jit(solution)/shard_map/ppermute | solution.py:45
  55.5 5.9 %collective-permute-start.4 = (f32[36,8,128]{2,1,0:T(8,128)S(1)}, f32[36,8,128]{2,1,0:T(8,128)S(1)}, u32[]{:S(2)}, u32[]{:S(2)}) collective-permute-start(f32[36,8,128]{2,1,0:T(8,128)S(1)} %get-tuple-element.31), channel_id=1, source_target_pairs={{0,1},{1,0},{2,3},{3,2},{4,5},{5,4},{6,7},{7,6},{8,9},{9,8},{10,11... | collective-permute-start | bytes 442376 | tf_op jit(solution)/shard_map/ppermute | solution.py:45
  58.3 5.9 %collective-permute-start.5 = (f32[36,8,128]{2,1,0:T(8,128)S(1)}, f32[36,8,128]{2,1,0:T(8,128)S(1)}, u32[]{:S(2)}, u32[]{:S(2)}) collective-permute-start(f32[36,8,128]{2,1,0:T(8,128)S(1)} %get-tuple-element.32), channel_id=1, source_target_pairs={{1,2},{2,1},{5,6},{6,5},{9,10},{10,9},{13,14},{14,13},{17,18},{18,... | collective-permute-start | bytes 442376 | tf_op jit(solution)/shard_map/ppermute | solution.py:44
  68.5 28.1 %collective-permute-start.6 = (f32[131,8,128]{2,1,0:T(8,128)S(1)}, f32[131,8,128]{2,1,0:T(8,128)S(1)}, u32[]{:S(2)}, u32[]{:S(2)}) collective-permute-start(f32[131,8,128]{2,1,0:T(8,128)S(1)} %get-tuple-element.37), channel_id=1, source_target_pairs={{0,16},{16,0},{32,48},{48,32},{64,80},{80,64},{96,112},{112,96},{1... | collective-permute-start | bytes 1609736 | tf_op jit(solution)/shard_map/ppermute | solution.py:45
  88.9 19.8 %collective-permute-start.7 = (f32[131,8,128]{2,1,0:T(8,128)S(1)}, f32[131,8,128]{2,1,0:T(8,128)S(1)}, u32[]{:S(2)}, u32[]{:S(2)}) collective-permute-start(f32[131,8,128]{2,1,0:T(8,128)S(1)} %get-tuple-element.38), channel_id=1, source_target_pairs={{16,32},{32,16},{48,64},{64,48},{80,96},{96,80},{112,128},{128,112... | collective-permute-start | bytes 1609736 | tf_op jit(solution)/shard_map/ppermute | solution.py:44
  113.4 8.3 %collective-permute-start.8 = (f32[24,8,128]{2,1,0:T(8,128)S(1)}, f32[24,8,128]{2,1,0:T(8,128)S(1)}, u32[]{:S(2)}, u32[]{:S(2)}) collective-permute-start(f32[24,8,128]{2,1,0:T(8,128)S(1)} %get-tuple-element.42), channel_id=1, source_target_pairs={{0,16},{16,0},{32,48},{48,32},{64,80},{80,64},{96,112},{112,96},{1... | collective-permute-start | bytes 294920 | tf_op jit(solution)/shard_map/ppermute | solution.py:45
  115.3 12.3 %collective-permute-start.9 = (f32[24,8,128]{2,1,0:T(8,128)S(1)}, f32[24,8,128]{2,1,0:T(8,128)S(1)}, u32[]{:S(2)}, u32[]{:S(2)}) collective-permute-start(f32[24,8,128]{2,1,0:T(8,128)S(1)} %get-tuple-element.43), channel_id=1, source_target_pairs={{16,32},{32,16},{48,64},{64,48},{80,96},{96,80},{112,128},{128,112... | collective-permute-start | bytes 294920 | tf_op jit(solution)/shard_map/ppermute | solution.py:44

commit v5 on v4

--- a/solution.py
+++ b/solution.py
@@ -8,11 +8,19 @@
 H = 0.15
 PAIRS = ((0, 5, 4), (5, 1, 3), (4, 3, 2))
 
-VB, CB, LB, MB = 120, 168, 176, 182
-N = 192
-PA, PV, PS, PR, PL, NP1 = 0, 36, 45, 69, 72, 76
+EB, VB, CB, LB, MB, N = 96, 108, 156, 164, 170, 176
+PA, PV, PS, PR, PL, NP1 = 0, 30, 39, 60, 63, 67
+X3 = [0, 5, 4]
 ALL12 = list(range(12))
 X6 = [0, 5, 4, 6, 11, 10]
+
+
+def entry_s(p, e):
+    if 1 <= p <= 8:
+        return (p - 1) * 12 + e
+    return EB + (6 if p == 9 else 0) + X6.index(e)
+
+
 MID = [
     ([("s", 1, e) for e in ALL12], 5),
     (
@@ -70,17 +78,21 @@
     fv, fs, rho, lam, av, as_ = held
     odd, off, _, _, _ = where_am_i(offsets)
     for out, up in ((out_a, 1 - odd), (out_b, odd)):
-        for i in range(4):
+        for k in range(4):
+            i = k + up * (3 - 2 * k)
             row = jnp.maximum(2 * up + i - off, 0)
-            for c in range(3):
-                out[PA + i * 9 + c] = av[c, row]
-            for c in range(6):
-                out[PA + i * 9 + 3 + c] = as_[c, row]
-                out[PS + i * 6 + c] = fs[c, i]
-        for i in range(3):
-            for c in range(3):
-                out[PV + i * 3 + c] = fv[c, i + up]
-            out[PR + i] = rho[i + up]
+            if k < 3:
+                for c in range(3):
+                    out[PA + k * 9 + c] = av[c, row]
+                    out[PV + k * 3 + c] = fv[c, k + up]
+                for c in range(6):
+                    out[PA + k * 9 + 3 + c] = as_[c, row]
+                    out[PS + k * 6 + c] = fs[c, i]
+                out[PR + k] = rho[k + up]
+            else:
+                for j, c in enumerate(X3):
+                    out[PA + 27 + j] = as_[c, row]
+                    out[PS + 18 + j] = fs[c, 3 - up]
         for i in range(2):
             for c in range(2):
                 out[PL + i * 2 + c] = lam[c, i]
@@ -97,28 +109,34 @@
         return jnp.where(low_is_a, rb[n], ra[n])
 
     def adjoint(p, ref, c, slot):
+        k = 3 - p if p < 5 else p - 6
+        n = PA + k * 9 + slot if k < 3 else PA + 27 + X3.index(c)
         if p < 2:
-            return low(PA + p * 9 + slot)
+            return low(n)
         if p > 7:
-            return high(PA + (p - 6) * 9 + slot)
+            return high(n)
         j = p - 2
         own = ref[c, jnp.clip(j - off, 0, 5)]
         if j < 2:
-            return jnp.where(j < off, low(PA + p * 9 + slot), own)
+            return jnp.where(j < off, low(n), own)
         if j > 3:
-            return jnp.where(j - 4 < noff, own, high(PA + (p - 6) * 9 + slot))
+            return jnp.where(j - 4 < noff, own, high(n))
         return own
 
     for p in range(10):
-        for c in range(6):
-            if p < 2:
-                f = low(PS + (p + 2) * 6 + c)
+        for c in range(6) if 1 <= p <= 8 else X3:
+            if p == 0:
+                f = low(PS + 18 + X3.index(c))
+            elif p == 1:
+                f = low(PS + c)
             elif p < 6:
                 f = fs[c, p - 2]
+            elif p < 9:
+                f = high(PS + (p - 6) * 6 + c)
             else:
-                f = high(PS + (p - 6) * 6 + c)
-            w[p * 12 + c] = f
-            w[p * 12 + 6 + c] = adjoint(p, as_, c, 3 + c)
+                f = high(PS + 18 + X3.index(c))
+            w[entry_s(p, c)] = f
+            w[entry_s(p, 6 + c)] = adjoint(p, as_, c, 3 + c)
     for p in range(1, 9):
         for c in range(3):
             if p < 2:
@@ -141,34 +159,41 @@
         for c, base in ((0, LB), (1, MB)):
             m = lam[c, p - 2] if p < 6 else high(PL + (p - 6) * 2 + c)
             w[base + p - 2] = (0.5 * H) * m
-    for n in range(188, N):
-        w[n] = jnp.zeros((8, 128), jnp.float32)
 
 
 def lanes():
     return lax.broadcasted_iota(jnp.int32, (8, 128), 1)
+
+
+def y_tile(gy_odd, w, ga, gb, t, n):
+    if t == 1:
+        return w[n]
+    return jnp.where((gy_odd == 1) == (t == 0), ga[n], gb[n])
 
 
 def edge_kernel(offsets, w, ga, gb, out_a, out_b):
     _, _, _, gy_odd, gz_odd = where_am_i(offsets)
     lane = lanes()
+    even = lax.rem(lane, 16) < 8
 
     def group(g, carry):
-        for out, up in ((out_a, 1 - gz_odd), (out_b, gz_odd)):
-            for t in range(3):
-                acc = jnp.zeros((8, 128), jnp.float32)
-                for k in range(16):
-                    n = g * 16 + k
-                    if t == 1:
-                        x = w[n]
-                    else:
-                        x = jnp.where((gy_odd == 1) == (t == 0), ga[n], gb[n])
-                    x = pltpu.roll(x, lax.rem(8 * k + 8 * up, 128), 1)
-                    acc = jnp.where((lane >= 8 * k) & (lane < 8 * k + 8), x, acc)
-                out[t * 12 + g] = acc
+        for t in range(3):
+            packed = []
+            for half in range(2):
+                acc = None
+                for k in range(8):
+                    x = y_tile(gy_odd, w, ga, gb, t, g * 16 + half * 8 + k)
+                    x = pltpu.roll(x, (8 + 16 * k) % 128, 1)
+                    acc = x if k == 0 else jnp.where(lane < 16 * k, acc, x)
+                packed.append(acc)
+            upper = jnp.where(even, packed[0], pltpu.roll(packed[1], 8, 1))
+            lower = jnp.where(even, pltpu.roll(packed[0], 120, 1), packed[1])
+            n = t * (N // 16) + g
+            out_a[n] = jnp.where(gz_odd == 1, lower, upper)
+            out_b[n] = jnp.where(gz_odd == 1, upper, lower)
         return carry
 
-    lax.fori_loop(0, 12, group, 0)
+    lax.fori_loop(0, N // 16, group, 0)
 
 
 def rows_diff(x):
@@ -356,27 +381,28 @@
     odd, _, _, gy_odd, gz_odd = where_am_i(offsets)
     lane = lanes()
 
+    even = lax.rem(lane, 16) < 8
+    edge = (lane < 8) | (lane >= 120)
+
     def group(g, carry):
         for t in range(3):
-            a, b = za[t * 12 + g], zb[t * 12 + g]
+            m = t * (N // 16) + g
+            a, b = za[m], zb[m]
             low = jnp.where(gz_odd == 1, a, b)
             high = jnp.where(gz_odd == 1, b, a)
+            packed = (
+                jnp.where(even, low, pltpu.roll(high, 8, 1)),
+                jnp.where(even, pltpu.roll(low, 120, 1), high),
+            )
             for k in range(16):
                 n = g * 16 + k
-                if t == 1:
-                    x = w[n]
-                else:
-                    x = jnp.where((gy_odd == 1) == (t == 0), ga[n], gb[n])
-                st[n, 8 * t : 8 * t + 8, 0:128] = x
-                h = pltpu.roll(high, (128 - 8 * k) % 128, 1)
-                l = pltpu.roll(low, (120 - 8 * k) % 128, 1)
-                st[n, 8 * t : 8 * t + 8, 128:256] = jnp.where(
-                    lane < 8, h, jnp.where(lane >= 120, l, 0.0)
-                )
+                st[n, 8 * t : 8 * t + 8, 0:128] = y_tile(gy_odd, w, ga, gb, t, n)
+                x = pltpu.roll(packed[k // 8], (120 - 16 * (k % 8)) % 128, 1)
+                st[n, 8 * t : 8 * t + 8, 128:256] = jnp.where(edge, x, 0.0)
         return carry
 
-    lax.fori_loop(0, 12, group, 0)
-    stress_at = lambda p, e: st[p * 12 + e]
+    lax.fori_loop(0, N // 16, group, 0)
+    stress_at = lambda p, e: st[entry_s(p, e)]
     velocity_step(
         range(1, 9),
         lambda p: st[CB + p - 1],
@@ -478,7 +504,7 @@
     recv = both_swaps(send_a, send_b, "grp")
     (win,) = call(window_kernel, "window", [(N, 8, 128)], (offsets, *held, *recv))
     ga, gb = both_swaps(win, win, "gy")
-    edges = call(edge_kernel, "edge", [(36, 8, 128)] * 2, (offsets, win, ga, gb))
+    edges = call(edge_kernel, "edge", [(3 * N // 16, 8, 128)] * 2, (offsets, win, ga, gb))
     za, zb = both_swaps(*edges, "gz")
     carried = [(72, 24, 256), (48, 24, 256), (18, 8, 128)]
     faces = lambda spec: [(face_tiles(spec), 8, 128)] * 2

time: 130 us -> 125 us (0.962)
  starting transfers between devices: 67.9 us -> 64.7 us
  waiting for transfers between devices: 44.3 us -> 42.6 us
    ppermute x5, starting transfers between devices: 31 us -> 27.5 us  [both_swaps(): first = lax.ppermute(value_a, axis, swaps(count, 0))]
    ppermute x5, waiting for transfers between devices: 42.5 us -> 41 us  [both_swaps(): second = lax.ppermute(value_b, axis, swaps(count, 1))]
where the time goes in v5:
time: 125 us
  starting transfers between devices  64.7 us (52%)
  waiting for transfers between devices  42.6 us (34%)
  Pallas kernels  15.9 us (13%)
    ppermute x5, waiting for transfers between devices, both_swaps(): second = lax.ppermute(value_b, axis, swaps(count, 1))  41 us
    ppermute x5, starting transfers between devices, both_swaps(): second = lax.ppermute(value_b, axis, swaps(count, 1))  37.1 us
    ppermute x5, starting transfers between devices, both_swaps(): first = lax.ppermute(value_a, axis, swaps(count, 0))  27.5 us
    pallas_call x6, Pallas kernels, call(): pl.pallas_call(kernel, out_shape=[jax.ShapeDtypeStruct(s, jnp.float32) fo...  15.9 us
  transfers between devices with their start and end apart: 10, of which 7 were waited for; matrix products, arithmetic and copies ran while one was open for 0% of the time, Pallas kernels for 0%

profile of v5, /device:TPU:37, one launch (start us, length us, event | category | flops | bytes accessed | tf_op | source)
XLA Modules:
  0.0 124.6 jit_solution(17695305205214760067)
XLA Ops:
  0.6 0.6 copy-done
  1.3 1.7 %pack.1 = (f32[67,8,128]{2,1,0:T(8,128)S(1)}, f32[67,8,128]{2,1,0:T(8,128)S(1)}, f32[3,4,8,128]{3,2,1,0:T(8,128)S(1)}, f32[6,4,8,128]{3,2,1,0:T(8,128)S(1)}, f32...) custom-call(s32[48]{0:T(128)S(1)} %copy-done, ...), custom_call_target="tpu_custom_call" | custom-call | tf_op jit(solution)/shard_map/pack/pallas_call | solution.py:481
  3.0 4.0 %collective-permute-start = (f32[67,8,128]{2,1,0:T(8,128)S(1)}, f32[67,8,128]{2,1,0:T(8,128)S(1)}, u32[]{:S(2)}, u32[]{:S(2)}) collective-permute-start(f32[67,8,128]{2,1,0:T(8,128)S(1)} %get-tuple-element.29), channel_id=1, source_target_pairs={{0,16},{16,0},{32,48},{48,32},{64,80},{80,64},{96,112},{112,96},{1... | collective-permute-start | bytes 823304 | tf_op jit(solution)/shard_map/ppermute | solution.py:53
  7.0 10.3 %collective-permute-start.1 = (f32[67,8,128]{2,1,0:T(8,128)S(1)}, f32[67,8,128]{2,1,0:T(8,128)S(1)}, u32[]{:S(2)}, u32[]{:S(2)}) collective-permute-start(f32[67,8,128]{2,1,0:T(8,128)S(1)} %get-tuple-element.30), channel_id=1, source_target_pairs={{16,32},{32,16},{48,64},{64,48},{80,96},{96,80},{112,128},{128,112... | collective-permute-start | bytes 823304 | tf_op jit(solution)/shard_map/ppermute | solution.py:52
  17.3 10.2 %collective-permute-done.1.rb = f32[67,8,128]{2,1,0:T(8,128)S(1)} collective-permute-done((f32[67,8,128]{2,1,0:T(8,128)S(1)}, f32[67,8,128]{2,1,0:T(8,128)S(1)}, u32[]{:S(2)}, u32[]{:S(2)}) %collective-permute-start.1) | collective-permute-done | bytes 274464 | tf_op jit(solution)/shard_map/ppermute | solution.py:52
  27.5 0.6 window.1.w
  28.1 11.8 %collective-permute-start.3 = (f32[176,8,128]{2,1,0:T(8,128)S(1)}, f32[176,8,128]{2,1,0:T(8,128)S(1)}, u32[]{:S(2)}, u32[]{:S(2)}) collective-permute-start(f32[176,8,128]{2,1,0:T(8,128)S(1)} %window.1.w), channel_id=1, source_target_pairs={{4,8},{8,4},{5,9},{9,5},{6,10},{10,6},{7,11},{11,7},{20,24},{24,20... | collective-permute-start | bytes 2162696 | tf_op jit(solution)/shard_map/ppermute | solution.py:52
  40.0 1.9 %collective-permute-start.2 = (f32[176,8,128]{2,1,0:T(8,128)S(1)}, f32[176,8,128]{2,1,0:T(8,128)S(1)}, u32[]{:S(2)}, u32[]{:S(2)}) collective-permute-start(f32[176,8,128]{2,1,0:T(8,128)S(1)} %window.1.w), channel_id=1, source_target_pairs={{0,4},{4,0},{8,12},{12,8},{1,5},{5,1},{9,13},{13,9},{2,6},{6,2},{1... | collective-permute-start | bytes 2162696 | tf_op jit(solution)/shard_map/ppermute | solution.py:53
  41.9 10.0 %collective-permute-done.3.gb = f32[176,8,128]{2,1,0:T(8,128)S(1)} collective-permute-done((f32[176,8,128]{2,1,0:T(8,128)S(1)}, f32[176,8,128]{2,1,0:T(8,128)S(1)}, u32[]{:S(2)}, u32[]{:S(2)}) %collective-permute-start.3) | collective-permute-done | bytes 720928 | tf_op jit(solution)/shard_map/ppermute | solution.py:52
  51.9 2.7 %edge.1 = (f32[33,8,128]{2,1,0:T(8,128)S(1)}, f32[33,8,128]{2,1,0:T(8,128)S(1)}) custom-call(s32[48]{0:T(128)S(1)} %copy-done, f32[176,8,128]{2,1,0:T(8,128)S(1)} %window.1.w, f32[176,8,128]{2,1,0:T(8,128)S(1)} %collective-permute-done.2.ga, f32[176,8,128]{2,1,0:T(8,128)S(1)} %collective-permute-done.3.gb), custom_call_target="tpu_custom_call" | custom-call | tf_op jit(solution)/shard_map/edge/pallas_call | solution.py:481
  54.6 2.8 %collective-permute-start.4 = (f32[33,8,128]{2,1,0:T(8,128)S(1)}, f32[33,8,128]{2,1,0:T(8,128)S(1)}, u32[]{:S(2)}, u32[]{:S(2)}) collective-permute-start(f32[33,8,128]{2,1,0:T(8,128)S(1)} %get-tuple-element.31), channel_id=1, source_target_pairs={{0,1},{1,0},{2,3},{3,2},{4,5},{5,4},{6,7},{7,6},{8,9},{9,8},{10,11... | collective-permute-start | bytes 405512 | tf_op jit(solution)/shard_map/ppermute | solution.py:53
  57.4 1.9 %collective-permute-start.5 = (f32[33,8,128]{2,1,0:T(8,128)S(1)}, f32[33,8,128]{2,1,0:T(8,128)S(1)}, u32[]{:S(2)}, u32[]{:S(2)}) collective-permute-start(f32[33,8,128]{2,1,0:T(8,128)S(1)} %get-tuple-element.32), channel_id=1, source_target_pairs={{1,2},{2,1},{5,6},{6,5},{9,10},{10,9},{13,14},{14,13},{17,18},{18,... | collective-permute-start | bytes 405512 | tf_op jit(solution)/shard_map/ppermute | solution.py:52
  59.3 1.0 collective-permute-done.4.za
  60.3 2.8 %collective-permute-done.5.zb = f32[33,8,128]{2,1,0:T(8,128)S(1)} collective-permute-done((f32[33,8,128]{2,1,0:T(8,128)S(1)}, f32[33,8,128]{2,1,0:T(8,128)S(1)}, u32[]{:S(2)}, u32[]{:S(2)}) %collective-permute-start.5) | collective-permute-done | bytes 135200 | tf_op jit(solution)/shard_map/ppermute | solution.py:52
  63.2 4.3 %first.1 = (f32[176,24,256]{2,1,0:T(8,128)S(1)}, f32[72,24,256]{2,1,0:T(8,128)S(1)}, f32[48,24,256]{2,1,0:T(8,128)S(1)}, f32[18,8,128]{2,1,0:T(8,128)S(1)}, f32[...) custom-call(s32[48]{0:T(128)S(1)} %copy-done, f32[176,8,128]{2,1,0:T(8,128)S(1)} %window.1.w, ...), custom_call_target="tpu_custom_call" | custom-call | tf_op jit(solution)/shard_map/first/pallas_call | solution.py:481
  67.5 16.8 %collective-permute-start.6 = (f32[131,8,128]{2,1,0:T(8,128)S(1)}, f32[131,8,128]{2,1,0:T(8,128)S(1)}, u32[]{:S(2)}, u32[]{:S(2)}) collective-permute-start(f32[131,8,128]{2,1,0:T(8,128)S(1)} %get-tuple-element.37), channel_id=1, source_target_pairs={{0,16},{16,0},{32,48},{48,32},{64,80},{80,64},{96,112},{112,96},{1... | collective-permute-start | bytes 1609736 | tf_op jit(solution)/shard_map/ppermute | solution.py:53
  84.3 6.7 %collective-permute-start.7 = (f32[131,8,128]{2,1,0:T(8,128)S(1)}, f32[131,8,128]{2,1,0:T(8,128)S(1)}, u32[]{:S(2)}, u32[]{:S(2)}) collective-permute-start(f32[131,8,128]{2,1,0:T(8,128)S(1)} %get-tuple-element.38), channel_id=1, source_target_pairs={{16,32},{32,16},{48,64},{64,48},{80,96},{96,80},{112,128},{128,112... | collective-permute-start | bytes 1609736 | tf_op jit(solution)/shard_map/ppermute | solution.py:52
  91.0 0.6 collective-permute-done.6.ra
  91.6 12.1 %collective-permute-done.7.rb = f32[131,8,128]{2,1,0:T(8,128)S(1)} collective-permute-done((f32[131,8,128]{2,1,0:T(8,128)S(1)}, f32[131,8,128]{2,1,0:T(8,128)S(1)}, u32[]{:S(2)}, u32[]{:S(2)}) %collective-permute-start.7) | collective-permute-done | bytes 536608 | tf_op jit(solution)/shard_map/ppermute | solution.py:52
  103.7 4.7 %middle.1 = (f32[72,24,256]{2,1,0:T(8,128)S(1)}, f32[48,24,256]{2,1,0:T(8,128)S(1)}, f32[18,8,128]{2,1,0:T(8,128)S(1)}, f32[24,8,128]{2,1,0:T(8,128)S(1)}, f32[24,8,128]{2,1,0:T(8,128)S(1)}) custom-call(s32[48]{0:T(128)S(1)} %copy-done, f32[176,24,256]{2,1,0:T(8,128)S(1)} %get-tuple-element.33.st, f32[72,24,256]{2,1,0:T(8,128)S(1)} %get-tuple-element.34.s_old, ...), custom_call_target="tpu_custom_call" | custom-call | tf_op jit(solution)/shard_map/middle/pallas_call | solution.py:481
  108.4 1.9 %collective-permute-start.8 = (f32[24,8,128]{2,1,0:T(8,128)S(1)}, f32[24,8,128]{2,1,0:T(8,128)S(1)}, u32[]{:S(2)}, u32[]{:S(2)}) collective-permute-start(f32[24,8,128]{2,1,0:T(8,128)S(1)} %get-tuple-element.42), channel_id=1, source_target_pairs={{0,16},{16,0},{32,48},{48,32},{64,80},{80,64},{96,112},{112,96},{1... | collective-permute-start | bytes 294920 | tf_op jit(solution)/shard_map/ppermute | solution.py:53
  110.3 6.4 %collective-permute-start.9 = (f32[24,8,128]{2,1,0:T(8,128)S(1)}, f32[24,8,128]{2,1,0:T(8,128)S(1)}, u32[]{:S(2)}, u32[]{:S(2)}) collective-permute-start(f32[24,8,128]{2,1,0:T(8,128)S(1)} %get-tuple-element.43), channel_id=1, source_target_pairs={{16,32},{32,16},{48,64},{64,48},{80,96},{96,80},{112,128},{128,112... | collective-permute-start | bytes 294920 | tf_op jit(solution)/shard_map/ppermute | solution.py:52
  116.8 5.8 %collective-permute-done.9.rb = f32[24,8,128]{2,1,0:T(8,128)S(1)} collective-permute-done((f32[24,8,128]{2,1,0:T(8,128)S(1)}, f32[24,8,128]{2,1,0:T(8,128)S(1)}, u32[]{:S(2)}, u32[]{:S(2)}) %collective-permute-start.9) | collective-permute-done | bytes 98336 | tf_op jit(solution)/shard_map/ppermute | solution.py:52
  122.6 2.0 %last.1 = (f32[6,8,128]{2,1,0:T(8,128)}, f32[2,6,8,128]{3,2,1,0:T(8,128)}) custom-call(s32[48]{0:T(128)S(1)} %copy-done, f32[176,24,256]{2,1,0:T(8,128)S(1)} %get-tuple-element.33.st, f32[72,24,256]{2,1,0:T(8,128)S(1)} %get-tuple-element.39.s_old, f32[48,24,256]{2,1,0:T(8,128)S(1)} %get-tuple-element.40.v_old, f32[18,8,128]{2,1,0:T(8,128)S(1)} %get-tuple-element.41.kern_old, ...), custom_call_target="tpu_custom_call" | custom-call | tf_op jit(solution)/shard_map/last/pallas_call | solution.py:481
  (4 shorter events, 0.0 us)
Async XLA Ops:
  0.6 0.7 copy-start
  3.0 14.3 %collective-permute-start = (f32[67,8,128]{2,1,0:T(8,128)S(1)}, f32[67,8,128]{2,1,0:T(8,128)S(1)}, u32[]{:S(2)}, u32[]{:S(2)}) collective-permute-start(f32[67,8,128]{2,1,0:T(8,128)S(1)} %get-tuple-element.29), channel_id=1, source_target_pairs={{0,16},{16,0},{32,48},{48,32},{64,80},{80,64},{96,112},{112,96},{1... | collective-permute-start | bytes 823304 | tf_op jit(solution)/shard_map/ppermute | solution.py:53
  7.0 20.5 %collective-permute-start.1 = (f32[67,8,128]{2,1,0:T(8,128)S(1)}, f32[67,8,128]{2,1,0:T(8,128)S(1)}, u32[]{:S(2)}, u32[]{:S(2)}) collective-permute-start(f32[67,8,128]{2,1,0:T(8,128)S(1)} %get-tuple-element.30), channel_id=1, source_target_pairs={{16,32},{32,16},{48,64},{64,48},{80,96},{96,80},{112,128},{128,112... | collective-permute-start | bytes 823304 | tf_op jit(solution)/shard_map/ppermute | solution.py:52
  28.1 23.8 %collective-permute-start.3 = (f32[176,8,128]{2,1,0:T(8,128)S(1)}, f32[176,8,128]{2,1,0:T(8,128)S(1)}, u32[]{:S(2)}, u32[]{:S(2)}) collective-permute-start(f32[176,8,128]{2,1,0:T(8,128)S(1)} %window.1.w), channel_id=1, source_target_pairs={{4,8},{8,4},{5,9},{9,5},{6,10},{10,6},{7,11},{11,7},{20,24},{24,20... | collective-permute-start | bytes 2162696 | tf_op jit(solution)/shard_map/ppermute | solution.py:52
  40.0 11.9 %collective-permute-start.2 = (f32[176,8,128]{2,1,0:T(8,128)S(1)}, f32[176,8,128]{2,1,0:T(8,128)S(1)}, u32[]{:S(2)}, u32[]{:S(2)}) collective-permute-start(f32[176,8,128]{2,1,0:T(8,128)S(1)} %window.1.w), channel_id=1, source_target_pairs={{0,4},{4,0},{8,12},{12,8},{1,5},{5,1},{9,13},{13,9},{2,6},{6,2},{1... | collective-permute-start | bytes 2162696 | tf_op jit(solution)/shard_map/ppermute | solution.py:53
  54.6 5.8 %collective-permute-start.4 = (f32[33,8,128]{2,1,0:T(8,128)S(1)}, f32[33,8,128]{2,1,0:T(8,128)S(1)}, u32[]{:S(2)}, u32[]{:S(2)}) collective-permute-start(f32[33,8,128]{2,1,0:T(8,128)S(1)} %get-tuple-element.31), channel_id=1, source_target_pairs={{0,1},{1,0},{2,3},{3,2},{4,5},{5,4},{6,7},{7,6},{8,9},{9,8},{10,11... | collective-permute-start | bytes 405512 | tf_op jit(solution)/shard_map/ppermute | solution.py:53
  57.4 5.8 %collective-permute-start.5 = (f32[33,8,128]{2,1,0:T(8,128)S(1)}, f32[33,8,128]{2,1,0:T(8,128)S(1)}, u32[]{:S(2)}, u32[]{:S(2)}) collective-permute-start(f32[33,8,128]{2,1,0:T(8,128)S(1)} %get-tuple-element.32), channel_id=1, source_target_pairs={{1,2},{2,1},{5,6},{6,5},{9,10},{10,9},{13,14},{14,13},{17,18},{18,... | collective-permute-start | bytes 405512 | tf_op jit(solution)/shard_map/ppermute | solution.py:52
  67.5 24.2 %collective-permute-start.6 = (f32[131,8,128]{2,1,0:T(8,128)S(1)}, f32[131,8,128]{2,1,0:T(8,128)S(1)}, u32[]{:S(2)}, u32[]{:S(2)}) collective-permute-start(f32[131,8,128]{2,1,0:T(8,128)S(1)} %get-tuple-element.37), channel_id=1, source_target_pairs={{0,16},{16,0},{32,48},{48,32},{64,80},{80,64},{96,112},{112,96},{1... | collective-permute-start | bytes 1609736 | tf_op jit(solution)/shard_map/ppermute | solution.py:53
  84.3 19.4 %collective-permute-start.7 = (f32[131,8,128]{2,1,0:T(8,128)S(1)}, f32[131,8,128]{2,1,0:T(8,128)S(1)}, u32[]{:S(2)}, u32[]{:S(2)}) collective-permute-start(f32[131,8,128]{2,1,0:T(8,128)S(1)} %get-tuple-element.38), channel_id=1, source_target_pairs={{16,32},{32,16},{48,64},{64,48},{80,96},{96,80},{112,128},{128,112... | collective-permute-start | bytes 1609736 | tf_op jit(solution)/shard_map/ppermute | solution.py:52
  108.4 8.4 %collective-permute-start.8 = (f32[24,8,128]{2,1,0:T(8,128)S(1)}, f32[24,8,128]{2,1,0:T(8,128)S(1)}, u32[]{:S(2)}, u32[]{:S(2)}) collective-permute-start(f32[24,8,128]{2,1,0:T(8,128)S(1)} %get-tuple-element.42), channel_id=1, source_target_pairs={{0,16},{16,0},{32,48},{48,32},{64,80},{80,64},{96,112},{112,96},{1... | collective-permute-start | bytes 294920 | tf_op jit(solution)/shard_map/ppermute | solution.py:53
  110.3 12.3 %collective-permute-start.9 = (f32[24,8,128]{2,1,0:T(8,128)S(1)}, f32[24,8,128]{2,1,0:T(8,128)S(1)}, u32[]{:S(2)}, u32[]{:S(2)}) collective-permute-start(f32[24,8,128]{2,1,0:T(8,128)S(1)} %get-tuple-element.43), channel_id=1, source_target_pairs={{16,32},{32,16},{48,64},{64,48},{80,96},{96,80},{112,128},{128,112... | collective-permute-start | bytes 294920 | tf_op jit(solution)/shard_map/ppermute | solution.py:52

commit v6 on v5

--- a/solution.py
+++ b/solution.py
@@ -4,6 +4,7 @@
 from jax.experimental import pallas as pl
 from jax.experimental.pallas import tpu as pltpu
 from jax.sharding import PartitionSpec as P
+
 
 H = 0.15
 PAIRS = ((0, 5, 4), (5, 1, 3), (4, 3, 2))
@@ -176,7 +177,7 @@
     lane = lanes()
     even = lax.rem(lane, 16) < 8
 
-    def group(g, carry):
+    def group(g):
         for t in range(3):
             packed = []
             for half in range(2):
@@ -191,9 +192,9 @@
             n = t * (N // 16) + g
             out_a[n] = jnp.where(gz_odd == 1, lower, upper)
             out_b[n] = jnp.where(gz_odd == 1, upper, lower)
-        return carry
-
-    lax.fori_loop(0, N // 16, group, 0)
+
+    for g in range(N // 16):
+        group(g)
 
 
 def rows_diff(x):
@@ -384,7 +385,7 @@
     even = lax.rem(lane, 16) < 8
     edge = (lane < 8) | (lane >= 120)
 
-    def group(g, carry):
+    def group(g):
         for t in range(3):
             m = t * (N // 16) + g
             a, b = za[m], zb[m]
@@ -399,9 +400,9 @@
                 st[n, 8 * t : 8 * t + 8, 0:128] = y_tile(gy_odd, w, ga, gb, t, n)
                 x = pltpu.roll(packed[k // 8], (120 - 16 * (k % 8)) % 128, 1)
                 st[n, 8 * t : 8 * t + 8, 128:256] = jnp.where(edge, x, 0.0)
-        return carry
-
-    lax.fori_loop(0, N // 16, group, 0)
+
+    for g in range(N // 16):
+        group(g)
     stress_at = lambda p, e: st[entry_s(p, e)]
     velocity_step(
         range(1, 9),
@@ -476,7 +477,7 @@
         modu[1, r] = jnp.where(live, kern[12 + row], 0.0)
 
 
-def call(kernel, name, outs, args, scratch=(), space=pltpu.VMEM):
+def call(kernel, outs, args, scratch=(), space=pltpu.VMEM):
     vmem = pl.BlockSpec(memory_space=pltpu.VMEM)
     return pl.pallas_call(
         kernel,
@@ -486,39 +487,35 @@
         out_specs=[vmem] * len(outs),
         scratch_shapes=[pltpu.VMEM(s, jnp.float32) if isinstance(s, tuple) else s for s in scratch],
         compiler_params=pltpu.CompilerParams(vmem_limit_bytes=VMEM_LIMIT),
-        name=name,
     )(*args)
 
 
-def shards(fwd_velocity, fwd_stress, density, lame, adj_velocity, adj_stress, offsets):
+def sensitivity(fwd_velocity, fwd_stress, density, lame, adj_velocity, adj_stress, offsets):
     raw = (fwd_velocity, fwd_stress, density, lame, adj_velocity, adj_stress)
     raw = [pltpu.with_memory_space_constraint(a, pltpu.HBM) for a in raw]
     send_a, send_b, *held = call(
         pack_kernel,
-        "pack",
         [(NP1, 8, 128)] * 2 + [a.shape for a in raw],
         (offsets, *raw),
         [pltpu.SemaphoreType.DMA((6,))],
         pltpu.HBM,
     )
     recv = both_swaps(send_a, send_b, "grp")
-    (win,) = call(window_kernel, "window", [(N, 8, 128)], (offsets, *held, *recv))
+    (win,) = call(window_kernel, [(N, 8, 128)], (offsets, *held, *recv))
     ga, gb = both_swaps(win, win, "gy")
-    edges = call(edge_kernel, "edge", [(3 * N // 16, 8, 128)] * 2, (offsets, win, ga, gb))
+    edges = call(edge_kernel, [(3 * N // 16, 8, 128)] * 2, (offsets, win, ga, gb))
     za, zb = both_swaps(*edges, "gz")
     carried = [(72, 24, 256), (48, 24, 256), (18, 8, 128)]
     faces = lambda spec: [(face_tiles(spec), 8, 128)] * 2
     halos = lambda spec: (2 * face_places(spec)[1], 24, 256)
     state, *moving, face_a, face_b = call(
         first_kernel,
-        "first",
         [(N, 24, 256)] + carried + faces(MID),
         (offsets, win, ga, gb, za, zb),
     )
     recv = both_swaps(face_a, face_b, "grp")
     *moving, face_a, face_b = call(
         middle_kernel,
-        "middle",
         carried + faces(LAST),
         (offsets, state, *moving, *recv),
         [halos(MID), (120, 24, 256), (72, 24, 256)],
@@ -526,7 +523,6 @@
     recv = both_swaps(face_a, face_b, "grp")
     dens, modu = call(
         last_kernel,
-        "last",
         [(6, 8, 128), (2, 6, 8, 128)],
         (offsets, state, *moving, *recv),
         [halos(LAST), (48, 24, 256), (18, 8, 128)],
@@ -536,7 +532,7 @@
 
 def solution(mesh):
     return jax.shard_map(
-        shards,
+        sensitivity,
         mesh=mesh,
         in_specs=(
             P(None, "grp", "gy", "gz"),

time: 125 us -> 126 us (level)
  the two profiles are of different devices: /device:TPU:37 before, /device:TPU:61 now
where the time goes in v6:
time: 126 us
  starting transfers between devices  65.7 us (52%)
  waiting for transfers between devices  41.7 us (33%)
  Pallas kernels  16.8 us (13%)
    ppermute x5, starting transfers between devices, both_swaps(): second = lax.ppermute(value_b, axis, swaps(count, 1))  46.8 us
    ppermute x5, waiting for transfers between devices, both_swaps(): second = lax.ppermute(value_b, axis, swaps(count, 1))  40.7 us
    ppermute x5, starting transfers between devices, both_swaps(): first = lax.ppermute(value_a, axis, swaps(count, 0))  18.9 us
    pallas_call x6, Pallas kernels, call(): pl.pallas_call(kernel, out_shape=[jax.ShapeDtypeStruct(s, jnp.float32) fo...  16.8 us
  transfers between devices with their start and end apart: 10, of which 6 were waited for; matrix products, arithmetic and copies ran while one was open for 0% of the time, Pallas kernels for 0%

profile of v6, /device:TPU:61, one launch (start us, length us, event | category | flops | bytes accessed | tf_op | source)
XLA Modules:
  0.0 125.6 jit_solution(130602855907478197)
XLA Ops:
  0.6 0.6 copy-done
  1.3 1.7 %shard_map.86 = (f32[67,8,128]{2,1,0:T(8,128)S(1)}, f32[67,8,128]{2,1,0:T(8,128)S(1)}, f32[3,4,8,128]{3,2,1,0:T(8,128)S(1)}, f32[6,4,8,128]{3,2,1,0:T(8,128)S(1)...) custom-call(s32[48]{0:T(128)S(1)} %copy-done, ...), custom_call_target="tpu_custom_call" | custom-call | tf_op jit(solution)/shard_map/pallas_call | solution.py:482
  3.0 4.0 %collective-permute-start = (f32[67,8,128]{2,1,0:T(8,128)S(1)}, f32[67,8,128]{2,1,0:T(8,128)S(1)}, u32[]{:S(2)}, u32[]{:S(2)}) collective-permute-start(f32[67,8,128]{2,1,0:T(8,128)S(1)} %get-tuple-element.29), channel_id=1, source_target_pairs={{0,16},{16,0},{32,48},{48,32},{64,80},{80,64},{96,112},{112,96},{1... | collective-permute-start | bytes 823304 | tf_op jit(solution)/shard_map/ppermute | solution.py:54
  7.0 11.1 %collective-permute-start.1 = (f32[67,8,128]{2,1,0:T(8,128)S(1)}, f32[67,8,128]{2,1,0:T(8,128)S(1)}, u32[]{:S(2)}, u32[]{:S(2)}) collective-permute-start(f32[67,8,128]{2,1,0:T(8,128)S(1)} %get-tuple-element.30), channel_id=1, source_target_pairs={{16,32},{32,16},{48,64},{64,48},{80,96},{96,80},{112,128},{128,112... | collective-permute-start | bytes 823304 | tf_op jit(solution)/shard_map/ppermute | solution.py:53
  18.2 10.2 %collective-permute-done.1.rb = f32[67,8,128]{2,1,0:T(8,128)S(1)} collective-permute-done((f32[67,8,128]{2,1,0:T(8,128)S(1)}, f32[67,8,128]{2,1,0:T(8,128)S(1)}, u32[]{:S(2)}, u32[]{:S(2)}) %collective-permute-start.1) | collective-permute-done | bytes 274464 | tf_op jit(solution)/shard_map/ppermute | solution.py:53
  28.4 0.6 shard_map.87.w
  29.0 11.2 %collective-permute-start.3 = (f32[176,8,128]{2,1,0:T(8,128)S(1)}, f32[176,8,128]{2,1,0:T(8,128)S(1)}, u32[]{:S(2)}, u32[]{:S(2)}) collective-permute-start(f32[176,8,128]{2,1,0:T(8,128)S(1)} %shard_map.87.w), channel_id=1, source_target_pairs={{4,8},{8,4},{5,9},{9,5},{6,10},{10,6},{7,11},{11,7},{20,24},{24,20... | collective-permute-start | bytes 2162696 | tf_op jit(solution)/shard_map/ppermute | solution.py:53
  40.3 1.9 %collective-permute-start.2 = (f32[176,8,128]{2,1,0:T(8,128)S(1)}, f32[176,8,128]{2,1,0:T(8,128)S(1)}, u32[]{:S(2)}, u32[]{:S(2)}) collective-permute-start(f32[176,8,128]{2,1,0:T(8,128)S(1)} %shard_map.87.w), channel_id=1, source_target_pairs={{0,4},{4,0},{8,12},{12,8},{1,5},{5,1},{9,13},{13,9},{2,6},{6,2},{1... | collective-permute-start | bytes 2162696 | tf_op jit(solution)/shard_map/ppermute | solution.py:54
  42.2 10.3 %collective-permute-done.3.gb = f32[176,8,128]{2,1,0:T(8,128)S(1)} collective-permute-done((f32[176,8,128]{2,1,0:T(8,128)S(1)}, f32[176,8,128]{2,1,0:T(8,128)S(1)}, u32[]{:S(2)}, u32[]{:S(2)}) %collective-permute-start.3) | collective-permute-done | bytes 720928 | tf_op jit(solution)/shard_map/ppermute | solution.py:53
  52.5 0.0 collective-permute-done.2.ga
  52.5 3.0 %shard_map.88 = (f32[33,8,128]{2,1,0:T(8,128)S(1)}, f32[33,8,128]{2,1,0:T(8,128)S(1)}) custom-call(s32[48]{0:T(128)S(1)} %copy-done, f32[176,8,128]{2,1,0:T(8,128)S(1)} %shard_map.87.w, f32[176,8,128]{2,1,0:T(8,128)S(1)} %collective-permute-done.2.ga, f32[176,8,128]{2,1,0:T(8,128)S(1)} %collective-permute-done.3.gb), custom_call_target="tpu_custom_call" | custom-call | tf_op jit(solution)/shard_map/pallas_call | solution.py:482
  55.5 2.8 %collective-permute-start.4 = (f32[33,8,128]{2,1,0:T(8,128)S(1)}, f32[33,8,128]{2,1,0:T(8,128)S(1)}, u32[]{:S(2)}, u32[]{:S(2)}) collective-permute-start(f32[33,8,128]{2,1,0:T(8,128)S(1)} %get-tuple-element.31), channel_id=1, source_target_pairs={{0,1},{1,0},{2,3},{3,2},{4,5},{5,4},{6,7},{7,6},{8,9},{9,8},{10,11... | collective-permute-start | bytes 405512 | tf_op jit(solution)/shard_map/ppermute | solution.py:54
  58.3 1.9 %collective-permute-start.5 = (f32[33,8,128]{2,1,0:T(8,128)S(1)}, f32[33,8,128]{2,1,0:T(8,128)S(1)}, u32[]{:S(2)}, u32[]{:S(2)}) collective-permute-start(f32[33,8,128]{2,1,0:T(8,128)S(1)} %get-tuple-element.32), channel_id=1, source_target_pairs={{1,2},{2,1},{5,6},{6,5},{9,10},{10,9},{13,14},{14,13},{17,18},{18,... | collective-permute-start | bytes 405512 | tf_op jit(solution)/shard_map/ppermute | solution.py:53
  60.2 1.0 collective-permute-done.4.za
  61.2 2.8 %collective-permute-done.5.zb = f32[33,8,128]{2,1,0:T(8,128)S(1)} collective-permute-done((f32[33,8,128]{2,1,0:T(8,128)S(1)}, f32[33,8,128]{2,1,0:T(8,128)S(1)}, u32[]{:S(2)}, u32[]{:S(2)}) %collective-permute-start.5) | collective-permute-done | bytes 135200 | tf_op jit(solution)/shard_map/ppermute | solution.py:53
  64.1 4.8 %shard_map.89 = (f32[176,24,256]{2,1,0:T(8,128)S(1)}, f32[72,24,256]{2,1,0:T(8,128)S(1)}, f32[48,24,256]{2,1,0:T(8,128)S(1)}, f32[18,8,128]{2,1,0:T(8,128)S(1)},...) custom-call(s32[48]{0:T(128)S(1)} %copy-done, f32[176,8,128]{2,1,0:T(8,128)S(1)} %shard_map.87.w, ...), custom_call_target="tpu_custom_call" | custom-call | tf_op jit(solution)/shard_map/pallas_call | solution.py:482
  68.9 8.3 %collective-permute-start.6 = (f32[131,8,128]{2,1,0:T(8,128)S(1)}, f32[131,8,128]{2,1,0:T(8,128)S(1)}, u32[]{:S(2)}, u32[]{:S(2)}) collective-permute-start(f32[131,8,128]{2,1,0:T(8,128)S(1)} %get-tuple-element.37), channel_id=1, source_target_pairs={{0,16},{16,0},{32,48},{48,32},{64,80},{80,64},{96,112},{112,96},{1... | collective-permute-start | bytes 1609736 | tf_op jit(solution)/shard_map/ppermute | solution.py:54
  77.1 16.1 %collective-permute-start.7 = (f32[131,8,128]{2,1,0:T(8,128)S(1)}, f32[131,8,128]{2,1,0:T(8,128)S(1)}, u32[]{:S(2)}, u32[]{:S(2)}) collective-permute-start(f32[131,8,128]{2,1,0:T(8,128)S(1)} %get-tuple-element.38), channel_id=1, source_target_pairs={{16,32},{32,16},{48,64},{64,48},{80,96},{96,80},{112,128},{128,112... | collective-permute-start | bytes 1609736 | tf_op jit(solution)/shard_map/ppermute | solution.py:53
  93.3 12.7 %collective-permute-done.7.rb = f32[131,8,128]{2,1,0:T(8,128)S(1)} collective-permute-done((f32[131,8,128]{2,1,0:T(8,128)S(1)}, f32[131,8,128]{2,1,0:T(8,128)S(1)}, u32[]{:S(2)}, u32[]{:S(2)}) %collective-permute-start.7) | collective-permute-done | bytes 536608 | tf_op jit(solution)/shard_map/ppermute | solution.py:53
  106.0 4.7 %shard_map.90 = (f32[72,24,256]{2,1,0:T(8,128)S(1)}, f32[48,24,256]{2,1,0:T(8,128)S(1)}, f32[18,8,128]{2,1,0:T(8,128)S(1)}, f32[24,8,128]{2,1,0:T(8,128)S(1)}, f32[24,8,128]{2,1,0:T(8,128)S(1)}) custom-call(s32[48]{0:T(128)S(1)} %copy-done, f32[176,24,256]{2,1,0:T(8,128)S(1)} %get-tuple-element.33.st, f32[72,24,256]{2,1,0:T(8,128)S(1)} %get-tuple-element.34.s_old, ...), custom_call_target="tpu_custom_call" | custom-call | tf_op jit(solution)/shard_map/pallas_call | solution.py:482
  110.6 1.9 %collective-permute-start.8 = (f32[24,8,128]{2,1,0:T(8,128)S(1)}, f32[24,8,128]{2,1,0:T(8,128)S(1)}, u32[]{:S(2)}, u32[]{:S(2)}) collective-permute-start(f32[24,8,128]{2,1,0:T(8,128)S(1)} %get-tuple-element.42), channel_id=1, source_target_pairs={{0,16},{16,0},{32,48},{48,32},{64,80},{80,64},{96,112},{112,96},{1... | collective-permute-start | bytes 294920 | tf_op jit(solution)/shard_map/ppermute | solution.py:54
  112.6 6.4 %collective-permute-start.9 = (f32[24,8,128]{2,1,0:T(8,128)S(1)}, f32[24,8,128]{2,1,0:T(8,128)S(1)}, u32[]{:S(2)}, u32[]{:S(2)}) collective-permute-start(f32[24,8,128]{2,1,0:T(8,128)S(1)} %get-tuple-element.43), channel_id=1, source_target_pairs={{16,32},{32,16},{48,64},{64,48},{80,96},{96,80},{112,128},{128,112... | collective-permute-start | bytes 294920 | tf_op jit(solution)/shard_map/ppermute | solution.py:53
  119.0 4.6 %collective-permute-done.9.rb = f32[24,8,128]{2,1,0:T(8,128)S(1)} collective-permute-done((f32[24,8,128]{2,1,0:T(8,128)S(1)}, f32[24,8,128]{2,1,0:T(8,128)S(1)}, u32[]{:S(2)}, u32[]{:S(2)}) %collective-permute-start.9) | collective-permute-done | bytes 98336 | tf_op jit(solution)/shard_map/ppermute | solution.py:53
  123.6 2.0 %shard_map.91 = (f32[6,8,128]{2,1,0:T(8,128)}, f32[2,6,8,128]{3,2,1,0:T(8,128)}) custom-call(s32[48]{0:T(128)S(1)} %copy-done, f32[176,24,256]{2,1,0:T(8,128)S(1)} %get-tuple-element.33.st, f32[72,24,256]{2,1,0:T(8,128)S(1)} %get-tuple-element.39.s_old, f32[48,24,256]{2,1,0:T(8,128)S(1)} %get-tuple-element.40.v_old, ...), custom_call_target="tpu_custom_call" | custom-call | tf_op jit(solution)/shard_map/pallas_call | solution.py:482
  (4 shorter events, 0.0 us)
Async XLA Ops:
  0.6 0.7 copy-start
  3.0 15.2 %collective-permute-start = (f32[67,8,128]{2,1,0:T(8,128)S(1)}, f32[67,8,128]{2,1,0:T(8,128)S(1)}, u32[]{:S(2)}, u32[]{:S(2)}) collective-permute-start(f32[67,8,128]{2,1,0:T(8,128)S(1)} %get-tuple-element.29), channel_id=1, source_target_pairs={{0,16},{16,0},{32,48},{48,32},{64,80},{80,64},{96,112},{112,96},{1... | collective-permute-start | bytes 823304 | tf_op jit(solution)/shard_map/ppermute | solution.py:54
  7.0 21.4 %collective-permute-start.1 = (f32[67,8,128]{2,1,0:T(8,128)S(1)}, f32[67,8,128]{2,1,0:T(8,128)S(1)}, u32[]{:S(2)}, u32[]{:S(2)}) collective-permute-start(f32[67,8,128]{2,1,0:T(8,128)S(1)} %get-tuple-element.30), channel_id=1, source_target_pairs={{16,32},{32,16},{48,64},{64,48},{80,96},{96,80},{112,128},{128,112... | collective-permute-start | bytes 823304 | tf_op jit(solution)/shard_map/ppermute | solution.py:53
  29.0 23.4 %collective-permute-start.3 = (f32[176,8,128]{2,1,0:T(8,128)S(1)}, f32[176,8,128]{2,1,0:T(8,128)S(1)}, u32[]{:S(2)}, u32[]{:S(2)}) collective-permute-start(f32[176,8,128]{2,1,0:T(8,128)S(1)} %shard_map.87.w), channel_id=1, source_target_pairs={{4,8},{8,4},{5,9},{9,5},{6,10},{10,6},{7,11},{11,7},{20,24},{24,20... | collective-permute-start | bytes 2162696 | tf_op jit(solution)/shard_map/ppermute | solution.py:53
  40.3 12.2 %collective-permute-start.2 = (f32[176,8,128]{2,1,0:T(8,128)S(1)}, f32[176,8,128]{2,1,0:T(8,128)S(1)}, u32[]{:S(2)}, u32[]{:S(2)}) collective-permute-start(f32[176,8,128]{2,1,0:T(8,128)S(1)} %shard_map.87.w), channel_id=1, source_target_pairs={{0,4},{4,0},{8,12},{12,8},{1,5},{5,1},{9,13},{13,9},{2,6},{6,2},{1... | collective-permute-start | bytes 2162696 | tf_op jit(solution)/shard_map/ppermute | solution.py:54
  55.5 5.8 %collective-permute-start.4 = (f32[33,8,128]{2,1,0:T(8,128)S(1)}, f32[33,8,128]{2,1,0:T(8,128)S(1)}, u32[]{:S(2)}, u32[]{:S(2)}) collective-permute-start(f32[33,8,128]{2,1,0:T(8,128)S(1)} %get-tuple-element.31), channel_id=1, source_target_pairs={{0,1},{1,0},{2,3},{3,2},{4,5},{5,4},{6,7},{7,6},{8,9},{9,8},{10,11... | collective-permute-start | bytes 405512 | tf_op jit(solution)/shard_map/ppermute | solution.py:54
  58.3 5.8 %collective-permute-start.5 = (f32[33,8,128]{2,1,0:T(8,128)S(1)}, f32[33,8,128]{2,1,0:T(8,128)S(1)}, u32[]{:S(2)}, u32[]{:S(2)}) collective-permute-start(f32[33,8,128]{2,1,0:T(8,128)S(1)} %get-tuple-element.32), channel_id=1, source_target_pairs={{1,2},{2,1},{5,6},{6,5},{9,10},{10,9},{13,14},{14,13},{17,18},{18,... | collective-permute-start | bytes 405512 | tf_op jit(solution)/shard_map/ppermute | solution.py:53
  68.9 24.4 %collective-permute-start.6 = (f32[131,8,128]{2,1,0:T(8,128)S(1)}, f32[131,8,128]{2,1,0:T(8,128)S(1)}, u32[]{:S(2)}, u32[]{:S(2)}) collective-permute-start(f32[131,8,128]{2,1,0:T(8,128)S(1)} %get-tuple-element.37), channel_id=1, source_target_pairs={{0,16},{16,0},{32,48},{48,32},{64,80},{80,64},{96,112},{112,96},{1... | collective-permute-start | bytes 1609736 | tf_op jit(solution)/shard_map/ppermute | solution.py:54
  77.1 28.8 %collective-permute-start.7 = (f32[131,8,128]{2,1,0:T(8,128)S(1)}, f32[131,8,128]{2,1,0:T(8,128)S(1)}, u32[]{:S(2)}, u32[]{:S(2)}) collective-permute-start(f32[131,8,128]{2,1,0:T(8,128)S(1)} %get-tuple-element.38), channel_id=1, source_target_pairs={{16,32},{32,16},{48,64},{64,48},{80,96},{96,80},{112,128},{128,112... | collective-permute-start | bytes 1609736 | tf_op jit(solution)/shard_map/ppermute | solution.py:53
  110.6 8.3 %collective-permute-start.8 = (f32[24,8,128]{2,1,0:T(8,128)S(1)}, f32[24,8,128]{2,1,0:T(8,128)S(1)}, u32[]{:S(2)}, u32[]{:S(2)}) collective-permute-start(f32[24,8,128]{2,1,0:T(8,128)S(1)} %get-tuple-element.42), channel_id=1, source_target_pairs={{0,16},{16,0},{32,48},{48,32},{64,80},{80,64},{96,112},{112,96},{1... | collective-permute-start | bytes 294920 | tf_op jit(solution)/shard_map/ppermute | solution.py:54
  112.6 11.1 %collective-permute-start.9 = (f32[24,8,128]{2,1,0:T(8,128)S(1)}, f32[24,8,128]{2,1,0:T(8,128)S(1)}, u32[]{:S(2)}, u32[]{:S(2)}) collective-permute-start(f32[24,8,128]{2,1,0:T(8,128)S(1)} %get-tuple-element.43), channel_id=1, source_target_pairs={{16,32},{32,16},{48,64},{64,48},{80,96},{96,80},{112,128},{128,112... | collective-permute-start | bytes 294920 | tf_op jit(solution)/shard_map/ppermute | solution.py:53

commit v7 on v6

--- a/solution.py
+++ b/solution.py
@@ -166,25 +166,19 @@
     return lax.broadcasted_iota(jnp.int32, (8, 128), 1)
 
 
-def y_tile(gy_odd, w, ga, gb, t, n):
-    if t == 1:
-        return w[n]
-    return jnp.where((gy_odd == 1) == (t == 0), ga[n], gb[n])
-
-
-def edge_kernel(offsets, w, ga, gb, out_a, out_b):
-    _, _, _, gy_odd, gz_odd = where_am_i(offsets)
+def edge_kernel(offsets, *refs):
+    tiles, (out_a, out_b) = refs[:-2], refs[-2:]
+    _, _, _, _, gz_odd = where_am_i(offsets)
     lane = lanes()
     even = lax.rem(lane, 16) < 8
 
-    def group(g):
-        for t in range(3):
+    def group(g, carry):
+        for t, ref in enumerate(tiles):
             packed = []
             for half in range(2):
                 acc = None
                 for k in range(8):
-                    x = y_tile(gy_odd, w, ga, gb, t, g * 16 + half * 8 + k)
-                    x = pltpu.roll(x, (8 + 16 * k) % 128, 1)
+                    x = pltpu.roll(ref[g * 16 + half * 8 + k], (8 + 16 * k) % 128, 1)
                     acc = x if k == 0 else jnp.where(lane < 16 * k, acc, x)
                 packed.append(acc)
             upper = jnp.where(even, packed[0], pltpu.roll(packed[1], 8, 1))
@@ -192,9 +186,9 @@
             n = t * (N // 16) + g
             out_a[n] = jnp.where(gz_odd == 1, lower, upper)
             out_b[n] = jnp.where(gz_odd == 1, upper, lower)
-
-    for g in range(N // 16):
-        group(g)
+        return carry
+
+    lax.fori_loop(0, N // 16, group, 0)
 
 
 def rows_diff(x):
@@ -378,17 +372,22 @@
                 halo[first + place[item], 16:24, :] = jnp.zeros((8, 256), jnp.float32)
 
 
-def first_kernel(offsets, w, ga, gb, za, zb, st, s_new, v_new, kern, face_a, face_b):
+def first_kernel(
+    offsets, w, ga, gb, za, zb, fa, fb, st, s_new, v_new, kern, face_a, face_b
+):
     odd, _, _, gy_odd, gz_odd = where_am_i(offsets)
     lane = lanes()
-
     even = lax.rem(lane, 16) < 8
     edge = (lane < 8) | (lane >= 120)
 
-    def group(g):
+    def group(g, carry):
         for t in range(3):
-            m = t * (N // 16) + g
-            a, b = za[m], zb[m]
+            near = (gy_odd == 1) == (t == 0)
+            if t == 1:
+                a, b = za[g], zb[g]
+            else:
+                a = jnp.where(near, za[N // 16 + g], fa[g])
+                b = jnp.where(near, zb[N // 16 + g], fb[g])
             low = jnp.where(gz_odd == 1, a, b)
             high = jnp.where(gz_odd == 1, b, a)
             packed = (
@@ -397,12 +396,13 @@
             )
             for k in range(16):
                 n = g * 16 + k
-                st[n, 8 * t : 8 * t + 8, 0:128] = y_tile(gy_odd, w, ga, gb, t, n)
+                x = w[n] if t == 1 else jnp.where(near, ga[n], gb[n])
+                st[n, 8 * t : 8 * t + 8, 0:128] = x
                 x = pltpu.roll(packed[k // 8], (120 - 16 * (k % 8)) % 128, 1)
                 st[n, 8 * t : 8 * t + 8, 128:256] = jnp.where(edge, x, 0.0)
-
-    for g in range(N // 16):
-        group(g)
+        return carry
+
+    lax.fori_loop(0, N // 16, group, 0)
     stress_at = lambda p, e: st[entry_s(p, e)]
     velocity_step(
         range(1, 9),
@@ -503,15 +503,17 @@
     recv = both_swaps(send_a, send_b, "grp")
     (win,) = call(window_kernel, [(N, 8, 128)], (offsets, *held, *recv))
     ga, gb = both_swaps(win, win, "gy")
-    edges = call(edge_kernel, [(3 * N // 16, 8, 128)] * 2, (offsets, win, ga, gb))
+    edges = call(edge_kernel, [(2 * N // 16, 8, 128)] * 2, (offsets, win, ga))
     za, zb = both_swaps(*edges, "gz")
+    edges = call(edge_kernel, [(N // 16, 8, 128)] * 2, (offsets, gb))
+    fa, fb = both_swaps(*edges, "gz")
     carried = [(72, 24, 256), (48, 24, 256), (18, 8, 128)]
     faces = lambda spec: [(face_tiles(spec), 8, 128)] * 2
     halos = lambda spec: (2 * face_places(spec)[1], 24, 256)
     state, *moving, face_a, face_b = call(
         first_kernel,
         [(N, 24, 256)] + carried + faces(MID),
-        (offsets, win, ga, gb, za, zb),
+        (offsets, win, ga, gb, za, zb, fa, fb),
     )
     recv = both_swaps(face_a, face_b, "grp")
     *moving, face_a, face_b = call(

time: 126 us -> 127 us (level)
  waiting for transfers between devices: 41.7 us -> 33.7 us
  starting transfers between devices: 65.7 us -> 73.1 us
    ppermute x5 -> x6, waiting for transfers between devices: 40.7 us -> 33.4 us  [both_swaps(): second = lax.ppermute(value_b, axis, swaps(count, 1))]
    ppermute x5 -> x6, starting transfers between devices: 18.9 us -> 24 us  [both_swaps(): first = lax.ppermute(value_a, axis, swaps(count, 0))]
    ppermute x5 -> x6, starting transfers between devices: 46.8 us -> 49.1 us  [both_swaps(): second = lax.ppermute(value_b, axis, swaps(count, 1))]
    pallas_call x6 -> x7, Pallas kernels: 16.8 us -> 18 us  [call(): pl.pallas_call(kernel, out_shape=[jax.ShapeDtypeStruct(s, jnp.float32) fo...]
  transfers between devices with their start and end apart: 10 -> 12, of which waited for: 6 -> 6; matrix products, arithmetic and copies ran while one was open for 0% -> 0% of each run, Pallas kernels for 0% -> 4%
where the time goes in v7:
time: 127 us; the launch traced here: 126 us
  starting transfers between devices  73.1 us (58%)
  waiting for transfers between devices  33.7 us (27%)
  Pallas kernels  18 us (14%)
    ppermute x6, starting transfers between devices, both_swaps(): second = lax.ppermute(value_b, axis, swaps(count, 1))  49.1 us
    ppermute x6, waiting for transfers between devices, both_swaps(): second = lax.ppermute(value_b, axis, swaps(count, 1))  33.4 us
    ppermute x6, starting transfers between devices, both_swaps(): first = lax.ppermute(value_a, axis, swaps(count, 0))  24 us
    pallas_call x7, Pallas kernels, call(): pl.pallas_call(kernel, out_shape=[jax.ShapeDtypeStruct(s, jnp.float32) fo...  18 us
  transfers between devices with their start and end apart: 12, of which 6 were waited for; matrix products, arithmetic and copies ran while one was open for 0% of the time, Pallas kernels for 4%

profile of v7, /device:TPU:61, one launch (start us, length us, event | category | flops | bytes accessed | tf_op | source)
XLA Modules:
  0.0 126.3 jit_solution(15871512202153795314)
XLA Ops:
  0.6 0.6 copy-done
  1.3 1.7 %shard_map.86 = (f32[67,8,128]{2,1,0:T(8,128)S(1)}, f32[67,8,128]{2,1,0:T(8,128)S(1)}, f32[3,4,8,128]{3,2,1,0:T(8,128)S(1)}, f32[6,4,8,128]{3,2,1,0:T(8,128)S(1)...) custom-call(s32[48]{0:T(128)S(1)} %copy-done, ...), custom_call_target="tpu_custom_call" | custom-call | tf_op jit(solution)/shard_map/pallas_call | solution.py:482
  3.0 4.0 %collective-permute-start = (f32[67,8,128]{2,1,0:T(8,128)S(1)}, f32[67,8,128]{2,1,0:T(8,128)S(1)}, u32[]{:S(2)}, u32[]{:S(2)}) collective-permute-start(f32[67,8,128]{2,1,0:T(8,128)S(1)} %get-tuple-element.31), channel_id=1, source_target_pairs={{0,16},{16,0},{32,48},{48,32},{64,80},{80,64},{96,112},{112,96},{1... | collective-permute-start | bytes 823304 | tf_op jit(solution)/shard_map/ppermute | solution.py:54
  7.0 11.1 %collective-permute-start.1 = (f32[67,8,128]{2,1,0:T(8,128)S(1)}, f32[67,8,128]{2,1,0:T(8,128)S(1)}, u32[]{:S(2)}, u32[]{:S(2)}) collective-permute-start(f32[67,8,128]{2,1,0:T(8,128)S(1)} %get-tuple-element.32), channel_id=1, source_target_pairs={{16,32},{32,16},{48,64},{64,48},{80,96},{96,80},{112,128},{128,112... | collective-permute-start | bytes 823304 | tf_op jit(solution)/shard_map/ppermute | solution.py:53
  18.2 10.2 %collective-permute-done.1.rb = f32[67,8,128]{2,1,0:T(8,128)S(1)} collective-permute-done((f32[67,8,128]{2,1,0:T(8,128)S(1)}, f32[67,8,128]{2,1,0:T(8,128)S(1)}, u32[]{:S(2)}, u32[]{:S(2)}) %collective-permute-start.1) | collective-permute-done | bytes 274464 | tf_op jit(solution)/shard_map/ppermute | solution.py:53
  29.0 3.2 %collective-permute-start.2 = (f32[176,8,128]{2,1,0:T(8,128)S(1)}, f32[176,8,128]{2,1,0:T(8,128)S(1)}, u32[]{:S(2)}, u32[]{:S(2)}) collective-permute-start(f32[176,8,128]{2,1,0:T(8,128)S(1)} %shard_map.87.refs_0_.w), channel_id=1, source_target_pairs={{0,4},{4,0},{8,12},{12,8},{1,5},{5,1},{9,13},{13,9},{2,6},{6,2},{1... | collective-permute-start | bytes 2162696 | tf_op jit(solution)/shard_map/ppermute | solution.py:54
  32.3 9.9 %collective-permute-start.3 = (f32[176,8,128]{2,1,0:T(8,128)S(1)}, f32[176,8,128]{2,1,0:T(8,128)S(1)}, u32[]{:S(2)}, u32[]{:S(2)}) collective-permute-start(f32[176,8,128]{2,1,0:T(8,128)S(1)} %shard_map.87.refs_0_.w), channel_id=1, source_target_pairs={{4,8},{8,4},{5,9},{9,5},{6,10},{10,6},{7,11},{11,7},{20,24},{24,20... | collective-permute-start | bytes 2162696 | tf_op jit(solution)/shard_map/ppermute | solution.py:53
  42.2 2.4 %shard_map.88 = (f32[22,8,128]{2,1,0:T(8,128)S(1)}, f32[22,8,128]{2,1,0:T(8,128)S(1)}) custom-call(s32[48]{0:T(128)S(1)} %copy-done, f32[176,8,128]{2,1,0:T(8,128)S(1)} %shard_map.87.refs_0_.w, f32[176,8,128]{2,1,0:T(8,128)S(1)} %collective-permute-done.2.refs_1_.ga), custom_call_target="tpu_custom_call" | custom-call | tf_op jit(solution)/shard_map/pallas_call | solution.py:482
  44.6 2.8 %collective-permute-start.4 = (f32[22,8,128]{2,1,0:T(8,128)S(1)}, f32[22,8,128]{2,1,0:T(8,128)S(1)}, u32[]{:S(2)}, u32[]{:S(2)}) collective-permute-start(f32[22,8,128]{2,1,0:T(8,128)S(1)} %get-tuple-element.33), channel_id=1, source_target_pairs={{0,1},{1,0},{2,3},{3,2},{4,5},{5,4},{6,7},{7,6},{8,9},{9,8},{10,11... | collective-permute-start | bytes 270344 | tf_op jit(solution)/shard_map/ppermute | solution.py:54
  47.5 1.9 %collective-permute-start.5 = (f32[22,8,128]{2,1,0:T(8,128)S(1)}, f32[22,8,128]{2,1,0:T(8,128)S(1)}, u32[]{:S(2)}, u32[]{:S(2)}) collective-permute-start(f32[22,8,128]{2,1,0:T(8,128)S(1)} %get-tuple-element.34), channel_id=1, source_target_pairs={{1,2},{2,1},{5,6},{6,5},{9,10},{10,9},{13,14},{14,13},{17,18},{18,... | collective-permute-start | bytes 270344 | tf_op jit(solution)/shard_map/ppermute | solution.py:53
  49.4 5.1 %collective-permute-done.3.refs_0_.gb = f32[176,8,128]{2,1,0:T(8,128)S(1)} collective-permute-done((f32[176,8,128]{2,1,0:T(8,128)S(1)}, f32[176,8,128]{2,1,0:T(8,128)S(1)}, u32[]{:S(2)}, u32[]{:S(2)}) %collective-permute-start.3) | collective-permute-done | bytes 720928 | tf_op jit(solution)/shard_map/ppermute | solution.py:53
  54.4 2.2 %shard_map.89 = (f32[11,8,128]{2,1,0:T(8,128)S(1)}, f32[11,8,128]{2,1,0:T(8,128)S(1)}) custom-call(s32[48]{0:T(128)S(1)} %copy-done, f32[176,8,128]{2,1,0:T(8,128)S(1)} %collective-permute-done.3.refs_0_.gb), custom_call_target="tpu_custom_call" | custom-call | tf_op jit(solution)/shard_map/pallas_call | solution.py:482
  56.7 2.8 %collective-permute-start.6 = (f32[11,8,128]{2,1,0:T(8,128)S(1)}, f32[11,8,128]{2,1,0:T(8,128)S(1)}, u32[]{:S(2)}, u32[]{:S(2)}) collective-permute-start(f32[11,8,128]{2,1,0:T(8,128)S(1)} %get-tuple-element.35), channel_id=1, source_target_pairs={{0,1},{1,0},{2,3},{3,2},{4,5},{5,4},{6,7},{7,6},{8,9},{9,8},{10,11... | collective-permute-start | bytes 135176 | tf_op jit(solution)/shard_map/ppermute | solution.py:54
  59.5 1.9 %collective-permute-start.7 = (f32[11,8,128]{2,1,0:T(8,128)S(1)}, f32[11,8,128]{2,1,0:T(8,128)S(1)}, u32[]{:S(2)}, u32[]{:S(2)}) collective-permute-start(f32[11,8,128]{2,1,0:T(8,128)S(1)} %get-tuple-element.36), channel_id=1, source_target_pairs={{1,2},{2,1},{5,6},{6,5},{9,10},{10,9},{13,14},{14,13},{17,18},{18,... | collective-permute-start | bytes 135176 | tf_op jit(solution)/shard_map/ppermute | solution.py:53
  61.8 2.8 %collective-permute-done.7.fb = f32[11,8,128]{2,1,0:T(8,128)S(1)} collective-permute-done((f32[11,8,128]{2,1,0:T(8,128)S(1)}, f32[11,8,128]{2,1,0:T(8,128)S(1)}, u32[]{:S(2)}, u32[]{:S(2)}) %collective-permute-start.7) | collective-permute-done | bytes 45088 | tf_op jit(solution)/shard_map/ppermute | solution.py:53
  64.6 4.3 %shard_map.90 = (f32[176,24,256]{2,1,0:T(8,128)S(1)}, f32[72,24,256]{2,1,0:T(8,128)S(1)}, f32[48,24,256]{2,1,0:T(8,128)S(1)}, f32[18,8,128]{2,1,0:T(8,128)S(1)},...) custom-call(s32[48]{0:T(128)S(1)} %copy-done, f32[176,8,128]{2,1,0:T(8,128)S(1)} %shard_map.87.refs_0_.w, ...), custom_call_target="tpu_custom_call" | custom-call | tf_op jit(solution)/shard_map/pallas_call | solution.py:482
  69.0 9.2 %collective-permute-start.8 = (f32[131,8,128]{2,1,0:T(8,128)S(1)}, f32[131,8,128]{2,1,0:T(8,128)S(1)}, u32[]{:S(2)}, u32[]{:S(2)}) collective-permute-start(f32[131,8,128]{2,1,0:T(8,128)S(1)} %get-tuple-element.41), channel_id=1, source_target_pairs={{0,16},{16,0},{32,48},{48,32},{64,80},{80,64},{96,112},{112,96},{1... | collective-permute-start | bytes 1609736 | tf_op jit(solution)/shard_map/ppermute | solution.py:54
  78.2 16.7 %collective-permute-start.9 = (f32[131,8,128]{2,1,0:T(8,128)S(1)}, f32[131,8,128]{2,1,0:T(8,128)S(1)}, u32[]{:S(2)}, u32[]{:S(2)}) collective-permute-start(f32[131,8,128]{2,1,0:T(8,128)S(1)} %get-tuple-element.42), channel_id=1, source_target_pairs={{16,32},{32,16},{48,64},{64,48},{80,96},{96,80},{112,128},{128,112... | collective-permute-start | bytes 1609736 | tf_op jit(solution)/shard_map/ppermute | solution.py:53
  94.9 11.7 %collective-permute-done.9.rb = f32[131,8,128]{2,1,0:T(8,128)S(1)} collective-permute-done((f32[131,8,128]{2,1,0:T(8,128)S(1)}, f32[131,8,128]{2,1,0:T(8,128)S(1)}, u32[]{:S(2)}, u32[]{:S(2)}) %collective-permute-start.9) | collective-permute-done | bytes 536608 | tf_op jit(solution)/shard_map/ppermute | solution.py:53
  106.6 4.7 %shard_map.91 = (f32[72,24,256]{2,1,0:T(8,128)S(1)}, f32[48,24,256]{2,1,0:T(8,128)S(1)}, f32[18,8,128]{2,1,0:T(8,128)S(1)}, f32[24,8,128]{2,1,0:T(8,128)S(1)}, f32[24,8,128]{2,1,0:T(8,128)S(1)}) custom-call(s32[48]{0:T(128)S(1)} %copy-done, f32[176,24,256]{2,1,0:T(8,128)S(1)} %get-tuple-element.37.st, f32[72,24,256]{2,1,0:T(8,128)S(1)} %get-tuple-element.38.s_old, ...), custom_call_target="tpu_custom_call" | custom-call | tf_op jit(solution)/shard_map/pallas_call | solution.py:482
  111.3 1.9 %collective-permute-start.10 = (f32[24,8,128]{2,1,0:T(8,128)S(1)}, f32[24,8,128]{2,1,0:T(8,128)S(1)}, u32[]{:S(2)}, u32[]{:S(2)}) collective-permute-start(f32[24,8,128]{2,1,0:T(8,128)S(1)} %get-tuple-element.46), channel_id=1, source_target_pairs={{0,16},{16,0},{32,48},{48,32},{64,80},{80,64},{96,112},{112,96},{1... | collective-permute-start | bytes 294920 | tf_op jit(solution)/shard_map/ppermute | solution.py:54
  113.2 7.5 %collective-permute-start.11 = (f32[24,8,128]{2,1,0:T(8,128)S(1)}, f32[24,8,128]{2,1,0:T(8,128)S(1)}, u32[]{:S(2)}, u32[]{:S(2)}) collective-permute-start(f32[24,8,128]{2,1,0:T(8,128)S(1)} %get-tuple-element.47), channel_id=1, source_target_pairs={{16,32},{32,16},{48,64},{64,48},{80,96},{96,80},{112,128},{128,112... | collective-permute-start | bytes 294920 | tf_op jit(solution)/shard_map/ppermute | solution.py:53
  120.7 3.6 %collective-permute-done.11.rb = f32[24,8,128]{2,1,0:T(8,128)S(1)} collective-permute-done((f32[24,8,128]{2,1,0:T(8,128)S(1)}, f32[24,8,128]{2,1,0:T(8,128)S(1)}, u32[]{:S(2)}, u32[]{:S(2)}) %collective-permute-start.11) | collective-permute-done | bytes 98336 | tf_op jit(solution)/shard_map/ppermute | solution.py:53
  124.3 2.0 %shard_map.92 = (f32[6,8,128]{2,1,0:T(8,128)}, f32[2,6,8,128]{3,2,1,0:T(8,128)}) custom-call(s32[48]{0:T(128)S(1)} %copy-done, f32[176,24,256]{2,1,0:T(8,128)S(1)} %get-tuple-element.37.st, f32[72,24,256]{2,1,0:T(8,128)S(1)} %get-tuple-element.43.s_old, f32[48,24,256]{2,1,0:T(8,128)S(1)} %get-tuple-element.44.v_old, ...), custom_call_target="tpu_custom_call" | custom-call | tf_op jit(solution)/shard_map/pallas_call | solution.py:482
  (9 shorter events, 1.0 us)
Async XLA Ops:
  0.6 0.7 copy-start
  3.0 15.2 %collective-permute-start = (f32[67,8,128]{2,1,0:T(8,128)S(1)}, f32[67,8,128]{2,1,0:T(8,128)S(1)}, u32[]{:S(2)}, u32[]{:S(2)}) collective-permute-start(f32[67,8,128]{2,1,0:T(8,128)S(1)} %get-tuple-element.31), channel_id=1, source_target_pairs={{0,16},{16,0},{32,48},{48,32},{64,80},{80,64},{96,112},{112,96},{1... | collective-permute-start | bytes 823304 | tf_op jit(solution)/shard_map/ppermute | solution.py:54
  7.0 21.4 %collective-permute-start.1 = (f32[67,8,128]{2,1,0:T(8,128)S(1)}, f32[67,8,128]{2,1,0:T(8,128)S(1)}, u32[]{:S(2)}, u32[]{:S(2)}) collective-permute-start(f32[67,8,128]{2,1,0:T(8,128)S(1)} %get-tuple-element.32), channel_id=1, source_target_pairs={{16,32},{32,16},{48,64},{64,48},{80,96},{96,80},{112,128},{128,112... | collective-permute-start | bytes 823304 | tf_op jit(solution)/shard_map/ppermute | solution.py:53
  29.0 13.2 %collective-permute-start.2 = (f32[176,8,128]{2,1,0:T(8,128)S(1)}, f32[176,8,128]{2,1,0:T(8,128)S(1)}, u32[]{:S(2)}, u32[]{:S(2)}) collective-permute-start(f32[176,8,128]{2,1,0:T(8,128)S(1)} %shard_map.87.refs_0_.w), channel_id=1, source_target_pairs={{0,4},{4,0},{8,12},{12,8},{1,5},{5,1},{9,13},{13,9},{2,6},{6,2},{1... | collective-permute-start | bytes 2162696 | tf_op jit(solution)/shard_map/ppermute | solution.py:54
  32.3 22.2 %collective-permute-start.3 = (f32[176,8,128]{2,1,0:T(8,128)S(1)}, f32[176,8,128]{2,1,0:T(8,128)S(1)}, u32[]{:S(2)}, u32[]{:S(2)}) collective-permute-start(f32[176,8,128]{2,1,0:T(8,128)S(1)} %shard_map.87.refs_0_.w), channel_id=1, source_target_pairs={{4,8},{8,4},{5,9},{9,5},{6,10},{10,6},{7,11},{11,7},{20,24},{24,20... | collective-permute-start | bytes 2162696 | tf_op jit(solution)/shard_map/ppermute | solution.py:53
  44.6 20.0 %collective-permute-start.4 = (f32[22,8,128]{2,1,0:T(8,128)S(1)}, f32[22,8,128]{2,1,0:T(8,128)S(1)}, u32[]{:S(2)}, u32[]{:S(2)}) collective-permute-start(f32[22,8,128]{2,1,0:T(8,128)S(1)} %get-tuple-element.33), channel_id=1, source_target_pairs={{0,1},{1,0},{2,3},{3,2},{4,5},{5,4},{6,7},{7,6},{8,9},{9,8},{10,11... | collective-permute-start | bytes 270344 | tf_op jit(solution)/shard_map/ppermute | solution.py:54
  47.5 17.1 %collective-permute-start.5 = (f32[22,8,128]{2,1,0:T(8,128)S(1)}, f32[22,8,128]{2,1,0:T(8,128)S(1)}, u32[]{:S(2)}, u32[]{:S(2)}) collective-permute-start(f32[22,8,128]{2,1,0:T(8,128)S(1)} %get-tuple-element.34), channel_id=1, source_target_pairs={{1,2},{2,1},{5,6},{6,5},{9,10},{10,9},{13,14},{14,13},{17,18},{18,... | collective-permute-start | bytes 270344 | tf_op jit(solution)/shard_map/ppermute | solution.py:53
  56.7 5.1 %collective-permute-start.6 = (f32[11,8,128]{2,1,0:T(8,128)S(1)}, f32[11,8,128]{2,1,0:T(8,128)S(1)}, u32[]{:S(2)}, u32[]{:S(2)}) collective-permute-start(f32[11,8,128]{2,1,0:T(8,128)S(1)} %get-tuple-element.35), channel_id=1, source_target_pairs={{0,1},{1,0},{2,3},{3,2},{4,5},{5,4},{6,7},{7,6},{8,9},{9,8},{10,11... | collective-permute-start | bytes 135176 | tf_op jit(solution)/shard_map/ppermute | solution.py:54
  59.5 5.1 %collective-permute-start.7 = (f32[11,8,128]{2,1,0:T(8,128)S(1)}, f32[11,8,128]{2,1,0:T(8,128)S(1)}, u32[]{:S(2)}, u32[]{:S(2)}) collective-permute-start(f32[11,8,128]{2,1,0:T(8,128)S(1)} %get-tuple-element.36), channel_id=1, source_target_pairs={{1,2},{2,1},{5,6},{6,5},{9,10},{10,9},{13,14},{14,13},{17,18},{18,... | collective-permute-start | bytes 135176 | tf_op jit(solution)/shard_map/ppermute | solution.py:53
  69.0 26.0 %collective-permute-start.8 = (f32[131,8,128]{2,1,0:T(8,128)S(1)}, f32[131,8,128]{2,1,0:T(8,128)S(1)}, u32[]{:S(2)}, u32[]{:S(2)}) collective-permute-start(f32[131,8,128]{2,1,0:T(8,128)S(1)} %get-tuple-element.41), channel_id=1, source_target_pairs={{0,16},{16,0},{32,48},{48,32},{64,80},{80,64},{96,112},{112,96},{1... | collective-permute-start | bytes 1609736 | tf_op jit(solution)/shard_map/ppermute | solution.py:54
  78.2 28.4 %collective-permute-start.9 = (f32[131,8,128]{2,1,0:T(8,128)S(1)}, f32[131,8,128]{2,1,0:T(8,128)S(1)}, u32[]{:S(2)}, u32[]{:S(2)}) collective-permute-start(f32[131,8,128]{2,1,0:T(8,128)S(1)} %get-tuple-element.42), channel_id=1, source_target_pairs={{16,32},{32,16},{48,64},{64,48},{80,96},{96,80},{112,128},{128,112... | collective-permute-start | bytes 1609736 | tf_op jit(solution)/shard_map/ppermute | solution.py:53
  111.3 9.4 %collective-permute-start.10 = (f32[24,8,128]{2,1,0:T(8,128)S(1)}, f32[24,8,128]{2,1,0:T(8,128)S(1)}, u32[]{:S(2)}, u32[]{:S(2)}) collective-permute-start(f32[24,8,128]{2,1,0:T(8,128)S(1)} %get-tuple-element.46), channel_id=1, source_target_pairs={{0,16},{16,0},{32,48},{48,32},{64,80},{80,64},{96,112},{112,96},{1... | collective-permute-start | bytes 294920 | tf_op jit(solution)/shard_map/ppermute | solution.py:54
  113.2 11.1 %collective-permute-start.11 = (f32[24,8,128]{2,1,0:T(8,128)S(1)}, f32[24,8,128]{2,1,0:T(8,128)S(1)}, u32[]{:S(2)}, u32[]{:S(2)}) collective-permute-start(f32[24,8,128]{2,1,0:T(8,128)S(1)} %get-tuple-element.47), channel_id=1, source_target_pairs={{16,32},{32,16},{48,64},{64,48},{80,96},{96,80},{112,128},{128,112... | collective-permute-start | bytes 294920 | tf_op jit(solution)/shard_map/ppermute | solution.py:53

commit v8 on v6

--- a/solution.py
+++ b/solution.py
@@ -69,9 +69,10 @@
     )
 
 
-def pack_kernel(offsets, *refs):
-    raw, (out_a, out_b), held, sems = refs[:6], refs[6:8], refs[8:14], refs[14]
-    copies = [pltpu.make_async_copy(raw[k], held[k], sems.at[k]) for k in range(6)]
+def pack_kernel(*refs):
+    raw, (out_a, out_b), held, (offsets, sems) = refs[:7], refs[7:9], refs[9:15], refs[15:]
+    to = (*held, offsets)
+    copies = [pltpu.make_async_copy(raw[k], to[k], sems.at[k]) for k in range(7)]
     for copy in copies:
         copy.start()
     for copy in copies:
@@ -166,6 +167,17 @@
     return lax.broadcasted_iota(jnp.int32, (8, 128), 1)
 
 
+def in_pairs(group, count):
+    def two(i, carry):
+        group(2 * i)
+        group(2 * i + 1)
+        return carry
+
+    lax.fori_loop(0, count // 2, two, 0)
+    if count % 2:
+        group(count - 1)
+
+
 def y_tile(gy_odd, w, ga, gb, t, n):
     if t == 1:
         return w[n]
@@ -193,8 +205,7 @@
             out_a[n] = jnp.where(gz_odd == 1, lower, upper)
             out_b[n] = jnp.where(gz_odd == 1, upper, lower)
 
-    for g in range(N // 16):
-        group(g)
+    in_pairs(group, N // 16)
 
 
 def rows_diff(x):
@@ -401,8 +412,7 @@
                 x = pltpu.roll(packed[k // 8], (120 - 16 * (k % 8)) % 128, 1)
                 st[n, 8 * t : 8 * t + 8, 128:256] = jnp.where(edge, x, 0.0)
 
-    for g in range(N // 16):
-        group(g)
+    in_pairs(group, N // 16)
     stress_at = lambda p, e: st[entry_s(p, e)]
     velocity_step(
         range(1, 9),
@@ -477,29 +487,34 @@
         modu[1, r] = jnp.where(live, kern[12 + row], 0.0)
 
 
-def call(kernel, outs, args, scratch=(), space=pltpu.VMEM):
+def call(kernel, outs, args, scratch=()):
     vmem = pl.BlockSpec(memory_space=pltpu.VMEM)
     return pl.pallas_call(
         kernel,
         out_shape=[jax.ShapeDtypeStruct(s, jnp.float32) for s in outs],
         in_specs=[pl.BlockSpec(memory_space=pltpu.SMEM)]
-        + [pl.BlockSpec(memory_space=space)] * (len(args) - 1),
+        + [vmem] * (len(args) - 1),
         out_specs=[vmem] * len(outs),
-        scratch_shapes=[pltpu.VMEM(s, jnp.float32) if isinstance(s, tuple) else s for s in scratch],
+        scratch_shapes=[pltpu.VMEM(s, jnp.float32) for s in scratch],
         compiler_params=pltpu.CompilerParams(vmem_limit_bytes=VMEM_LIMIT),
     )(*args)
 
 
 def sensitivity(fwd_velocity, fwd_stress, density, lame, adj_velocity, adj_stress, offsets):
     raw = (fwd_velocity, fwd_stress, density, lame, adj_velocity, adj_stress)
-    raw = [pltpu.with_memory_space_constraint(a, pltpu.HBM) for a in raw]
-    send_a, send_b, *held = call(
+    hbm = pl.BlockSpec(memory_space=pltpu.HBM)
+    send_a, send_b, *held = pl.pallas_call(
         pack_kernel,
-        [(NP1, 8, 128)] * 2 + [a.shape for a in raw],
-        (offsets, *raw),
-        [pltpu.SemaphoreType.DMA((6,))],
-        pltpu.HBM,
-    )
+        out_shape=[
+            jax.ShapeDtypeStruct(s, jnp.float32)
+            for s in [(NP1, 8, 128)] * 2 + [a.shape for a in raw]
+        ],
+        in_specs=[hbm] * 7,
+        out_specs=[pl.BlockSpec(memory_space=pltpu.VMEM)] * 8,
+        scratch_shapes=[pltpu.SMEM(offsets.shape, jnp.int32), pltpu.SemaphoreType.DMA((7,))],
+        compiler_params=pltpu.CompilerParams(vmem_limit_bytes=VMEM_LIMIT),
+        name="pack",
+    )(*[pltpu.with_memory_space_constraint(a, pltpu.HBM) for a in (*raw, offsets)])
     recv = both_swaps(send_a, send_b, "grp")
     (win,) = call(window_kernel, [(N, 8, 128)], (offsets, *held, *recv))
     ga, gb = both_swaps(win, win, "gy")

time: 126 us -> 124 us (0.984)
  the two profiles are of different devices: /device:TPU:61 before, /device:TPU:37 now
where the time goes in v8:
time: 124 us; the launch traced here: 123 us
  starting transfers between devices  65.1 us (52%)
  waiting for transfers between devices  42.6 us (34%)
  Pallas kernels  14.2 us (11%)
    ppermute x5, waiting for transfers between devices, both_swaps(): second = lax.ppermute(value_b, axis, swaps(count, 1))  41.5 us
    ppermute x5, starting transfers between devices, both_swaps(): second = lax.ppermute(value_b, axis, swaps(count, 1))  37.6 us
    ppermute x5, starting transfers between devices, both_swaps(): first = lax.ppermute(value_a, axis, swaps(count, 0))  27.5 us
    pallas_call x5, Pallas kernels, call(): pl.pallas_call(kernel, out_shape=[jax.ShapeDtypeStruct(s, jnp.float32) fo...  13 us
  transfers between devices with their start and end apart: 10, of which 7 were waited for; matrix products, arithmetic and copies ran while one was open for 0% of the time, Pallas kernels for 0%

profile of v8, /device:TPU:37, one launch (start us, length us, event | category | flops | bytes accessed | tf_op | source)
XLA Modules:
  0.0 123.3 jit_solution(895206907351000085)
XLA Ops:
  0.6 1.2 pack.1
  1.8 4.0 %collective-permute-start = (f32[67,8,128]{2,1,0:T(8,128)S(1)}, f32[67,8,128]{2,1,0:T(8,128)S(1)}, u32[]{:S(2)}, u32[]{:S(2)}) collective-permute-start(f32[67,8,128]{2,1,0:T(8,128)S(1)} %get-tuple-element.29), channel_id=1, source_target_pairs={{0,16},{16,0},{32,48},{48,32},{64,80},{80,64},{96,112},{112,96},{1... | collective-permute-start | bytes 823304 | tf_op jit(solution)/shard_map/ppermute | solution.py:54
  5.8 10.2 %collective-permute-start.1 = (f32[67,8,128]{2,1,0:T(8,128)S(1)}, f32[67,8,128]{2,1,0:T(8,128)S(1)}, u32[]{:S(2)}, u32[]{:S(2)}) collective-permute-start(f32[67,8,128]{2,1,0:T(8,128)S(1)} %get-tuple-element.30), channel_id=1, source_target_pairs={{16,32},{32,16},{48,64},{64,48},{80,96},{96,80},{112,128},{128,112... | collective-permute-start | bytes 823304 | tf_op jit(solution)/shard_map/ppermute | solution.py:53
  16.1 10.2 %collective-permute-done.1.rb = f32[67,8,128]{2,1,0:T(8,128)S(1)} collective-permute-done((f32[67,8,128]{2,1,0:T(8,128)S(1)}, f32[67,8,128]{2,1,0:T(8,128)S(1)}, u32[]{:S(2)}, u32[]{:S(2)}) %collective-permute-start.1) | collective-permute-done | bytes 274464 | tf_op jit(solution)/shard_map/ppermute | solution.py:53
  26.4 0.7 copy-done
  27.0 0.6 shard_map.86.w
  27.6 11.8 %collective-permute-start.3 = (f32[176,8,128]{2,1,0:T(8,128)S(1)}, f32[176,8,128]{2,1,0:T(8,128)S(1)}, u32[]{:S(2)}, u32[]{:S(2)}) collective-permute-start(f32[176,8,128]{2,1,0:T(8,128)S(1)} %shard_map.86.w), channel_id=1, source_target_pairs={{4,8},{8,4},{5,9},{9,5},{6,10},{10,6},{7,11},{11,7},{20,24},{24,20... | collective-permute-start | bytes 2162696 | tf_op jit(solution)/shard_map/ppermute | solution.py:53
  39.5 1.9 %collective-permute-start.2 = (f32[176,8,128]{2,1,0:T(8,128)S(1)}, f32[176,8,128]{2,1,0:T(8,128)S(1)}, u32[]{:S(2)}, u32[]{:S(2)}) collective-permute-start(f32[176,8,128]{2,1,0:T(8,128)S(1)} %shard_map.86.w), channel_id=1, source_target_pairs={{0,4},{4,0},{8,12},{12,8},{1,5},{5,1},{9,13},{13,9},{2,6},{6,2},{1... | collective-permute-start | bytes 2162696 | tf_op jit(solution)/shard_map/ppermute | solution.py:54
  41.4 10.0 %collective-permute-done.3.gb = f32[176,8,128]{2,1,0:T(8,128)S(1)} collective-permute-done((f32[176,8,128]{2,1,0:T(8,128)S(1)}, f32[176,8,128]{2,1,0:T(8,128)S(1)}, u32[]{:S(2)}, u32[]{:S(2)}) %collective-permute-start.3) | collective-permute-done | bytes 720928 | tf_op jit(solution)/shard_map/ppermute | solution.py:53
  51.4 2.1 %shard_map.87 = (f32[33,8,128]{2,1,0:T(8,128)S(1)}, f32[33,8,128]{2,1,0:T(8,128)S(1)}) custom-call(s32[48]{0:T(128)S(1)} %copy-done, f32[176,8,128]{2,1,0:T(8,128)S(1)} %shard_map.86.w, f32[176,8,128]{2,1,0:T(8,128)S(1)} %collective-permute-done.2.ga, f32[176,8,128]{2,1,0:T(8,128)S(1)} %collective-permute-done.3.gb), custom_call_target="tpu_custom_call" | custom-call | tf_op jit(solution)/shard_map/pallas_call | solution.py:492
  53.5 2.8 %collective-permute-start.4 = (f32[33,8,128]{2,1,0:T(8,128)S(1)}, f32[33,8,128]{2,1,0:T(8,128)S(1)}, u32[]{:S(2)}, u32[]{:S(2)}) collective-permute-start(f32[33,8,128]{2,1,0:T(8,128)S(1)} %get-tuple-element.31), channel_id=1, source_target_pairs={{0,1},{1,0},{2,3},{3,2},{4,5},{5,4},{6,7},{7,6},{8,9},{9,8},{10,11... | collective-permute-start | bytes 405512 | tf_op jit(solution)/shard_map/ppermute | solution.py:54
  56.3 1.9 %collective-permute-start.5 = (f32[33,8,128]{2,1,0:T(8,128)S(1)}, f32[33,8,128]{2,1,0:T(8,128)S(1)}, u32[]{:S(2)}, u32[]{:S(2)}) collective-permute-start(f32[33,8,128]{2,1,0:T(8,128)S(1)} %get-tuple-element.32), channel_id=1, source_target_pairs={{1,2},{2,1},{5,6},{6,5},{9,10},{10,9},{13,14},{14,13},{17,18},{18,... | collective-permute-start | bytes 405512 | tf_op jit(solution)/shard_map/ppermute | solution.py:53
  58.3 1.0 collective-permute-done.4.za
  59.2 2.8 %collective-permute-done.5.zb = f32[33,8,128]{2,1,0:T(8,128)S(1)} collective-permute-done((f32[33,8,128]{2,1,0:T(8,128)S(1)}, f32[33,8,128]{2,1,0:T(8,128)S(1)}, u32[]{:S(2)}, u32[]{:S(2)}) %collective-permute-start.5) | collective-permute-done | bytes 135200 | tf_op jit(solution)/shard_map/ppermute | solution.py:53
  62.1 3.6 %shard_map.88 = (f32[176,24,256]{2,1,0:T(8,128)S(1)}, f32[72,24,256]{2,1,0:T(8,128)S(1)}, f32[48,24,256]{2,1,0:T(8,128)S(1)}, f32[18,8,128]{2,1,0:T(8,128)S(1)},...) custom-call(s32[48]{0:T(128)S(1)} %copy-done, f32[176,8,128]{2,1,0:T(8,128)S(1)} %shard_map.86.w, ...), custom_call_target="tpu_custom_call" | custom-call | tf_op jit(solution)/shard_map/pallas_call | solution.py:492
  65.7 16.8 %collective-permute-start.6 = (f32[131,8,128]{2,1,0:T(8,128)S(1)}, f32[131,8,128]{2,1,0:T(8,128)S(1)}, u32[]{:S(2)}, u32[]{:S(2)}) collective-permute-start(f32[131,8,128]{2,1,0:T(8,128)S(1)} %get-tuple-element.37), channel_id=1, source_target_pairs={{0,16},{16,0},{32,48},{48,32},{64,80},{80,64},{96,112},{112,96},{1... | collective-permute-start | bytes 1609736 | tf_op jit(solution)/shard_map/ppermute | solution.py:54
  82.5 7.2 %collective-permute-start.7 = (f32[131,8,128]{2,1,0:T(8,128)S(1)}, f32[131,8,128]{2,1,0:T(8,128)S(1)}, u32[]{:S(2)}, u32[]{:S(2)}) collective-permute-start(f32[131,8,128]{2,1,0:T(8,128)S(1)} %get-tuple-element.38), channel_id=1, source_target_pairs={{16,32},{32,16},{48,64},{64,48},{80,96},{96,80},{112,128},{128,112... | collective-permute-start | bytes 1609736 | tf_op jit(solution)/shard_map/ppermute | solution.py:53
  89.7 0.2 collective-permute-done.6.ra
  89.9 12.6 %collective-permute-done.7.rb = f32[131,8,128]{2,1,0:T(8,128)S(1)} collective-permute-done((f32[131,8,128]{2,1,0:T(8,128)S(1)}, f32[131,8,128]{2,1,0:T(8,128)S(1)}, u32[]{:S(2)}, u32[]{:S(2)}) %collective-permute-start.7) | collective-permute-done | bytes 536608 | tf_op jit(solution)/shard_map/ppermute | solution.py:53
  102.4 4.7 %shard_map.89 = (f32[72,24,256]{2,1,0:T(8,128)S(1)}, f32[48,24,256]{2,1,0:T(8,128)S(1)}, f32[18,8,128]{2,1,0:T(8,128)S(1)}, f32[24,8,128]{2,1,0:T(8,128)S(1)}, f32[24,8,128]{2,1,0:T(8,128)S(1)}) custom-call(s32[48]{0:T(128)S(1)} %copy-done, f32[176,24,256]{2,1,0:T(8,128)S(1)} %get-tuple-element.33.st, f32[72,24,256]{2,1,0:T(8,128)S(1)} %get-tuple-element.34.s_old, ...), custom_call_target="tpu_custom_call" | custom-call | tf_op jit(solution)/shard_map/pallas_call | solution.py:492
  107.1 1.9 %collective-permute-start.8 = (f32[24,8,128]{2,1,0:T(8,128)S(1)}, f32[24,8,128]{2,1,0:T(8,128)S(1)}, u32[]{:S(2)}, u32[]{:S(2)}) collective-permute-start(f32[24,8,128]{2,1,0:T(8,128)S(1)} %get-tuple-element.42), channel_id=1, source_target_pairs={{0,16},{16,0},{32,48},{48,32},{64,80},{80,64},{96,112},{112,96},{1... | collective-permute-start | bytes 294920 | tf_op jit(solution)/shard_map/ppermute | solution.py:54
  109.0 6.4 %collective-permute-start.9 = (f32[24,8,128]{2,1,0:T(8,128)S(1)}, f32[24,8,128]{2,1,0:T(8,128)S(1)}, u32[]{:S(2)}, u32[]{:S(2)}) collective-permute-start(f32[24,8,128]{2,1,0:T(8,128)S(1)} %get-tuple-element.43), channel_id=1, source_target_pairs={{16,32},{32,16},{48,64},{64,48},{80,96},{96,80},{112,128},{128,112... | collective-permute-start | bytes 294920 | tf_op jit(solution)/shard_map/ppermute | solution.py:53
  115.4 5.9 %collective-permute-done.9.rb = f32[24,8,128]{2,1,0:T(8,128)S(1)} collective-permute-done((f32[24,8,128]{2,1,0:T(8,128)S(1)}, f32[24,8,128]{2,1,0:T(8,128)S(1)}, u32[]{:S(2)}, u32[]{:S(2)}) %collective-permute-start.9) | collective-permute-done | bytes 98336 | tf_op jit(solution)/shard_map/ppermute | solution.py:53
  121.3 2.0 %shard_map.90 = (f32[6,8,128]{2,1,0:T(8,128)}, f32[2,6,8,128]{3,2,1,0:T(8,128)}) custom-call(s32[48]{0:T(128)S(1)} %copy-done, f32[176,24,256]{2,1,0:T(8,128)S(1)} %get-tuple-element.33.st, f32[72,24,256]{2,1,0:T(8,128)S(1)} %get-tuple-element.39.s_old, f32[48,24,256]{2,1,0:T(8,128)S(1)} %get-tuple-element.40.v_old, ...), custom_call_target="tpu_custom_call" | custom-call | tf_op jit(solution)/shard_map/pallas_call | solution.py:492
  (4 shorter events, 0.0 us)
Async XLA Ops:
  1.8 14.3 %collective-permute-start = (f32[67,8,128]{2,1,0:T(8,128)S(1)}, f32[67,8,128]{2,1,0:T(8,128)S(1)}, u32[]{:S(2)}, u32[]{:S(2)}) collective-permute-start(f32[67,8,128]{2,1,0:T(8,128)S(1)} %get-tuple-element.29), channel_id=1, source_target_pairs={{0,16},{16,0},{32,48},{48,32},{64,80},{80,64},{96,112},{112,96},{1... | collective-permute-start | bytes 823304 | tf_op jit(solution)/shard_map/ppermute | solution.py:54
  5.8 20.5 %collective-permute-start.1 = (f32[67,8,128]{2,1,0:T(8,128)S(1)}, f32[67,8,128]{2,1,0:T(8,128)S(1)}, u32[]{:S(2)}, u32[]{:S(2)}) collective-permute-start(f32[67,8,128]{2,1,0:T(8,128)S(1)} %get-tuple-element.30), channel_id=1, source_target_pairs={{16,32},{32,16},{48,64},{64,48},{80,96},{96,80},{112,128},{128,112... | collective-permute-start | bytes 823304 | tf_op jit(solution)/shard_map/ppermute | solution.py:53
  26.4 0.7 copy-start
  27.6 23.8 %collective-permute-start.3 = (f32[176,8,128]{2,1,0:T(8,128)S(1)}, f32[176,8,128]{2,1,0:T(8,128)S(1)}, u32[]{:S(2)}, u32[]{:S(2)}) collective-permute-start(f32[176,8,128]{2,1,0:T(8,128)S(1)} %shard_map.86.w), channel_id=1, source_target_pairs={{4,8},{8,4},{5,9},{9,5},{6,10},{10,6},{7,11},{11,7},{20,24},{24,20... | collective-permute-start | bytes 2162696 | tf_op jit(solution)/shard_map/ppermute | solution.py:53
  39.5 11.9 %collective-permute-start.2 = (f32[176,8,128]{2,1,0:T(8,128)S(1)}, f32[176,8,128]{2,1,0:T(8,128)S(1)}, u32[]{:S(2)}, u32[]{:S(2)}) collective-permute-start(f32[176,8,128]{2,1,0:T(8,128)S(1)} %shard_map.86.w), channel_id=1, source_target_pairs={{0,4},{4,0},{8,12},{12,8},{1,5},{5,1},{9,13},{13,9},{2,6},{6,2},{1... | collective-permute-start | bytes 2162696 | tf_op jit(solution)/shard_map/ppermute | solution.py:54
  53.5 5.8 %collective-permute-start.4 = (f32[33,8,128]{2,1,0:T(8,128)S(1)}, f32[33,8,128]{2,1,0:T(8,128)S(1)}, u32[]{:S(2)}, u32[]{:S(2)}) collective-permute-start(f32[33,8,128]{2,1,0:T(8,128)S(1)} %get-tuple-element.31), channel_id=1, source_target_pairs={{0,1},{1,0},{2,3},{3,2},{4,5},{5,4},{6,7},{7,6},{8,9},{9,8},{10,11... | collective-permute-start | bytes 405512 | tf_op jit(solution)/shard_map/ppermute | solution.py:54
  56.3 5.8 %collective-permute-start.5 = (f32[33,8,128]{2,1,0:T(8,128)S(1)}, f32[33,8,128]{2,1,0:T(8,128)S(1)}, u32[]{:S(2)}, u32[]{:S(2)}) collective-permute-start(f32[33,8,128]{2,1,0:T(8,128)S(1)} %get-tuple-element.32), channel_id=1, source_target_pairs={{1,2},{2,1},{5,6},{6,5},{9,10},{10,9},{13,14},{14,13},{17,18},{18,... | collective-permute-start | bytes 405512 | tf_op jit(solution)/shard_map/ppermute | solution.py:53
  65.7 24.2 %collective-permute-start.6 = (f32[131,8,128]{2,1,0:T(8,128)S(1)}, f32[131,8,128]{2,1,0:T(8,128)S(1)}, u32[]{:S(2)}, u32[]{:S(2)}) collective-permute-start(f32[131,8,128]{2,1,0:T(8,128)S(1)} %get-tuple-element.37), channel_id=1, source_target_pairs={{0,16},{16,0},{32,48},{48,32},{64,80},{80,64},{96,112},{112,96},{1... | collective-permute-start | bytes 1609736 | tf_op jit(solution)/shard_map/ppermute | solution.py:54
  82.5 19.9 %collective-permute-start.7 = (f32[131,8,128]{2,1,0:T(8,128)S(1)}, f32[131,8,128]{2,1,0:T(8,128)S(1)}, u32[]{:S(2)}, u32[]{:S(2)}) collective-permute-start(f32[131,8,128]{2,1,0:T(8,128)S(1)} %get-tuple-element.38), channel_id=1, source_target_pairs={{16,32},{32,16},{48,64},{64,48},{80,96},{96,80},{112,128},{128,112... | collective-permute-start | bytes 1609736 | tf_op jit(solution)/shard_map/ppermute | solution.py:53
  107.1 8.3 %collective-permute-start.8 = (f32[24,8,128]{2,1,0:T(8,128)S(1)}, f32[24,8,128]{2,1,0:T(8,128)S(1)}, u32[]{:S(2)}, u32[]{:S(2)}) collective-permute-start(f32[24,8,128]{2,1,0:T(8,128)S(1)} %get-tuple-element.42), channel_id=1, source_target_pairs={{0,16},{16,0},{32,48},{48,32},{64,80},{80,64},{96,112},{112,96},{1... | collective-permute-start | bytes 294920 | tf_op jit(solution)/shard_map/ppermute | solution.py:54
  109.0 12.3 %collective-permute-start.9 = (f32[24,8,128]{2,1,0:T(8,128)S(1)}, f32[24,8,128]{2,1,0:T(8,128)S(1)}, u32[]{:S(2)}, u32[]{:S(2)}) collective-permute-start(f32[24,8,128]{2,1,0:T(8,128)S(1)} %get-tuple-element.43), channel_id=1, source_target_pairs={{16,32},{32,16},{48,64},{64,48},{80,96},{96,80},{112,128},{128,112... | collective-permute-start | bytes 294920 | tf_op jit(solution)/shard_map/ppermute | solution.py:53
